TPU v7x, 32 devices: a whole 2x2x4 slice. The times are simulated.
32 devices in a mesh: dp: 4 (over x, core), ctx: 8 (over z, y).
Axes of the slice: x: 2, y: 2, z: 4, core: 2. Of those that a mesh axis runs over, the one named last changes fastest.
Arguments:
- inputs: bfloat16 [12, 1024, 960], P('dp', 'ctx'), may hold values from -6 to 6
- gain_one: bfloat16 [960], P('ctx'), may hold values from 0.099609375 to 1.8984375
- query_weight: bfloat16 [960, 960], P('dp', 'ctx'), may hold values from -0.1875 to 0.1875
- key_weight: bfloat16 [960, 320], P('dp', 'ctx'), may hold values from -0.1875 to 0.1875
- value_weight: bfloat16 [960, 320], P('dp', 'ctx'), may hold values from -0.1875 to 0.1875
- output_weight: bfloat16 [960, 960], P('dp', 'ctx'), may hold values from -1.5 to 1.5
- gain_two: bfloat16 [960], P('ctx'), may hold values from 0.099609375 to 1.8984375
- gate_weight: bfloat16 [960, 2560], P('dp', 'ctx'), may hold values from -0.1875 to 0.1875
- up_weight: bfloat16 [960, 2560], P('dp', 'ctx'), may hold values from -0.1875 to 0.1875
- down_weight: bfloat16 [2560, 960], P('dp', 'ctx'), may hold values from -0.25 to 0.25
- segment_ids: int32 [12, 1024], P('dp', 'ctx'), may hold values from 0 to 3, never falling along the last dimension, each value on 1 to 512 neighbouring positions
- cotangent: bfloat16 [12, 1024, 960], P('dp', 'ctx'), may hold values from -6 to 6
Outputs:
- output: bfloat16 [12, 1024, 960], P('dp', 'ctx')
- input_grad: bfloat16 [12, 1024, 960], P('dp', 'ctx')
- gain_one_grad: float32 [960], P('ctx')
- w_query_grad: float32 [960, 960], P('dp', 'ctx')
- w_key_grad: float32 [960, 320], P('dp', 'ctx')
- w_value_grad: float32 [960, 320], P('dp', 'ctx')
- w_out_grad: float32 [960, 960], P('dp', 'ctx')
- gain_two_grad: float32 [960], P('ctx')
- w_gate_grad: float32 [960, 2560], P('dp', 'ctx')
- w_up_grad: float32 [960, 2560], P('dp', 'ctx')
- w_down_grad: float32 [2560, 960], P('dp', 'ctx')
Inputs may be any that keep to these rules, and one draw needn't show every extreme that they name: `segment_ids`: along each sequence the ids never fall; each id marks one document of 1 to 512 tokens, and some document has exactly 512.
All inputs are finite; a program needn't handle non-finite values.
Results may differ from a plain program's by a relative error of at most 0.023.
Values may be sent and summed in bfloat16 or wider, within the bound.
No kernel may reach another device: no remote copies, remote signals or barrier semaphores. Data moves between devices by JAX's collectives and lax.ppermute only.
A program may use at most 192 MiB of HBM per device.

v0:
```python
import math

import jax
import jax.numpy as jnp
from jax import lax
from jax.sharding import PartitionSpec as P

QUERY_HEADS = 15
KEY_VALUE_HEADS = 5
HEAD_DIM = 64


epsilon = 1e-05
rope_base = 10000.0
masked = -1e30


def rotate(values):
    half_width = values.shape[-1] // 2
    return jnp.concatenate([-values[..., half_width:], values[..., :half_width]], axis=-1)


def rope_tables(positions, head_width):
    freq_index = jnp.arange(head_width // 2, dtype=jnp.float32)
    frequency = jnp.exp(freq_index * (-2.0 * math.log(rope_base) / head_width))
    angles = positions[:, None] * frequency[None, :]
    angles = jnp.concatenate([angles, angles], axis=-1)
    return (jnp.cos(angles), jnp.sin(angles))


def rms_scale(values):
    return lax.rsqrt(jnp.mean(values * values, axis=-1, keepdims=True) + epsilon)


def inverse_rotate(grads, cosine_table, sine_values):
    return grads * cosine_table - rotate(grads * sine_values)


def collect(
    query_weight,
    key_weight,
    value_weight,
    output_weight,
    gate_weight,
    up_weight,
    down_weight,
    gain_one,
    gain_two,
):
    (
        query_weight,
        key_weight,
        value_weight,
        output_weight,
        gate_weight,
        up_weight,
        down_weight,
        gain_one,
        gain_two,
    ) = (
        lax.all_gather(query_weight, "ctx", axis=1, tiled=True),
        lax.all_gather(key_weight, "ctx", axis=1, tiled=True),
        lax.all_gather(value_weight, "ctx", axis=1, tiled=True),
        lax.all_gather(output_weight, "ctx", axis=1, tiled=True),
        lax.all_gather(gate_weight, "ctx", axis=1, tiled=True),
        lax.all_gather(up_weight, "ctx", axis=1, tiled=True),
        lax.all_gather(down_weight, "ctx", axis=1, tiled=True),
        lax.all_gather(gain_one, "ctx", axis=0, tiled=True),
        lax.all_gather(gain_two, "ctx", axis=0, tiled=True),
    )
    query_weight, key_weight, value_weight, output_weight, gate_weight, up_weight, down_weight = (
        lax.all_gather(query_weight, "dp", axis=0, tiled=True),
        lax.all_gather(key_weight, "dp", axis=0, tiled=True),
        lax.all_gather(value_weight, "dp", axis=0, tiled=True),
        lax.all_gather(output_weight, "dp", axis=0, tiled=True),
        lax.all_gather(gate_weight, "dp", axis=0, tiled=True),
        lax.all_gather(up_weight, "dp", axis=0, tiled=True),
        lax.all_gather(down_weight, "dp", axis=0, tiled=True),
    )
    return (
        query_weight,
        key_weight,
        value_weight,
        output_weight,
        gate_weight,
        up_weight,
        down_weight,
        gain_one,
        gain_two,
    )


def spread(g_query, g_key, g_value, g_out, g_gate, g_up, g_down, g_gain_one, g_gain_two):
    g_query, g_key, g_value, g_out, g_gate, g_up, g_down = (
        lax.psum_scatter(
            g_query.astype(jnp.bfloat16), "dp", scatter_dimension=0, tiled=True
        ).astype(jnp.float32),
        lax.psum_scatter(g_key.astype(jnp.bfloat16), "dp", scatter_dimension=0, tiled=True).astype(
            jnp.float32
        ),
        lax.psum_scatter(
            g_value.astype(jnp.bfloat16), "dp", scatter_dimension=0, tiled=True
        ).astype(jnp.float32),
        lax.psum_scatter(g_out.astype(jnp.bfloat16), "dp", scatter_dimension=0, tiled=True).astype(
            jnp.float32
        ),
        lax.psum_scatter(g_gate.astype(jnp.bfloat16), "dp", scatter_dimension=0, tiled=True).astype(
            jnp.float32
        ),
        lax.psum_scatter(g_up.astype(jnp.bfloat16), "dp", scatter_dimension=0, tiled=True).astype(
            jnp.float32
        ),
        lax.psum_scatter(g_down.astype(jnp.bfloat16), "dp", scatter_dimension=0, tiled=True).astype(
            jnp.float32
        ),
    )
    g_query, g_key, g_value, g_out, g_gate, g_up, g_down, g_gain_one, g_gain_two = (
        lax.psum_scatter(
            g_query.astype(jnp.bfloat16), "ctx", scatter_dimension=1, tiled=True
        ).astype(jnp.float32),
        lax.psum_scatter(g_key.astype(jnp.bfloat16), "ctx", scatter_dimension=1, tiled=True).astype(
            jnp.float32
        ),
        lax.psum_scatter(
            g_value.astype(jnp.bfloat16), "ctx", scatter_dimension=1, tiled=True
        ).astype(jnp.float32),
        lax.psum_scatter(g_out.astype(jnp.bfloat16), "ctx", scatter_dimension=1, tiled=True).astype(
            jnp.float32
        ),
        lax.psum_scatter(
            g_gate.astype(jnp.bfloat16), "ctx", scatter_dimension=1, tiled=True
        ).astype(jnp.float32),
        lax.psum_scatter(g_up.astype(jnp.bfloat16), "ctx", scatter_dimension=1, tiled=True).astype(
            jnp.float32
        ),
        lax.psum_scatter(
            g_down.astype(jnp.bfloat16), "ctx", scatter_dimension=1, tiled=True
        ).astype(jnp.float32),
        lax.psum_scatter(
            g_gain_one.astype(jnp.bfloat16), "ctx", scatter_dimension=0, tiled=True
        ).astype(jnp.float32),
        lax.psum_scatter(
            g_gain_two.astype(jnp.bfloat16), "ctx", scatter_dimension=0, tiled=True
        ).astype(jnp.float32),
    )
    g_gain_one, g_gain_two = lax.psum((g_gain_one, g_gain_two), "dp")
    return (g_query, g_key, g_value, g_out, g_gate, g_up, g_down, g_gain_one, g_gain_two)


def per_device(
    inputs,
    gain_one,
    query_weight,
    key_weight,
    value_weight,
    output_weight,
    gain_two,
    gate_weight,
    up_weight,
    down_weight,
    segment_ids,
    cotangent,
):
    sequence_total, total_rows, model_width = inputs.shape
    query_group_width = QUERY_HEADS // KEY_VALUE_HEADS
    score_scale = HEAD_DIM ** (-0.5)
    f32 = jnp.float32
    b16 = jnp.bfloat16
    wq_full, wk_full, wv_full, wo_full, wg_full, wu_full, wd_full, gain_a, gain_b = collect(
        query_weight,
        key_weight,
        value_weight,
        output_weight,
        gate_weight,
        up_weight,
        down_weight,
        gain_one,
        gain_two,
    )
    query_pos = lax.axis_index("ctx") * total_rows + jnp.arange(total_rows, dtype=jnp.int32)
    cosine_table, sine_values = rope_tables(query_pos.astype(f32), HEAD_DIM)
    cosine_table = cosine_table[None, :, None, :]
    sine_values = sine_values[None, :, None, :]
    input_single = inputs.astype(f32)
    inv_one = rms_scale(input_single)
    first_normed = (input_single * inv_one * gain_a.astype(f32)).astype(b16)
    query_pre = jnp.einsum(
        "std,de->ste", first_normed, wq_full, preferred_element_type=f32
    ).reshape(sequence_total, total_rows, QUERY_HEADS, HEAD_DIM)
    key_unrotated = jnp.einsum(
        "std,de->ste", first_normed, wk_full, preferred_element_type=f32
    ).reshape(sequence_total, total_rows, KEY_VALUE_HEADS, HEAD_DIM)
    value_lowered = jnp.einsum(
        "std,de->ste", first_normed, wv_full, preferred_element_type=f32
    ).astype(b16)
    query_rotated = (query_pre * cosine_table + rotate(query_pre) * sine_values).astype(b16)
    key_rotated = (key_unrotated * cosine_table + rotate(key_unrotated) * sine_values).astype(b16)
    keys_all, values_all, segs_all = (
        lax.all_gather(
            key_rotated.reshape(sequence_total, total_rows, KEY_VALUE_HEADS * HEAD_DIM),
            "ctx",
            axis=1,
            tiled=True,
        ),
        lax.all_gather(value_lowered, "ctx", axis=1, tiled=True),
        lax.all_gather(segment_ids, "ctx", axis=1, tiled=True),
    )
    sequence_length = keys_all.shape[1]
    key_window = 512
    span_count = sequence_length // key_window
    query_head_states = query_rotated.reshape(
        sequence_total, total_rows, KEY_VALUE_HEADS, query_group_width, HEAD_DIM
    )

    def block_scores(step_index):
        leading_key = step_index * key_window
        key_rows = lax.dynamic_slice_in_dim(keys_all, leading_key, key_window, 1).reshape(
            sequence_total, key_window, KEY_VALUE_HEADS, HEAD_DIM
        )
        value_rows = lax.dynamic_slice_in_dim(values_all, leading_key, key_window, 1).reshape(
            sequence_total, key_window, KEY_VALUE_HEADS, HEAD_DIM
        )
        seg_keys = lax.dynamic_slice_in_dim(segs_all, leading_key, key_window, 1)
        key_pos = leading_key + jnp.arange(key_window, dtype=jnp.int32)
        raw_scores = (
            jnp.einsum("stgrd,skgd->sgrtk", query_head_states, key_rows, preferred_element_type=f32)
            * score_scale
        )
        allowed = (segment_ids[:, :, None] == seg_keys[:, None, :]) & (
            query_pos[None, :, None] >= key_pos[None, None, :]
        )
        scores = jnp.where(allowed[:, None, None], raw_scores, masked)
        return (scores, key_rows, value_rows)

    def first_pass(step_index, carry):
        row_max, row_sum = carry
        scores, key_rows, value_rows = block_scores(step_index)
        new_max = jnp.maximum(row_max, jnp.max(scores, axis=-1))
        row_sum = row_sum * jnp.exp(row_max - new_max) + jnp.sum(
            jnp.exp(scores - new_max[..., None]), axis=-1
        )
        return (new_max, row_sum)

    statistic_layout = (sequence_total, KEY_VALUE_HEADS, query_group_width, total_rows)
    row_max, row_sum = lax.fori_loop(
        0,
        span_count,
        first_pass,
        (jnp.full(statistic_layout, masked, f32), jnp.zeros(statistic_layout, f32)),
    )
    log_total = row_max + jnp.log(row_sum)

    def second_pass(step_index, att_sum):
        scores, key_rows, value_rows = block_scores(step_index)
        probs = jnp.exp(scores - log_total[..., None])
        return att_sum + jnp.einsum(
            "sgrtk,skgd->stgrd", probs.astype(b16), value_rows, preferred_element_type=f32
        )

    head_layout = (sequence_total, total_rows, KEY_VALUE_HEADS, query_group_width, HEAD_DIM)
    att_sum = lax.fori_loop(0, span_count, second_pass, jnp.zeros(head_layout, f32))
    att_low = att_sum.reshape(sequence_total, total_rows, QUERY_HEADS * HEAD_DIM).astype(b16)
    residual_state = input_single + jnp.einsum(
        "ste,ed->std", att_low, wo_full, preferred_element_type=f32
    )
    inv_two = rms_scale(residual_state)
    second_normed = (residual_state * inv_two * gain_b.astype(f32)).astype(b16)
    gate_preactivation = jnp.einsum(
        "std,df->stf", second_normed, wg_full, preferred_element_type=f32
    )
    up_preactivation = jnp.einsum("std,df->stf", second_normed, wu_full, preferred_element_type=f32)
    hidden_state = (jax.nn.silu(gate_preactivation) * up_preactivation).astype(b16)
    output = (
        residual_state
        + jnp.einsum("stf,fd->std", hidden_state, wd_full, preferred_element_type=f32)
    ).astype(b16)
    wq_full, wk_full, wv_full, wo_full, wg_full, wu_full, wd_full, gain_a, gain_b = collect(
        query_weight,
        key_weight,
        value_weight,
        output_weight,
        gate_weight,
        up_weight,
        down_weight,
        gain_one,
        gain_two,
    )
    gain_af = gain_a.astype(f32)
    gain_bf = gain_b.astype(f32)
    out_grad = cotangent.astype(f32)
    g_down = jnp.einsum("stf,std->fd", hidden_state, cotangent, preferred_element_type=f32)
    d_hidden = jnp.einsum("std,fd->stf", cotangent, wd_full, preferred_element_type=f32)
    sigmoid_gate = jax.nn.sigmoid(gate_preactivation)
    d_up = (d_hidden * gate_preactivation * sigmoid_gate).astype(b16)
    d_gate = (
        d_hidden
        * up_preactivation
        * sigmoid_gate
        * (1.0 + gate_preactivation * (1.0 - sigmoid_gate))
    ).astype(b16)
    g_gate = jnp.einsum("std,stf->df", second_normed, d_gate, preferred_element_type=f32)
    g_up = jnp.einsum("std,stf->df", second_normed, d_up, preferred_element_type=f32)
    d_normed_two = jnp.einsum(
        "stf,df->std", d_gate, wg_full, preferred_element_type=f32
    ) + jnp.einsum("stf,df->std", d_up, wu_full, preferred_element_type=f32)
    g_gain_two = jnp.sum(d_normed_two * residual_state * inv_two, axis=(0, 1))
    scaled_two = gain_bf * d_normed_two
    d_mid = (
        out_grad
        + inv_two * scaled_two
        - residual_state
        * inv_two**3
        * jnp.mean(scaled_two * residual_state, axis=-1, keepdims=True)
    )
    d_mid_low = d_mid.astype(b16)
    g_out = jnp.einsum("ste,std->ed", att_low, d_mid_low, preferred_element_type=f32)
    attention_output_grad = jnp.einsum(
        "std,ed->ste", d_mid_low, wo_full, preferred_element_type=f32
    ).astype(b16)
    attention_heads_grad = attention_output_grad.reshape(
        sequence_total, total_rows, KEY_VALUE_HEADS, query_group_width, HEAD_DIM
    )
    delta = jnp.transpose(
        jnp.sum(attention_heads_grad.astype(f32) * att_sum, axis=-1), (0, 2, 3, 1)
    )

    def third_pass(step_index, carry):
        dq_sum, key_grad_total, value_grad_total = carry
        leading_key = step_index * key_window
        scores, key_rows, value_rows = block_scores(step_index)
        probs = jnp.exp(scores - log_total[..., None])
        d_probs = jnp.einsum(
            "stgrd,skgd->sgrtk", attention_heads_grad, value_rows, preferred_element_type=f32
        )
        d_scores = (probs * (d_probs - delta[..., None])).astype(b16)
        value_grad_rows = jnp.einsum(
            "sgrtk,stgrd->skgd", probs.astype(b16), attention_heads_grad, preferred_element_type=f32
        )
        key_grad_rows = (
            jnp.einsum("sgrtk,stgrd->skgd", d_scores, query_head_states, preferred_element_type=f32)
            * score_scale
        )
        dq_sum = (
            dq_sum
            + jnp.einsum("sgrtk,skgd->stgrd", d_scores, key_rows, preferred_element_type=f32)
            * score_scale
        )
        key_grad_total = lax.dynamic_update_slice_in_dim(
            key_grad_total,
            key_grad_rows.reshape(sequence_total, key_window, KEY_VALUE_HEADS * HEAD_DIM),
            leading_key,
            1,
        )
        value_grad_total = lax.dynamic_update_slice_in_dim(
            value_grad_total,
            value_grad_rows.reshape(sequence_total, key_window, KEY_VALUE_HEADS * HEAD_DIM),
            leading_key,
            1,
        )
        return (dq_sum, key_grad_total, value_grad_total)

    key_value_layout = (sequence_total, sequence_length, KEY_VALUE_HEADS * HEAD_DIM)
    dq_sum, key_grad_total, value_grad_total = lax.fori_loop(
        0,
        span_count,
        third_pass,
        (
            jnp.zeros(head_layout, f32),
            jnp.zeros(key_value_layout, f32),
            jnp.zeros(key_value_layout, f32),
        ),
    )
    key_grad_local, dv_mine = (
        lax.psum_scatter(
            key_grad_total.astype(jnp.bfloat16), "ctx", scatter_dimension=1, tiled=True
        ).astype(jnp.float32),
        lax.psum_scatter(
            value_grad_total.astype(jnp.bfloat16), "ctx", scatter_dimension=1, tiled=True
        ).astype(jnp.float32),
    )
    d_query = (
        inverse_rotate(
            dq_sum.reshape(sequence_total, total_rows, QUERY_HEADS, HEAD_DIM),
            cosine_table,
            sine_values,
        )
        .astype(b16)
        .reshape(sequence_total, total_rows, QUERY_HEADS * HEAD_DIM)
    )
    d_key = (
        inverse_rotate(
            key_grad_local.reshape(sequence_total, total_rows, KEY_VALUE_HEADS, HEAD_DIM),
            cosine_table,
            sine_values,
        )
        .astype(b16)
        .reshape(sequence_total, total_rows, KEY_VALUE_HEADS * HEAD_DIM)
    )
    d_value = dv_mine.astype(b16)
    g_query = jnp.einsum("std,ste->de", first_normed, d_query, preferred_element_type=f32)
    g_key = jnp.einsum("std,ste->de", first_normed, d_key, preferred_element_type=f32)
    g_value = jnp.einsum("std,ste->de", first_normed, d_value, preferred_element_type=f32)
    d_normed_one = (
        jnp.einsum("ste,de->std", d_query, wq_full, preferred_element_type=f32)
        + jnp.einsum("ste,de->std", d_key, wk_full, preferred_element_type=f32)
        + jnp.einsum("ste,de->std", d_value, wv_full, preferred_element_type=f32)
    )
    g_gain_one = jnp.sum(d_normed_one * input_single * inv_one, axis=(0, 1))
    scaled_one = gain_af * d_normed_one
    input_grad = (
        d_mid
        + inv_one * scaled_one
        - input_single * inv_one**3 * jnp.mean(scaled_one * input_single, axis=-1, keepdims=True)
    ).astype(b16)
    g_query, g_key, g_value, g_out, g_gate, g_up, g_down, g_gain_one, g_gain_two = spread(
        g_query, g_key, g_value, g_out, g_gate, g_up, g_down, g_gain_one, g_gain_two
    )
    return (
        output,
        input_grad,
        g_gain_one,
        g_query,
        g_key,
        g_value,
        g_out,
        g_gain_two,
        g_gate,
        g_up,
        g_down,
    )


def solution(mesh):
    placed = (
        P("dp", "ctx", None),
        P("ctx"),
        P("dp", "ctx"),
        P("dp", "ctx"),
        P("dp", "ctx"),
        P("dp", "ctx"),
        P("ctx"),
        P("dp", "ctx"),
        P("dp", "ctx"),
        P("dp", "ctx"),
        P("dp", "ctx"),
        P("dp", "ctx", None),
    )
    return jax.shard_map(
        per_device,
        mesh=mesh,
        in_specs=placed,
        out_specs=(
            P("dp", "ctx", None),
            P("dp", "ctx", None),
            P("ctx"),
            P("dp", "ctx"),
            P("dp", "ctx"),
            P("dp", "ctx"),
            P("dp", "ctx"),
            P("ctx"),
            P("dp", "ctx"),
            P("dp", "ctx"),
            P("dp", "ctx"),
        ),
        check_vma=False,
    )
```

profile of v0, /device:TPU:0, one launch (start us, length us, event | category | flops | bytes accessed | tf_op | source)
XLA Modules:
  0.0 1371.2 jit_solution(14728444002015944315)
XLA Ops:
  10.4 33.4 %all_gather.81 = bf16[240,960]{0,1:T(8,128)(2,1)S(1)} all-gather(bf16[240,120]{0,1:T(8,128)(2,1)S(1)} %copy.70), channel_id=1, replica_groups=mesh['dp'=4,'ctx'=8] {'ctx'}, dimensions={1}, use_global_device_ids=true | all-gather | bytes 518400 | tf_op jit(solution)/shard_map/all_gather | solution.py:61
  46.7 21.3 %all-reduce.7 = (bf16[960]{0:T(1024)(128)(2,1)S(1)}, bf16[960]{0:T(1024)(128)(2,1)S(1)}) all-reduce(bf16[960]{0:T(1024)(128)(2,1)S(1)} %dynamic-update-slice, bf16[960]{0:T(1024)(128)(2,1)S(1)} %dynamic-update-slice.1), channel_id=1, replica_groups=mesh['dp'=4,'ctx'=8] {'ctx'}, use_global_device_ids=true, to_apply=%add | all-reduce | flops 1920 | bytes 7680
  68.0 31.1 %all_gather.78 = bf16[240,320]{0,1:T(8,128)(2,1)S(1)} all-gather(bf16[240,40]{0,1:T(8,128)(2,1)S(1)} %copy-done.37), channel_id=1, replica_groups=mesh['dp'=4,'ctx'=8] {'ctx'}, dimensions={1}, use_global_device_ids=true | all-gather | bytes 172800 | tf_op jit(solution)/shard_map/all_gather | solution.py:62
  99.1 8.0 all-gather.1
  111.4 30.9 %all_gather.74 = bf16[240,320]{0,1:T(8,128)(2,1)S(1)} all-gather(bf16[240,40]{0,1:T(8,128)(2,1)S(1)} %copy-done.38), channel_id=1, replica_groups=mesh['dp'=4,'ctx'=8] {'ctx'}, dimensions={1}, use_global_device_ids=true | all-gather | bytes 172800 | tf_op jit(solution)/shard_map/all_gather | solution.py:63
  152.0 31.5 %all_gather.83 = bf16[240,960]{0,1:T(8,128)(2,1)S(1)} all-gather(bf16[240,120]{0,1:T(8,128)(2,1)S(1)} %copy.73), channel_id=1, replica_groups=mesh['dp'=4,'ctx'=8] {'ctx'}, dimensions={1}, use_global_device_ids=true | all-gather | bytes 518400 | tf_op jit(solution)/shard_map/all_gather | solution.py:64
  187.9 26.3 %all_gather.77 = s32[3,1024]{1,0:T(4,128)S(1)} all-gather(s32[3,128]{1,0:T(4,128)S(1)} %copy-done.31), channel_id=1, replica_groups=mesh['dp'=4,'ctx'=8] {'ctx'}, dimensions={1}, use_global_device_ids=true | all-gather | bytes 13824 | tf_op jit(solution)/shard_map/all_gather | solution.py:206
  220.4 30.0 %while.48 = (s32[]{:T(128)}, f32[3,5,3,128]{3,2,1,0:T(4,128)S(1)}, f32[3,5,3,128]{3,2,1,0:T(4,128)S(1)}, s32[3,128]{1,0:T(4,128)S(1)}, s32[3,1024]{1,0:T(4,128)S...) while((s32[]{:T(128)}, f32[3,5,3,128]{3,2,1,0:T(4,128)S(1)}, ...), condition=%wide.region_4.5_spmd.clone, body=%wide.region_1.4_spmd.clone.sunk | while | flops 398619392 | bytes 28325060 | solution.py:245
  250.4 18.2 %all-gather.13.cloned.1.call-done = bf16[3,1024,320]{1,2,0:T(8,128)(2,1)} async-done(((bf16[3,128,320]{1,2,0:T(8,128)(2,1)}), bf16[3,1024,320]{1,2,0:T(8,128)(2,1)}) %all-gather.13.cloned.1.call-update) | async-done | bytes 1966096 | tf_op jit(solution)/shard_map/all_gather | solution.py:205
  268.6 19.0 %while.49 = (s32[]{:T(128)}, f32[3,128,5,3,64]{1,4,3,2,0:T(8,128)}, bf16[3,1024,320]{1,2,0:T(8,128)(2,1)}, s32[3,128]{1,0:T(4,128)S(1)}, s32[3,1024]{1,0:T(4,128...) while((s32[]{:T(128)}, f32[3,128,5,3,64]{1,4,3,2,0:T(8,128)}, ...), condition=%wide.region_6.7_spmd.clone, body=%wide.region_5.6_spmd.clone.sunk | while | flops 767967872 | bytes 10157261 | solution.py:261
  296.1 34.9 %all-gather.31.cloned.1.call-done = bf16[2560,960]{0,1:T(8,128)(2,1)} async-done(((bf16[640,960]{0,1:T(8,128)(2,1)}), bf16[2560,960]{0,1:T(8,128)(2,1)}) %all-gather.31.cloned.1.call-update) | async-done | bytes 4915216 | tf_op jit(solution)/shard_map/all_gather | solution.py:78
  337.6 33.6 %all-gather.27.cloned.1.call-done = bf16[960,2560]{1,0:T(8,128)(2,1)} async-done(((bf16[240,2560]{1,0:T(8,128)(2,1)}), bf16[960,2560]{1,0:T(8,128)(2,1)}) %all-gather.27.cloned.1.call-update) | async-done | bytes 4915216 | tf_op jit(solution)/shard_map/all_gather | solution.py:77
  377.9 33.3 %all-gather.23.cloned.1.call-done = bf16[960,2560]{1,0:T(8,128)(2,1)} async-done(((bf16[240,2560]{1,0:T(8,128)(2,1)}), bf16[960,2560]{1,0:T(8,128)(2,1)}) %all-gather.23.cloned.1.call-update) | async-done | bytes 4915216 | tf_op jit(solution)/shard_map/all_gather | solution.py:76
  411.2 10.4 multiply_convert_fusion.1
  437.8 60.5 %while.50 = (s32[]{:T(128)}, f32[3,128,5,3,64]{1,4,3,2,0:T(8,128)S(1)}, bf16[3,1024,320]{1,2,0:T(8,128)(2,1)}, bf16[3,1024,320]{1,2,0:T(8,128)(2,1)}, bf16[3,102...) while((s32[]{:T(128)}, ...), condition=%wide.region_11.12_spmd.clone, body=%wide.region_10.11_spmd.clone.sunk | while | flops 1919476352 | bytes 176779728 | solution.py:363
  532.1 46.9 %reduce-scatter.49.cloned.1.call-done = bf16[128,960]{1,0:T(8,128)(2,1)} async-done(((bf16[1024,960]{1,0:T(8,128)(2,1)}), bf16[128,960]{1,0:T(8,128)(2,1)}) %reduce-scatter.49.cloned.1.call-update) | async-done | bytes 245776
  583.4 65.6 %reduce-scatter.51.cloned.1.call-done = bf16[128,960]{1,0:T(8,128)(2,1)} async-done(((bf16[1024,960]{1,0:T(8,128)(2,1)}), bf16[128,960]{1,0:T(8,128)(2,1)}) %reduce-scatter.51.cloned.1.call-update) | async-done | bytes 245776
  673.1 7.9 copy.111
  683.3 31.2 %reduce-scatter.43.cloned.1.call-done = bf16[240,960]{1,0:T(8,128)(2,1)} async-done(((bf16[960,960]{1,0:T(8,128)(2,1)}), bf16[240,960]{1,0:T(8,128)(2,1)}) %reduce-scatter.43.cloned.1.call-update) | async-done | bytes 460816 | tf_op jit(solution)/shard_map/reduce_scatter | solution.py:104
  716.5 23.9 %reduce-scatter.55.cloned.1.call-done = bf16[240,320]{1,0:T(8,128)(2,1)} async-done(((bf16[960,320]{1,0:T(8,128)(2,1)}), bf16[240,320]{1,0:T(8,128)(2,1)}) %reduce-scatter.55.cloned.1.call-update) | async-done | bytes 153616
  742.2 23.7 %reduce-scatter.57.cloned.1.call-done = bf16[240,320]{1,0:T(8,128)(2,1)} async-done(((bf16[960,320]{1,0:T(8,128)(2,1)}), bf16[240,320]{1,0:T(8,128)(2,1)}) %reduce-scatter.57.cloned.1.call-update) | async-done | bytes 153616
  767.7 49.9 %reduce-scatter.45.cloned.1.call-done = bf16[240,2560]{1,0:T(8,128)(2,1)} async-done(((bf16[960,2560]{1,0:T(8,128)(2,1)}), bf16[240,2560]{1,0:T(8,128)(2,1)}) %reduce-scatter.45.cloned.1.call-update) | async-done | bytes 1228816 | tf_op jit(solution)/shard_map/reduce_scatter | solution.py:107
  820.1 49.4 %reduce-scatter.47.cloned.1.call-done = bf16[240,2560]{1,0:T(8,128)(2,1)} async-done(((bf16[960,2560]{1,0:T(8,128)(2,1)}), bf16[240,2560]{1,0:T(8,128)(2,1)}) %reduce-scatter.47.cloned.1.call-update) | async-done | bytes 1228816 | tf_op jit(solution)/shard_map/reduce_scatter | solution.py:110
  872.0 51.5 %reduce-scatter.65.cloned.1.call-done = bf16[640,960]{1,0:T(8,128)(2,1)} async-done(((bf16[2560,960]{1,0:T(8,128)(2,1)}), bf16[640,960]{1,0:T(8,128)(2,1)}) %reduce-scatter.65.cloned.1.call-update) | async-done | bytes 1228816
  939.1 21.4 %all-reduce.6 = (bf16[960]{0:T(1024)(128)(2,1)S(1)}, bf16[960]{0:T(1024)(128)(2,1)S(1)}) all-reduce(bf16[960]{0:T(1024)(128)(2,1)S(1)} %get-tuple-element.699, bf16[960]{0:T(1024)(128)(2,1)S(1)} %copy-done.43), channel_id=4, replica_groups=mesh['dp'=4,'ctx'=8] {'ctx'}, use_global_device_ids=true, to_apply=%region_16.17.clone | all-reduce | flops 1920 | bytes 7680
  969.4 17.0 %reduce-scatter.53.cloned.1.call-done = bf16[120,240]{1,0:T(8,128)(2,1)} async-done(((bf16[960,240]{1,0:T(8,128)(2,1)}), bf16[120,240]{1,0:T(8,128)(2,1)}) %reduce-scatter.53.cloned.1.call-update) | async-done | bytes 57616
  988.0 60.5 %reduce-scatter.59.cloned.1.call-done = bf16[120,240]{1,0:T(8,128)(2,1)} async-done(((bf16[960,240]{1,0:T(8,128)(2,1)}), bf16[120,240]{1,0:T(8,128)(2,1)}) %reduce-scatter.59.cloned.1.call-update) | async-done | bytes 57616
  1050.1 55.7 %reduce-scatter.39.cloned.1.call-done = bf16[240,40]{0,1:T(8,128)(2,1)} async-done(((bf16[240,320]{0,1:T(8,128)(2,1)}), bf16[240,40]{0,1:T(8,128)(2,1)}) %reduce-scatter.39.cloned.1.call-update) | async-done | bytes 19216 | tf_op jit(solution)/shard_map/reduce_scatter | solution.py:121
  1107.2 56.1 %reduce-scatter.41.cloned.1.call-done = bf16[240,40]{0,1:T(8,128)(2,1)} async-done(((bf16[240,320]{0,1:T(8,128)(2,1)}), bf16[240,40]{0,1:T(8,128)(2,1)}) %reduce-scatter.41.cloned.1.call-update) | async-done | bytes 19216 | tf_op jit(solution)/shard_map/reduce_scatter | solution.py:124
  1164.7 65.6 %reduce-scatter.61.cloned.1.call-done = bf16[320,240]{1,0:T(8,128)(2,1)} async-done(((bf16[2560,240]{1,0:T(8,128)(2,1)}), bf16[320,240]{1,0:T(8,128)(2,1)}) %reduce-scatter.61.cloned.1.call-update) | async-done | bytes 153616
  1232.2 65.1 %reduce-scatter.63.cloned.1.call-done = bf16[320,240]{1,0:T(8,128)(2,1)} async-done(((bf16[2560,240]{1,0:T(8,128)(2,1)}), bf16[320,240]{1,0:T(8,128)(2,1)}) %reduce-scatter.63.cloned.1.call-update) | async-done | bytes 153616
  1299.3 63.3 %reduce-scatter.67.cloned.1.call-done = bf16[640,120]{0,1:T(8,128)(2,1)} async-done(((bf16[640,960]{0,1:T(8,128)(2,1)}), bf16[640,120]{0,1:T(8,128)(2,1)}) %reduce-scatter.67.cloned.1.call-update) | async-done | bytes 153616
  (350 shorter events, 285.8 us)
Async XLA Ops:
  7.2 60.8 %copy-start.37 = (bf16[240,40]{0,1:T(8,128)(2,1)S(1)}, bf16[240,40]{0,1:T(8,128)(2,1)}, u32[]{:S(2)}) copy-start(bf16[240,40]{0,1:T(8,128)(2,1)} %param.21) | copy-start | bytes 57604
  7.2 177.3 %all-gather.29.cloned.1.call-start = ((), (), s32[]{:S(2)}) async-start(), calls=%async_computation.24 | async-start | bytes 1382400 | tf_op jit(solution)/shard_map/all_gather | solution.py:67
  8.0 177.4 %all-gather.25.cloned.1.call-start = ((), (), s32[]{:S(2)}) async-start(), calls=%async_computation.22 | async-start | bytes 1474560 | tf_op jit(solution)/shard_map/all_gather | solution.py:66
  8.7 205.5 %all-gather.21.cloned.1.call-start = ((), (), s32[]{:S(2)}) async-start(), calls=%async_computation.20 | async-start | bytes 1474560 | tf_op jit(solution)/shard_map/all_gather | solution.py:65
  9.4 207.5 %all-gather.17.cloned.1.call-start = ((), (), s32[]{:S(2)}) async-start(), calls=%async_computation.18 | async-start | bytes 2457600 | tf_op jit(solution)/shard_map/all_gather | solution.py:72
  44.9 63.6 %copy-start.8 = (bf16[3,128,960]{1,2,0:T(8,128)(2,1)S(1)}, bf16[3,128,960]{1,2,0:T(8,128)(2,1)}, u32[]{:S(2)}) copy-start(bf16[3,128,960]{1,2,0:T(8,128)(2,1)} %param.18) | copy-start | bytes 2211844
  44.9 175.5 %all-gather.15.cloned.1.call-start = ((), (), s32[]{:S(2)}) async-start(), calls=%async_computation.17 | async-start | bytes 2211840 | tf_op jit(solution)/shard_map/all_gather | solution.py:199
  68.0 148.9 %copy-start.35 = (f32[960]{0:T(1024)}, f32[960]{0:T(1024)S(1)}, u32[]{:S(2)}) copy-start(f32[960]{0:T(1024)S(1)} %convert_element_type.177) | copy-start | bytes 11524
  108.4 111.6 %copy-start.27 = (f32[128,64]{0,1:T(8,128)}, f32[128,64]{0,1:T(8,128)S(1)}, u32[]{:S(2)}) copy-start(f32[128,64]{0,1:T(8,128)S(1)} %get-tuple-element.785) | copy-start | bytes 98308
  108.4 111.6 %copy-start.32 = (f32[128,64]{0,1:T(8,128)}, f32[128,64]{0,1:T(8,128)S(1)}, u32[]{:S(2)}) copy-start(f32[128,64]{0,1:T(8,128)S(1)} %get-tuple-element.784) | copy-start | bytes 98308
  109.2 107.8 %copy-start.39 = (f32[3,128]{1,0:T(4,128)}, f32[3,128]{1,0:T(4,128)S(1)}, u32[]{:S(2)}) copy-start(f32[3,128]{1,0:T(4,128)S(1)} %get-tuple-element.787) | copy-start | bytes 4612
  111.4 157.2 %all-gather.13.cloned.1.call-start = ((), (), s32[]{:S(2)}) async-start(), calls=%async_computation.16 | async-start | bytes 2211840 | tf_op jit(solution)/shard_map/all_gather | solution.py:205
  151.8 139.0 %all-gather.19.cloned.1.call-start = ((), (), s32[]{:S(2)}) async-start(), calls=%async_computation.19 | async-start | bytes 2457600 | tf_op jit(solution)/shard_map/all_gather | solution.py:75
  184.5 146.5 %all-gather.31.cloned.1.call-start = ((), (), s32[]{:S(2)}) async-start(), calls=%async_computation.25 | async-start | bytes 6144000 | tf_op jit(solution)/shard_map/all_gather | solution.py:78
  185.2 185.9 %all-gather.27.cloned.1.call-start = ((), (), s32[]{:S(2)}) async-start(), calls=%async_computation.23 | async-start | bytes 6144000 | tf_op jit(solution)/shard_map/all_gather | solution.py:77
  187.8 223.4 %all-gather.23.cloned.1.call-start = ((), (), s32[]{:S(2)}) async-start(), calls=%async_computation.21 | async-start | bytes 6144000 | tf_op jit(solution)/shard_map/all_gather | solution.py:76
  216.6 362.3 %reduce-scatter.49.cloned.1.call-start = ((), (), s32[]{:S(2)}) async-start(), calls=%async_computation.32 | async-start | bytes 2359296
  511.2 137.8 %reduce-scatter.51.cloned.1.call-start = ((), (), s32[]{:S(2)}) async-start(), calls=%async_computation.33 | async-start | bytes 2359296
  523.8 157.3 %reduce-scatter.37.cloned.1.call-start = ((), (), s32[]{:S(2)}) async-start(), calls=%async_computation.26 | async-start | bytes 2457600 | tf_op jit(solution)/shard_map/reduce_scatter | solution.py:95
  529.4 185.0 %reduce-scatter.43.cloned.1.call-start = ((), (), s32[]{:S(2)}) async-start(), calls=%async_computation.29 | async-start | bytes 2457600 | tf_op jit(solution)/shard_map/reduce_scatter | solution.py:104
  532.0 208.4 %reduce-scatter.55.cloned.1.call-start = ((), (), s32[]{:S(2)}) async-start(), calls=%async_computation.35 | async-start | bytes 921600
  583.3 182.6 %reduce-scatter.57.cloned.1.call-start = ((), (), s32[]{:S(2)}) async-start(), calls=%async_computation.36 | async-start | bytes 921600
  654.2 163.5 %reduce-scatter.45.cloned.1.call-start = ((), (), s32[]{:S(2)}) async-start(), calls=%async_computation.30 | async-start | bytes 6144000 | tf_op jit(solution)/shard_map/reduce_scatter | solution.py:107
  660.1 209.3 %reduce-scatter.47.cloned.1.call-start = ((), (), s32[]{:S(2)}) async-start(), calls=%async_computation.31 | async-start | bytes 6144000 | tf_op jit(solution)/shard_map/reduce_scatter | solution.py:110
  666.1 257.3 %reduce-scatter.65.cloned.1.call-start = ((), (), s32[]{:S(2)}) async-start(), calls=%async_computation.40 | async-start | bytes 6553600
  681.0 305.4 %reduce-scatter.53.cloned.1.call-start = ((), (), s32[]{:S(2)}) async-start(), calls=%async_computation.34 | async-start | bytes 552960
  683.2 365.3 %reduce-scatter.59.cloned.1.call-start = ((), (), s32[]{:S(2)}) async-start(), calls=%async_computation.37 | async-start | bytes 552960
  716.5 389.4 %reduce-scatter.39.cloned.1.call-start = ((), (), s32[]{:S(2)}) async-start(), calls=%async_computation.27 | async-start | bytes 184320 | tf_op jit(solution)/shard_map/reduce_scatter | solution.py:121
  742.1 421.2 %reduce-scatter.41.cloned.1.call-start = ((), (), s32[]{:S(2)}) async-start(), calls=%async_computation.28 | async-start | bytes 184320 | tf_op jit(solution)/shard_map/reduce_scatter | solution.py:124
  767.7 462.6 %reduce-scatter.61.cloned.1.call-start = ((), (), s32[]{:S(2)}) async-start(), calls=%async_computation.38 | async-start | bytes 1474560
  820.1 477.3 %reduce-scatter.63.cloned.1.call-start = ((), (), s32[]{:S(2)}) async-start(), calls=%async_computation.39 | async-start | bytes 1474560
  871.9 490.6 %reduce-scatter.67.cloned.1.call-start = ((), (), s32[]{:S(2)}) async-start(), calls=%async_computation.41 | async-start | bytes 1382400
  (55 other events, 460.6 us)
Sparse Core Ops, SparseCore 0:
  10.2 45.0 all-gather.28
  57.5 42.0 all-gather.24
  101.8 41.3 all-gather.20
  145.1 20.7 all-gather.16
  168.4 50.1 all-gather.14
  221.0 47.6 all-gather.12
  270.8 20.0 all-gather.18
  292.4 38.5 all-gather.30
  332.5 38.5 all-gather.26
  372.6 38.5 all-gather.22
  511.3 67.6 reduce-scatter.48
  582.4 66.5 reduce-scatter.50
  651.5 29.6 reduce-scatter.36
  683.8 30.6 reduce-scatter.42
  717.4 22.9 reduce-scatter.54
  742.9 22.9 reduce-scatter.56
  768.3 49.2 reduce-scatter.44
  820.2 49.1 reduce-scatter.46
  872.0 51.3 reduce-scatter.64
  927.0 59.3 reduce-scatter.52
  990.1 58.3 reduce-scatter.58
  1052.5 53.2 reduce-scatter.38
  1109.9 53.3 reduce-scatter.40
  1166.9 63.3 reduce-scatter.60
  1234.1 63.2 reduce-scatter.62
  1301.1 61.4 reduce-scatter.66
where the time goes:
time: 1380 us; the launch traced here: 1370 us
  waiting for transfers between devices  849 us (62%)
  blocking collectives  217 us (16%)
  matrix products  146 us (11%)
  local copies, waits for them, and re-layouts  106 us (8%)
  other arithmetic  33.6 us (2%)
  between operations  16.7 us (1%)
    unnamed x36, waiting for transfers between devices  486 us
    unnamed x123, local copies, waits for them, and re-layouts  72.4 us
    reduce_scatter x1, waiting for transfers between devices, spread(): lax.psum_scatter(g_value.astype(jnp.bfloat16), 'ctx', scatter_dimension=1...  56.1 us
    reduce_scatter x1, waiting for transfers between devices, spread(): lax.psum_scatter(g_key.astype(jnp.bfloat16), 'ctx', scatter_dimension=1,...  55.7 us
    reduce_scatter x1, waiting for transfers between devices, spread(): lax.psum_scatter(g_gate.astype(jnp.bfloat16), 'dp', scatter_dimension=0,...  49.9 us
    reduce_scatter x1, waiting for transfers between devices, spread(): lax.psum_scatter(g_up.astype(jnp.bfloat16), 'dp', scatter_dimension=0, ti...  49.4 us
    unnamed x2, blocking collectives  42.7 us
    all_gather x1, waiting for transfers between devices, collect(): lax.all_gather(down_weight, 'dp', axis=0, tiled=True)  34.9 us
  transfers between devices with their start and end apart: 26, of which 21 were waited for; matrix products, arithmetic and copies ran while one was open for 13% of the time, Pallas kernels for 0%

commit v1 on v0

v1 whole, which is shorter than its diff:
```python
import functools
import math

import jax
import jax.numpy as jnp
from jax import lax
from jax.experimental import pallas as pl
from jax.experimental.pallas import tpu as pltpu
from jax.sharding import PartitionSpec as P

QUERY_HEADS = 15
KEY_VALUE_HEADS = 5
HEAD_DIM = 64
GROUP = QUERY_HEADS // KEY_VALUE_HEADS
HALF = HEAD_DIM // 2

epsilon = 1e-05
rope_base = 10000.0
masked = -1e30
f32 = jnp.float32
b16 = jnp.bfloat16


def bits_of(axis, size):
    masks = []
    mask = size // 2
    while mask:
        masks.append((axis, mask))
        mask //= 2
    return masks


def swap(values, axis, mask):
    size = lax.axis_size(axis)
    return lax.ppermute(values, axis, [(i, i ^ mask) for i in range(size)])


def bit(axis, mask):
    return (lax.axis_index(axis) // mask) % 2


def gather(block, order, major):
    rows, cols = block.shape
    have = []
    buf = block[None]
    for step in order:
        got = swap(buf, *step)
        before = [b for b in have if major.index(b) < major.index(step)]
        pre = 2 ** len(before)
        shape = (pre, buf.shape[0] // pre, rows, cols)
        mine, theirs = buf.reshape(shape), got.reshape(shape)
        upper = bit(*step) == 1
        buf = jnp.stack(
            [jnp.where(upper, theirs, mine), jnp.where(upper, mine, theirs)], axis=1
        ).reshape(-1, rows, cols)
        have.append(step)
    return buf


def scatter(buf, order, major):
    count, rows, cols = buf.shape
    have = list(major)
    for index, step in enumerate(order):
        pre = 2 ** have.index(step)
        shape = (pre, 2, buf.shape[0] // (2 * pre), rows, cols)
        parts = buf.reshape(shape)
        own = bit(*step)
        send = lax.dynamic_index_in_dim(parts, 1 - own, 1, keepdims=False)
        keep = lax.dynamic_index_in_dim(parts, own, 1, keepdims=False)
        got = swap(send, *step)
        buf = (keep.astype(f32) + got.astype(f32)).reshape(-1, rows, cols)
        if index < len(order) - 1:
            buf = buf.astype(b16)
        have.remove(step)
    return buf[0]


def shift_outer(values, by):
    size = lax.axis_size("ctx")
    return lax.ppermute(
        values, "ctx", [(i, i + 2 * by) for i in range(size) if 0 <= i + 2 * by < size]
    )


def dot(a, b, dims):
    return lax.dot_general(a, b, (dims, ((), ())), preferred_element_type=f32)


def fill_bias(blocks, tokens, place, seg_refs, bias):
    queries = jnp.broadcast_to(seg_refs[0][0:1, :].astype(f32), (tokens, tokens))
    for j in range(blocks):
        keys = jnp.broadcast_to(seg_refs[j][0:1, :].astype(f32), (tokens, tokens)).T
        allowed = (keys == queries) & (place >= j)
        if j == 0:
            key_row = lax.broadcasted_iota(jnp.int32, (tokens, tokens), 0)
            query_col = lax.broadcasted_iota(jnp.int32, (tokens, tokens), 1)
            allowed = allowed & (key_row <= query_col)
        bias[j * tokens : (j + 1) * tokens, :] = jnp.where(allowed, 0.0, masked)


def heads_side(ref):
    return jnp.concatenate(
        [ref[h * HEAD_DIM : (h + 1) * HEAD_DIM, :] for h in range(GROUP)], axis=1
    )


def forward_kernel(blocks, tokens, place_ref, *refs):
    q_ref = refs[0]
    k_refs = refs[1 : 1 + blocks]
    v_refs = refs[1 + blocks : 1 + 2 * blocks]
    seg_refs = refs[1 + 2 * blocks : 1 + 3 * blocks]
    att_ref, lse_ref, bias = refs[1 + 3 * blocks :]

    @pl.when(pl.program_id(1) == 0)
    def _():
        fill_bias(blocks, tokens, place_ref[0], seg_refs, bias)

    keys = jnp.concatenate([r[...] for r in k_refs], axis=1)
    values = jnp.concatenate([r[...] for r in v_refs], axis=1)
    scores = dot(keys, heads_side(q_ref), ((0,), (0,)))
    for h in range(GROUP):
        own = scores[:, h * tokens : (h + 1) * tokens] + bias[...]
        top = jnp.max(own, axis=0, keepdims=True)
        probs = jnp.exp(own - top)
        total = jnp.sum(probs, axis=0, keepdims=True)
        out = dot(values, probs.astype(b16), ((1,), (0,)))
        att_ref[h * HEAD_DIM : (h + 1) * HEAD_DIM, :] = (out / total).astype(b16)
        lse_ref[0, h : h + 1, :] = top + jnp.log(total)


def backward_kernel(blocks, tokens, place_ref, *refs):
    q_ref, datt_ref, lse_ref = refs[:3]
    k_refs = refs[3 : 3 + blocks]
    v_refs = refs[3 + blocks : 3 + 2 * blocks]
    seg_refs = refs[3 + 2 * blocks : 3 + 3 * blocks]
    dq_ref = refs[3 + 3 * blocks]
    dkv_refs = refs[4 + 3 * blocks : 4 + 4 * blocks]
    bias, p_scr, ds_scr = refs[4 + 4 * blocks :]

    @pl.when(pl.program_id(1) == 0)
    def _():
        fill_bias(blocks, tokens, place_ref[0], seg_refs, bias)

    keys = jnp.concatenate([r[...] for r in k_refs], axis=1)
    values = jnp.concatenate([r[...] for r in v_refs], axis=1)
    queries = heads_side(q_ref)
    grads = heads_side(datt_ref)
    scores = dot(keys, queries, ((0,), (0,)))
    d_probs = dot(values, grads, ((0,), (0,)))
    for h in range(GROUP):
        lanes = slice(h * tokens, (h + 1) * tokens)
        probs = jnp.exp(scores[:, lanes] + bias[...] - lse_ref[0, h : h + 1, :])
        weighted = probs * d_probs[:, lanes]
        delta = jnp.sum(weighted, axis=0, keepdims=True)
        p_scr[:, lanes] = probs.astype(b16)
        ds_scr[:, lanes] = (weighted - probs * delta).astype(b16)
    d_scores = ds_scr[...]
    dq = dot(keys, d_scores, ((1,), (0,)))
    for h in range(GROUP):
        dq_ref[h * HEAD_DIM : (h + 1) * HEAD_DIM, :] = dq[:, h * tokens : (h + 1) * tokens]
    dk = dot(queries, d_scores, ((1,), (1,)))
    dv = dot(grads, p_scr[...], ((1,), (1,)))
    for j in range(blocks):
        lanes = slice(j * tokens, (j + 1) * tokens)
        dkv_refs[j][0] = dk[:, lanes].astype(b16)
        dkv_refs[j][1] = dv[:, lanes].astype(b16)


def kv_specs(blocks, tokens):
    per_group = (HEAD_DIM, tokens)
    key = pl.BlockSpec(per_group, lambda s, g, _: (g, s))
    value = pl.BlockSpec(per_group, lambda s, g, _: (KEY_VALUE_HEADS + g, s))
    seg_row = 2 * KEY_VALUE_HEADS * HEAD_DIM // 16
    seg = pl.BlockSpec((16, tokens), lambda s, g, _: (seg_row, s))
    return [key] * blocks + [value] * blocks + [seg] * blocks


def attend(place, q_rot, pieces, sequences, tokens):
    blocks = len(pieces)
    heads = pl.BlockSpec((GROUP * HEAD_DIM, tokens), lambda s, g, _: (g, s))
    stat = pl.BlockSpec((1, 8, tokens), lambda s, g, _: (g, 0, s))
    wide = sequences * tokens
    return pl.pallas_call(
        functools.partial(forward_kernel, blocks, tokens),
        grid_spec=pltpu.PrefetchScalarGridSpec(
            num_scalar_prefetch=1,
            grid=(sequences, KEY_VALUE_HEADS),
            in_specs=[heads] + kv_specs(blocks, tokens),
            out_specs=[heads, stat],
            scratch_shapes=[pltpu.VMEM((blocks * tokens, tokens), f32)],
        ),
        out_shape=[
            jax.ShapeDtypeStruct((QUERY_HEADS * HEAD_DIM, wide), b16),
            jax.ShapeDtypeStruct((KEY_VALUE_HEADS, 8, wide), f32),
        ],
        compiler_params=pltpu.CompilerParams(vmem_limit_bytes=40 << 20),
        name="attend",
    )(place, q_rot, *pieces, *pieces, *pieces)


def attend_back(place, q_rot, datt, lse, pieces, sequences, tokens):
    blocks = len(pieces)
    heads = pl.BlockSpec((GROUP * HEAD_DIM, tokens), lambda s, g, _: (g, s))
    stat = pl.BlockSpec((1, 8, tokens), lambda s, g, _: (g, 0, s))
    pair = pl.BlockSpec((2, HEAD_DIM, tokens), lambda s, g, _: (0, g, s))
    wide = sequences * tokens
    return pl.pallas_call(
        functools.partial(backward_kernel, blocks, tokens),
        grid_spec=pltpu.PrefetchScalarGridSpec(
            num_scalar_prefetch=1,
            grid=(sequences, KEY_VALUE_HEADS),
            in_specs=[heads, heads, stat] + kv_specs(blocks, tokens),
            out_specs=[heads] + [pair] * blocks,
            scratch_shapes=[
                pltpu.VMEM((blocks * tokens, tokens), f32),
                pltpu.VMEM((blocks * tokens, GROUP * tokens), b16),
                pltpu.VMEM((blocks * tokens, GROUP * tokens), b16),
            ],
        ),
        out_shape=[jax.ShapeDtypeStruct((QUERY_HEADS * HEAD_DIM, wide), f32)]
        + [jax.ShapeDtypeStruct((2, KEY_VALUE_HEADS * HEAD_DIM, wide), b16)] * blocks,
        compiler_params=pltpu.CompilerParams(vmem_limit_bytes=48 << 20),
        name="attend_back",
    )(place, q_rot, datt, lse, *pieces, *pieces, *pieces)


def per_device(
    inputs,
    gain_one,
    query_weight,
    key_weight,
    value_weight,
    output_weight,
    gain_two,
    gate_weight,
    up_weight,
    down_weight,
    segment_ids,
    cotangent,
):
    dp, ctx = lax.axis_size("dp"), lax.axis_size("ctx")
    sequences, tokens, width = inputs.shape
    total = sequences * tokens
    rows = query_weight.shape[0]
    q_cols, kv_cols = query_weight.shape[1], key_weight.shape[1]
    ff_cols = gate_weight.shape[1]
    ff = ff_cols * ctx
    down_rows, out_cols = down_weight.shape
    kv_width = KEY_VALUE_HEADS * HEAD_DIM

    dp_bits, ctx_bits = bits_of("dp", dp), bits_of("ctx", ctx)
    dp_major = dp_bits + ctx_bits
    ctx_major = ctx_bits + dp_bits
    x_last = ctx_bits + dp_bits
    y_last = ctx_bits[:-1] + dp_bits[:-1] + ctx_bits[-1:] + dp_bits[-1:]

    place = lax.axis_index("ctx")

    gains = jnp.stack([gain_one, gain_two])
    gain_rows = -(-gains.size // rows)
    gains = jnp.pad(gains.reshape(-1), (0, gain_rows * rows - gains.size)).reshape(gain_rows, rows)
    pad_rows = -(q_cols + 2 * kv_cols + gain_rows) % 16
    qkv_block = jnp.concatenate(
        [query_weight.T, key_weight.T, value_weight.T, gains, jnp.zeros((pad_rows, rows), b16)]
    )
    qkv_all = gather(qkv_block, y_last, dp_major).reshape(dp, ctx, -1, rows)
    out_all = gather(output_weight.T, x_last, dp_major).reshape(dp, ctx, -1, rows)
    gu_all = gather(jnp.concatenate([gate_weight, up_weight], axis=1), x_last, ctx_major).reshape(
        ctx, dp, rows, 2 * ff_cols
    )
    down_all = gather(down_weight.T, y_last, dp_major).reshape(dp, ctx, out_cols, down_rows)

    def columns(piece):
        return jnp.transpose(piece, (1, 2, 0, 3)).reshape(-1, dp * rows)

    wq = columns(qkv_all[:, :, :q_cols])
    wk = columns(qkv_all[:, :, q_cols : q_cols + kv_cols])
    wv = columns(qkv_all[:, :, q_cols + kv_cols : q_cols + 2 * kv_cols])
    w_qkv = jnp.concatenate([wq, wk, wv])
    first_gain = q_cols + 2 * kv_cols
    gain_all = qkv_all[0, :, first_gain : first_gain + gain_rows].reshape(ctx, -1)
    gain_part = gain_one.shape[0]
    gain_a = gain_all[:, :gain_part].reshape(width).astype(f32)
    gain_b = gain_all[:, gain_part : 2 * gain_part].reshape(width).astype(f32)
    wo = columns(out_all)

    x = inputs.reshape(total, width).astype(f32)
    inv_one = lax.rsqrt(jnp.mean(x * x, axis=-1, keepdims=True) + epsilon)
    normed_one = (x * inv_one * gain_a).astype(b16)
    qkv = dot(w_qkv, normed_one, ((1,), (1,)))
    positions = (place * tokens + jnp.arange(tokens, dtype=jnp.int32)).astype(f32)
    positions = jnp.tile(positions, sequences)
    frequency = jnp.exp(jnp.arange(HALF, dtype=f32) * (-2.0 * math.log(rope_base) / HEAD_DIM))
    angles = frequency[:, None] * positions[None, :]
    cosine, sine = jnp.cos(angles), jnp.sin(angles)

    def turn(values, sign):
        parts = values.reshape(-1, 2, HALF, total)
        low, high = parts[:, 0], parts[:, 1]
        return jnp.stack(
            [low * cosine - sign * high * sine, high * cosine + sign * low * sine], axis=1
        ).reshape(-1, total)

    score_scale = HEAD_DIM ** (-0.5)
    q_rot = (turn(qkv[:width], 1.0) * score_scale).astype(b16)
    k_rot = turn(qkv[width : width + kv_width], 1.0).astype(b16)
    v_low = qkv[width + kv_width :].astype(b16)
    seg_row = jnp.pad(segment_ids.reshape(1, total).astype(b16), ((0, 15), (0, 0)))
    own = jnp.concatenate([k_rot, v_low, seg_row])

    steps = ctx // 4
    inner = bit("ctx", 1)
    straight = [own]
    for _ in range(steps):
        straight.append(shift_outer(straight[-1], 1))
    crossed = [
        swap(jnp.where(inner == 0, straight[k], straight[k + 1]), "ctx", 1) for k in range(steps)
    ]
    pieces = []
    for k in range(steps):
        pieces += [straight[k], crossed[k]]
    pieces.append(straight[steps])

    place_arg = place.reshape(1).astype(jnp.int32)
    att, lse = attend(place_arg, q_rot, pieces, sequences, tokens)

    mid = x + dot(att, wo, ((0,), (1,)))
    inv_two = lax.rsqrt(jnp.mean(mid * mid, axis=-1, keepdims=True) + epsilon)
    normed_two = (mid * inv_two * gain_b).astype(b16)
    w_gate = jnp.transpose(gu_all[..., :ff_cols], (1, 2, 0, 3)).reshape(width, ff)
    w_up = jnp.transpose(gu_all[..., ff_cols:], (1, 2, 0, 3)).reshape(width, ff)
    w_down = jnp.transpose(down_all, (1, 2, 0, 3)).reshape(width, ff)
    gate = dot(normed_two, w_gate, ((1,), (0,)))
    up = dot(normed_two, w_up, ((1,), (0,)))
    sigma = jax.nn.sigmoid(gate)
    hidden = (gate * sigma * up).astype(b16)
    output = (mid + dot(hidden, w_down, ((1,), (1,)))).astype(b16)

    cot = cotangent.reshape(total, width)
    d_hidden = dot(cot, w_down, ((1,), (0,)))
    d_up = (d_hidden * gate * sigma).astype(b16)
    d_gate = (d_hidden * up * sigma * (1.0 + gate * (1.0 - sigma))).astype(b16)
    g_down = dot(cot, hidden, ((0,), (0,))).astype(b16)
    g_down = jnp.transpose(g_down.reshape(ctx, out_cols, dp, down_rows), (2, 0, 1, 3))
    g_down = scatter(
        g_down.reshape(dp * ctx, out_cols, down_rows), y_last[::-1], dp_major
    )
    g_gate = dot(normed_two, d_gate, ((0,), (0,))).astype(b16)
    g_up = dot(normed_two, d_up, ((0,), (0,))).astype(b16)
    g_gu = jnp.concatenate(
        [
            jnp.transpose(g.reshape(dp, rows, ctx, ff_cols), (2, 0, 1, 3))
            for g in (g_gate, g_up)
        ],
        axis=-1,
    )
    g_gu = scatter(g_gu.reshape(ctx * dp, rows, 2 * ff_cols), x_last[::-1], ctx_major)
    d_normed_two = dot(d_gate, w_gate, ((1,), (1,))) + dot(d_up, w_up, ((1,), (1,)))
    g_gain_two = jnp.sum(d_normed_two * mid * inv_two, axis=0)
    scaled_two = gain_b * d_normed_two
    d_mid = (
        cot.astype(f32)
        + inv_two * scaled_two
        - mid * inv_two**3 * jnp.mean(scaled_two * mid, axis=-1, keepdims=True)
    )
    d_mid_low = d_mid.astype(b16)

    def to_blocks(grad, n):
        return jnp.transpose(grad.reshape(ctx, n, dp, rows), (2, 0, 1, 3))

    g_out = dot(d_mid_low, att, ((0,), (1,))).astype(b16)
    g_out = scatter(
        to_blocks(g_out, out_cols).reshape(dp * ctx, out_cols, rows), x_last[::-1], dp_major
    )
    d_att = dot(wo, d_mid_low, ((0,), (1,))).astype(b16)
    dq_rot, *parts = attend_back(place_arg, q_rot, d_att, lse, pieces, sequences, tokens)

    returned = [swap(parts[2 * k + 1], "ctx", 1).astype(f32) for k in range(steps)]
    here = []
    for k in range(steps + 1):
        value = parts[2 * k].astype(f32)
        if k < steps:
            value = value + jnp.where(inner == 0, returned[k], 0.0)
        if k > 0:
            value = value + jnp.where(inner == 1, returned[k - 1], 0.0)
        here.append(value)
    carried = here[steps]
    for k in range(steps, 0, -1):
        carried = here[k - 1] + shift_outer(carried.astype(b16), -1).astype(f32)

    d_q = (turn(dq_rot, -1.0) * score_scale).astype(b16)
    d_k = turn(carried[0], -1.0).astype(b16)
    d_v = carried[1].astype(b16)
    d_qkv = jnp.concatenate([d_q, d_k, d_v])
    g_qkv = dot(d_qkv, normed_one, ((1,), (0,))).astype(b16)
    d_normed_one = dot(d_qkv, w_qkv, ((0,), (0,)))
    g_gain_one = jnp.sum(d_normed_one * x * inv_one, axis=0)
    scaled_one = gain_a * d_normed_one
    input_grad = (
        d_mid
        + inv_one * scaled_one
        - x * inv_one**3 * jnp.mean(scaled_one * x, axis=-1, keepdims=True)
    ).astype(b16)

    g_gains = jnp.concatenate(
        [g_gain_one.reshape(ctx, gain_part), g_gain_two.reshape(ctx, gain_part)], axis=1
    ).astype(b16)
    g_gains = jnp.pad(g_gains, ((0, 0), (0, gain_rows * rows - 2 * gain_part)))
    g_gains = jnp.broadcast_to(g_gains.reshape(1, ctx, gain_rows, rows), (dp, ctx, gain_rows, rows))
    g_block = jnp.concatenate(
        [
            to_blocks(g_qkv[:width], q_cols),
            to_blocks(g_qkv[width : width + kv_width], kv_cols),
            to_blocks(g_qkv[width + kv_width :], kv_cols),
            g_gains,
            jnp.zeros((dp, ctx, pad_rows, rows), b16),
        ],
        axis=2,
    )
    g_block = scatter(g_block.reshape(dp * ctx, -1, rows), y_last[::-1], dp_major)
    g_gains = g_block[first_gain : first_gain + gain_rows].reshape(-1)
    return (
        output.reshape(sequences, tokens, width),
        input_grad.reshape(sequences, tokens, width),
        g_gains[:gain_part],
        g_block[:q_cols].T,
        g_block[q_cols : q_cols + kv_cols].T,
        g_block[q_cols + kv_cols : first_gain].T,
        g_out.T,
        g_gains[gain_part : 2 * gain_part],
        g_gu[:, :ff_cols],
        g_gu[:, ff_cols:],
        g_down.T,
    )


def solution(mesh):
    act = P("dp", "ctx", None)
    weight = P("dp", "ctx")
    gain = P("ctx")
    return jax.shard_map(
        per_device,
        mesh=mesh,
        in_specs=(
            act, gain, weight, weight, weight, weight, gain, weight, weight, weight, P("dp", "ctx"), act,
        ),
        out_specs=(
            act, act, gain, weight, weight, weight, weight, gain, weight, weight, weight,
        ),
        check_vma=False,
    )
```

time: 1380 us -> 786 us (0.57)
  waiting for transfers between devices: 849 us -> 261 us
  blocking collectives: 217 us -> 0 us
  local copies, waits for them, and re-layouts: 106 us -> 268 us
  matrix products: 146 us -> 58.3 us
  other arithmetic: 33.6 us -> 91.9 us
  starting transfers between devices: 1.28 us -> 53.3 us
  Pallas kernels: 0 us -> 38.9 us
  between operations: 16.7 us -> 2.73 us
    unnamed x36 -> x0, waiting for transfers between devices: 486 us -> none
    ppermute x0 -> x48, waiting for transfers between devices: none -> 261 us  [the longest x44 225 us: swap(): return lax.ppermute(values, axis, [(i, i ^ mask) for i in range(size)])]
    reduce_scatter x6 -> x0, waiting for transfers between devices: 242 us -> none  [the longest x1 56.1 us: spread(): lax.psum_scatter(g_value.astype(jnp.bfloat16), 'ctx', scatter_dimension=1...]
    all_gather x7 -> x0, blocking collectives: 168 us -> none  [the longest x1 33.4 us: collect(): lax.all_gather(query_weight, 'ctx', axis=1, tiled=True)]
    all_gather x10 -> x0, waiting for transfers between devices: 121 us -> none  [the longest x1 34.9 us: collect(): lax.all_gather(down_weight, 'dp', axis=0, tiled=True)]
    reshape x0 -> x22, local copies, waits for them, and re-layouts: none -> 106 us  [the longest x4 37.4 us: per_device(): g.reshape(dp, rows, ctx, ff_cols)]
    dot_general x35 -> x15, matrix products: 146 us -> 58.3 us  [dot(): return lax.dot_general(a, b, (dims, ((), ())), preferred_element_type=f32)]
    ppermute x0 -> x48, starting transfers between devices: none -> 53.3 us  [the longest x44 41.8 us: swap(): return lax.ppermute(values, axis, [(i, i ^ mask) for i in range(size)])]
  transfers between devices with their start and end apart: 26 -> 48, of which waited for: 21 -> 21; matrix products, arithmetic and copies ran while one was open for 13% -> 36% of each run, Pallas kernels for 0% -> 2%
where the time goes in v1:
time: 786 us; the launch traced here: 775 us
  local copies, waits for them, and re-layouts  268 us (34%)
  waiting for transfers between devices  261 us (33%)
  other arithmetic  91.9 us (12%)
  matrix products  58.3 us (7%)
  starting transfers between devices  53.3 us (7%)
  Pallas kernels  38.9 us (5%)
    ppermute x44, waiting for transfers between devices, swap(): return lax.ppermute(values, axis, [(i, i ^ mask) for i in range(size)])  225 us
    dot_general x15, matrix products, dot(): return lax.dot_general(a, b, (dims, ((), ())), preferred_element_type=f32)  58.3 us
    ppermute x44, starting transfers between devices, swap(): return lax.ppermute(values, axis, [(i, i ^ mask) for i in range(size)])  41.8 us
    reshape x4, local copies, waits for them, and re-layouts, per_device(): g.reshape(dp, rows, ctx, ff_cols)  37.4 us
    ppermute x4, waiting for transfers between devices, shift_outer(): lax.ppermute(values, 'ctx', [(i, i + 2 * by) for i in range(size) if 0 <=...  35.8 us
    another operation x31, other arithmetic, gather(): jnp.stack([jnp.where(upper, theirs, mine), jnp.where(upper, mine, theirs)...  30.1 us
    unnamed x170, local copies, waits for them, and re-layouts  28.1 us
    pallas_call x1, Pallas kernels, attend_back(): pl.pallas_call(functools.partial(backward_kernel, blocks, tokens), grid_s...  23.7 us
  transfers between devices with their start and end apart: 48, of which 21 were waited for; matrix products, arithmetic and copies ran while one was open for 36% of the time, Pallas kernels for 2%

profile of v1, /device:TPU:0, one launch (start us, length us, event | category | flops | bytes accessed | tf_op | source)
XLA Modules:
  0.0 774.5 jit_solution(4994661443289288573)
XLA Ops:
  23.6 8.4 %collective-permute-done.1 = bf16[2,208,240]{2,1,0:T(8,128)(2,1)S(1)} collective-permute-done((bf16[2,208,240]{2,1,0:T(8,128)(2,1)S(1)}, bf16[2,208,240]{2,1,0:T(8,128)(2,1)S(1)}, u32[]{:S(2)}, u32[]{:S(2)}) %collective-permute-start.1) | collective-permute-done | bytes 199712 | tf_op jit(solution)/shard_map/ppermute | solution.py:35
  44.2 8.5 %collective-permute-done.15 = bf16[2,240,640]{2,1,0:T(8,128)(2,1)S(1)} collective-permute-done((bf16[2,240,640]{2,1,0:T(8,128)(2,1)S(1)}, bf16[2,240,640]{2,1,0:T(8,128)(2,1)S(1)}, u32[]{:S(2)}, u32[]{:S(2)}) %collective-permute-start.15) | collective-permute-done | bytes 614432 | tf_op jit(solution)/shard_map/ppermute | solution.py:35
  58.3 34.3 %collective-permute-done.11 = bf16[4,120,240]{2,1,0:T(8,128)(2,1)S(1)} collective-permute-done((bf16[4,120,240]{2,1,0:T(8,128)(2,1)S(1)}, bf16[4,120,240]{2,1,0:T(8,128)(2,1)S(1)}, u32[]{:S(2)}, u32[]{:S(2)}) %collective-permute-start.11) | collective-permute-done | bytes 230432 | tf_op jit(solution)/shard_map/ppermute | solution.py:35
  98.1 62.7 %collective-permute-done.12 = bf16[8,120,240]{2,1,0:T(8,128)(2,1)S(1)} collective-permute-done((bf16[8,120,240]{2,1,0:T(8,128)(2,1)S(1)}, bf16[8,120,240]{2,1,0:T(8,128)(2,1)S(1)}, u32[]{:S(2)}, u32[]{:S(2)}) %collective-permute-start.12) | collective-permute-done | bytes 460832 | tf_op jit(solution)/shard_map/ppermute | solution.py:35
  162.2 11.4 %collective-permute-done.21 = bf16[4,120,640]{2,1,0:T(8,128)(2,1)S(1)} collective-permute-done((bf16[4,120,640]{2,1,0:T(8,128)(2,1)S(1)}, bf16[4,120,640]{2,1,0:T(8,128)(2,1)S(1)}, u32[]{:S(2)}, u32[]{:S(2)}) %collective-permute-start.21) | collective-permute-done | bytes 614432 | tf_op jit(solution)/shard_map/ppermute | solution.py:35
  223.1 7.5 collective-permute-done.5.refs_3_.refs_8_.refs_13_.refs_5_.refs_10_.refs_15_
  270.1 15.2 %attend.1 = (bf16[960,384]{1,0:T(8,128)(2,1)S(1)}, f32[5,8,384]{2,1,0:T(8,128)S(1)}) custom-call(s32[1]{0:T(128)} %bitcast.1.place_ref, bf16[960,384]{1,0:T(8,128)(2,1)S(1)} %bitcast.405, bf16[656,384]{1,0:T(8,128)(2,1)S(1)} %fusion.24.refs_1_.refs_6_.refs_11_.refs_3_.refs_8_.refs_13_, ...), custom_call_target="tpu_custom_call" | custom-call | tf_op jit(solution)/shard_map/attend/pallas_call | solution.py:183
  298.6 8.4 %select_bitcast_fusion.1 = (bf16[16,1,1,240,640]{4,3,0,2,1:T(8,128)(2,1)}, bf16[16,1,1,240,640]{4,3,0,2,1:T(8,128)(2,1)}) fusion(bf16[16,240,640]{2,1,0:T(8,128)(2,1)} %collective-permute-done.18, pred[]{:T(512)S(6)} %eq.80, bf16[8,2,1,240,640]{4,3,1,0,2:T(8,128)(2,1)} %copy.165), kind=kLoop, calls=%fused_computation.17 | loop fusion | flops 4915200 | bytes 19660800 | tf_op jit(solution)/shard_map/stack | solution.py:53
  307.0 8.7 %pad_maximum_fusion.1 = bf16[16,2,1,240,640]{4,3,0,2,1:T(8,128)(2,1)} fusion(bf16[16,1,1,240,640]{4,3,0,2,1:T(8,128)(2,1)} %get-tuple-element.78, bf16[16,1,1,240,640]{4,3,0,2,1:T(8,128)(2,1)} %get-tuple-element.77), kind=kLoop, calls=%fused_computation.1 | loop fusion | flops 4915200 | bytes 19660800 | tf_op jit(solution)/shard_map/stack | solution.py:53
  315.7 8.3 %copy.166 = bf16[16,2,1,240,640]{4,3,1,0,2:T(8,128)(2,1)} copy(bf16[16,2,1,240,640]{4,3,0,2,1:T(8,128)(2,1)} %pad_maximum_fusion.1) | data formatting | bytes 19660800 | tf_op jit(solution)/shard_map/stack | solution.py:53
  324.0 11.5 %slice_bitcast_fusion.1 = (bf16[4,240,8,320]{3,1,0,2:T(8,128)(2,1)}, bf16[4,240,8,320]{3,1,0,2:T(8,128)(2,1)}) fusion(bf16[8,4,240,640]{3,2,1,0:T(8,128)(2,1)} %bitcast.407), kind=kLoop, calls=%fused_computation.5 | loop fusion | bytes 19660800 | tf_op jit(solution)/shard_map/transpose | solution.py:330
  335.5 10.5 %copy.167 = bf16[4,240,8,320]{1,0,3,2:T(4,128)(2,1)} copy(bf16[4,240,8,320]{3,1,0,2:T(8,128)(2,1)} %get-tuple-element.75) | data formatting | bytes 9830400 | tf_op jit(solution)/shard_map/transpose | solution.py:330
  346.0 9.9 %reshape.1267 = bf16[960,2560]{0,1:T(8,128)(2,1)} reshape(bf16[4,240,8,320]{1,0,3,2:T(4,128)(2,1)} %copy.167) | data formatting | bytes 9830400 | tf_op jit(solution)/shard_map/reshape | solution.py:330
  355.9 10.3 %copy.168 = bf16[4,240,8,320]{1,0,3,2:T(4,128)(2,1)} copy(bf16[4,240,8,320]{3,1,0,2:T(8,128)(2,1)} %get-tuple-element.76) | data formatting | bytes 9830400 | tf_op jit(solution)/shard_map/transpose | solution.py:331
  366.1 9.8 %reshape.1268 = bf16[960,2560]{0,1:T(8,128)(2,1)} reshape(bf16[4,240,8,320]{1,0,3,2:T(4,128)(2,1)} %copy.168) | data formatting | bytes 9830400 | tf_op jit(solution)/shard_map/reshape | solution.py:331
  387.2 7.1 multiply_convert_fusion
  418.9 23.7 %attend_back.1 = (f32[960,384]{1,0:T(8,128)}, bf16[2,320,384]{2,1,0:T(8,128)(2,1)S(1)}, bf16[2,320,384]{2,1,0:T(8,128)(2,1)S(1)}, bf16[2,320,384]{2,1,0:T(8,128)...) custom-call(s32[1]{0:T(128)} %bitcast.1.place_ref, bf16[960,384]{1,0:T(8,128)(2,1)S(1)} %bitcast.406, ...), custom_call_target="tpu_custom_call" | custom-call | tf_op jit(solution)/shard_map/attend_back/pallas_call | solution.py:207
  455.1 10.0 %reshape.1306 = bf16[4,240,8,320]{3,2,1,0:T(8,128)(2,1)} reshape(bf16[960,2560]{1,0:T(8,128)(2,1)} %convolution_convert_fusion.1) | data formatting | bytes 9830400 | tf_op jit(solution)/shard_map/reshape | solution.py:352
  465.1 8.7 %copy.201 = bf16[4,240,8,320]{1,0,3,2:T(4,128)(2,1)} copy(bf16[4,240,8,320]{3,2,1,0:T(8,128)(2,1)} %reshape.1306) | data formatting | bytes 9830400 | tf_op jit(solution)/shard_map/reshape | solution.py:352
  473.8 10.0 %reshape.1305 = bf16[4,240,8,320]{3,2,1,0:T(8,128)(2,1)} reshape(bf16[960,2560]{1,0:T(8,128)(2,1)} %convolution_convert_fusion.2) | data formatting | bytes 9830400 | tf_op jit(solution)/shard_map/reshape | solution.py:352
  483.7 8.7 %copy.200 = bf16[4,240,8,320]{1,0,3,2:T(4,128)(2,1)} copy(bf16[4,240,8,320]{3,2,1,0:T(8,128)(2,1)} %reshape.1305) | data formatting | bytes 9830400 | tf_op jit(solution)/shard_map/reshape | solution.py:352
  492.4 19.9 %pad_maximum_fusion = bf16[8,4,240,640]{2,1,3,0:T(4,128)(2,1)} fusion(bf16[8,4,240,320]{2,1,3,0:T(4,128)(2,1)} %bitcast.410, bf16[8,4,240,320]{2,1,3,0:T(4,128)(2,1)} %bitcast.411), kind=kLoop, calls=%fused_computation | loop fusion | flops 4915200 | bytes 19660800 | tf_op jit(solution)/shard_map/concatenate | solution.py:350
  512.4 16.8 %copy.190 = bf16[8,4,240,640]{3,2,1,0:T(8,128)(2,1)} copy(bf16[8,4,240,640]{2,1,3,0:T(4,128)(2,1)} %pad_maximum_fusion) | data formatting | bytes 19660800 | tf_op jit(solution)/shard_map/concatenate | solution.py:350
  543.8 9.3 %reshape.1286 = bf16[8,120,4,640]{3,2,1,0:T(4,128)(2,1)} reshape(bf16[960,2560]{1,0:T(8,128)(2,1)} %fusion.3) | data formatting | bytes 9830400 | tf_op jit(solution)/shard_map/reshape | solution.py:344
  566.7 11.2 %collective-permute-done.26 = bf16[2,320,384]{2,1,0:T(8,128)(2,1)} collective-permute-done((bf16[2,320,384]{2,1,0:T(8,128)(2,1)}, bf16[2,320,384]{2,1,0:T(8,128)(2,1)}, u32[]{:S(2)}, u32[]{:S(2)}) %collective-permute-start.26) | collective-permute-done | bytes 491552 | tf_op jit(solution)/shard_map/ppermute | solution.py:80
  583.8 10.7 %collective-permute-done.27 = bf16[2,320,384]{2,1,0:T(8,128)(2,1)S(1)} collective-permute-done((bf16[2,320,384]{2,1,0:T(8,128)(2,1)S(1)}, bf16[2,320,384]{2,1,0:T(8,128)(2,1)S(1)}, u32[]{:S(2)}, u32[]{:S(2)}) %collective-permute-start.27) | collective-permute-done | bytes 491552 | tf_op jit(solution)/shard_map/ppermute | solution.py:80
  623.4 14.1 %concatenate.97 = bf16[4,8,208,240]{3,2,1,0:T(8,128)(2,1)S(1)} concatenate(bf16[4,8,120,240]{3,2,1,0:T(8,128)(2,1)} %bitcast.435, bf16[4,8,40,240]{3,2,1,0:T(8,128)(2,1)} %copy.185, bf16[4,8,40,240]{3,2,1,0:T(8,128)(2,1)} %copy.186, bf16[4,8,1,240]{3,2,1,0:T(2,128)(2,1)} %broadcast_in_dim.30, bf16[4,8,7,240]{3,2,1,0:T(8,128)(2,1)S(1)} %broadcast_in_dim.31), dimensions={2} | concatenate | bytes 6389760 | tf_op jit(solution)/shard_map/concatenate | solution.py:410
  666.9 18.1 %collective-permute-done.44 = bf16[8,1,120,640]{3,2,0,1:T(8,128)(2,1)} collective-permute-done((bf16[8,1,120,640]{3,2,0,1:T(8,128)(2,1)}, bf16[8,1,120,640]{3,2,0,1:T(8,128)(2,1)}, u32[]{:S(2)}, u32[]{:S(2)}) %collective-permute-start.44) | collective-permute-done | bytes 1228832 | tf_op jit(solution)/shard_map/ppermute | solution.py:35
  687.3 13.7 %collective-permute-done.29 = bf16[8,1,208,240]{3,2,0,1:T(8,128)(2,1)} collective-permute-done((bf16[8,1,208,240]{3,2,0,1:T(8,128)(2,1)}, bf16[8,1,208,240]{3,2,0,1:T(8,128)(2,1)}, u32[]{:S(2)}, u32[]{:S(2)}) %collective-permute-start.29) | collective-permute-done | bytes 798752 | tf_op jit(solution)/shard_map/ppermute | solution.py:35
  709.3 17.2 %collective-permute-done.30 = bf16[1,4,208,240]{3,2,1,0:T(8,128)(2,1)S(1)} collective-permute-done((bf16[1,4,208,240]{3,2,1,0:T(8,128)(2,1)S(1)}, bf16[1,4,208,240]{3,2,1,0:T(8,128)(2,1)S(1)}, u32[]{:S(2)}, u32[]{:S(2)}) %collective-permute-start.30) | collective-permute-done | bytes 399392 | tf_op jit(solution)/shard_map/ppermute | solution.py:35
  746.8 11.5 %collective-permute-done.41 = bf16[2,1,240,640]{3,2,0,1:T(8,128)(2,1)S(1)} collective-permute-done((bf16[2,1,240,640]{3,2,0,1:T(8,128)(2,1)S(1)}, bf16[2,1,240,640]{3,2,0,1:T(8,128)(2,1)S(1)}, u32[]{:S(2)}, u32[]{:S(2)}) %collective-permute-start.41) | collective-permute-done | bytes 614432 | tf_op jit(solution)/shard_map/ppermute | solution.py:35
  760.8 11.3 %collective-permute-done.42 = bf16[1,1,240,640]{3,2,0,1:T(8,128)(2,1)S(1)} collective-permute-done((bf16[1,1,240,640]{3,2,0,1:T(8,128)(2,1)S(1)}, bf16[1,1,240,640]{3,2,0,1:T(8,128)(2,1)S(1)}, u32[]{:S(2)}, u32[]{:S(2)}) %collective-permute-start.42) | collective-permute-done | bytes 307232 | tf_op jit(solution)/shard_map/ppermute | solution.py:35
  (439 shorter events, 324.5 us)
Async XLA Ops:
  11.9 25.6 %collective-permute-start.9 = (bf16[1,120,240]{2,1,0:T(8,128)(2,1)}, bf16[1,120,240]{2,1,0:T(8,128)(2,1)}, u32[]{:S(2)}, u32[]{:S(2)}) collective-permute-start(bf16[1,120,240]{2,1,0:T(8,128)(2,1)} %bitcast.38), channel_id=1, source_target_pairs={{0,4},{1,5},{2,6},{3,7},{4,0},{5,1},{6,2},{7,3},{8,12},{9,13},{10,... | collective-permute-start | bytes 172808 | tf_op jit(solution)/shard_map/ppermute | solution.py:35
  15.0 21.0 %collective-permute-start.14 = (bf16[1,240,640]{2,1,0:T(8,128)(2,1)}, bf16[1,240,640]{2,1,0:T(8,128)(2,1)}, u32[]{:S(2)}, u32[]{:S(2)}) collective-permute-start(bf16[1,240,640]{2,1,0:T(8,128)(2,1)} %maximum_bitcast_fusion.1), channel_id=1, source_target_pairs={{0,4},{1,5},{2,6},{3,7},{4,0},{5,1},{6,2},{7,3},{8,12},{9,13},{10,... | collective-permute-start | bytes 921608 | tf_op jit(solution)/shard_map/ppermute | solution.py:35
  17.9 37.8 %collective-permute-start.19 = (bf16[1,120,640]{2,1,0:T(8,128)(2,1)}, bf16[1,120,640]{2,1,0:T(8,128)(2,1)}, u32[]{:S(2)}, u32[]{:S(2)}) collective-permute-start(bf16[1,120,640]{2,1,0:T(8,128)(2,1)} %bitcast.489), channel_id=1, source_target_pairs={{0,4},{1,5},{2,6},{3,7},{4,0},{5,1},{6,2},{7,3},{8,12},{9,13},{10,... | collective-permute-start | bytes 460808 | tf_op jit(solution)/shard_map/ppermute | solution.py:35
  42.6 50.0 %collective-permute-start.3 = (bf16[8,208,240]{2,1,0:T(8,128)(2,1)S(1)}, bf16[8,208,240]{2,1,0:T(8,128)(2,1)S(1)}, u32[]{:S(2)}, u32[]{:S(2)}) collective-permute-start(bf16[8,208,240]{2,1,0:T(8,128)(2,1)S(1)} %bitcast.453), channel_id=1, source_target_pairs={{0,1},{1,0},{2,3},{3,2},{4,5},{5,4},{6,7},{7,6},{8,9},{9,8},{10,11... | collective-permute-start | bytes 2396168 | tf_op jit(solution)/shard_map/ppermute | solution.py:35
  53.0 40.2 %collective-permute-start.16 = (bf16[4,240,640]{2,1,0:T(8,128)(2,1)S(1)}, bf16[4,240,640]{2,1,0:T(8,128)(2,1)S(1)}, u32[]{:S(2)}, u32[]{:S(2)}) collective-permute-start(bf16[4,240,640]{2,1,0:T(8,128)(2,1)S(1)} %bitcast.444), channel_id=1, source_target_pairs={{0,1},{1,0},{2,3},{3,2},{4,5},{5,4},{6,7},{7,6},{8,9},{9,8},{10,11... | collective-permute-start | bytes 3686408 | tf_op jit(solution)/shard_map/ppermute | solution.py:35
  54.7 37.9 %collective-permute-start.11 = (bf16[4,120,240]{2,1,0:T(8,128)(2,1)S(1)}, bf16[4,120,240]{2,1,0:T(8,128)(2,1)S(1)}, u32[]{:S(2)}, u32[]{:S(2)}) collective-permute-start(bf16[4,120,240]{2,1,0:T(8,128)(2,1)S(1)} %bitcast.482), channel_id=1, source_target_pairs={{0,1},{1,0},{2,3},{3,2},{4,5},{5,4},{6,7},{7,6},{8,9},{9,8},{10,11... | collective-permute-start | bytes 691208 | tf_op jit(solution)/shard_map/ppermute | solution.py:35
  56.8 39.6 %collective-permute-start.20 = (bf16[2,120,640]{2,1,0:T(8,128)(2,1)S(1)}, bf16[2,120,640]{2,1,0:T(8,128)(2,1)S(1)}, u32[]{:S(2)}, u32[]{:S(2)}) collective-permute-start(bf16[2,120,640]{2,1,0:T(8,128)(2,1)S(1)} %maximum_bitcast_fusion.2), channel_id=1, source_target_pairs={{0,2},{1,3},{2,0},{3,1},{4,6},{5,7},{6,4},{7,5},{8,10},{9,11},{10,... | collective-permute-start | bytes 921608 | tf_op jit(solution)/shard_map/ppermute | solution.py:35
  93.1 83.3 %collective-permute-start.4 = (bf16[16,208,240]{2,1,0:T(8,128)(2,1)S(1)}, bf16[16,208,240]{2,1,0:T(8,128)(2,1)S(1)}, u32[]{:S(2)}, u32[]{:S(2)}) collective-permute-start(bf16[16,208,240]{2,1,0:T(8,128)(2,1)S(1)} %bitcast.436), channel_id=1, source_target_pairs={{0,8},{8,0},{16,24},{24,16},{1,9},{9,1},{17,25},{25,17},{2,10},{10... | collective-permute-start | bytes 4792328 | tf_op jit(solution)/shard_map/ppermute | solution.py:35
  94.1 83.7 %collective-permute-start.17 = (bf16[8,240,640]{2,1,0:T(8,128)(2,1)S(1)}, bf16[8,240,640]{2,1,0:T(8,128)(2,1)S(1)}, u32[]{:S(2)}, u32[]{:S(2)}) collective-permute-start(bf16[8,240,640]{2,1,0:T(8,128)(2,1)S(1)} %bitcast.427), channel_id=1, source_target_pairs={{0,16},{8,24},{16,0},{24,8},{1,17},{9,25},{17,1},{25,9},{2,18},{10... | collective-permute-start | bytes 7372808 | tf_op jit(solution)/shard_map/ppermute | solution.py:35
  95.8 65.1 %collective-permute-start.12 = (bf16[8,120,240]{2,1,0:T(8,128)(2,1)S(1)}, bf16[8,120,240]{2,1,0:T(8,128)(2,1)S(1)}, u32[]{:S(2)}, u32[]{:S(2)}) collective-permute-start(bf16[8,120,240]{2,1,0:T(8,128)(2,1)S(1)} %bitcast.470), channel_id=1, source_target_pairs={{0,16},{8,24},{16,0},{24,8},{1,17},{9,25},{17,1},{25,9},{2,18},{10... | collective-permute-start | bytes 1382408 | tf_op jit(solution)/shard_map/ppermute | solution.py:35
  96.5 77.1 %collective-permute-start.21 = (bf16[4,120,640]{2,1,0:T(8,128)(2,1)S(1)}, bf16[4,120,640]{2,1,0:T(8,128)(2,1)S(1)}, u32[]{:S(2)}, u32[]{:S(2)}) collective-permute-start(bf16[4,120,640]{2,1,0:T(8,128)(2,1)S(1)} %bitcast.465), channel_id=1, source_target_pairs={{0,16},{8,24},{16,0},{24,8},{1,17},{9,25},{17,1},{25,9},{2,18},{10... | collective-permute-start | bytes 1843208 | tf_op jit(solution)/shard_map/ppermute | solution.py:35
  162.2 75.4 %collective-permute-start.13 = (bf16[16,120,240]{2,1,0:T(8,128)(2,1)}, bf16[16,120,240]{2,1,0:T(8,128)(2,1)}, u32[]{:S(2)}, u32[]{:S(2)}) collective-permute-start(bf16[16,120,240]{2,1,0:T(8,128)(2,1)} %bitcast.53), channel_id=1, source_target_pairs={{0,8},{8,0},{16,24},{24,16},{1,9},{9,1},{17,25},{25,17},{2,10},{10... | collective-permute-start | bytes 2764808 | tf_op jit(solution)/shard_map/ppermute | solution.py:35
  174.9 44.4 %collective-permute-start.22 = (bf16[8,120,640]{2,1,0:T(8,128)(2,1)}, bf16[8,120,640]{2,1,0:T(8,128)(2,1)}, u32[]{:S(2)}, u32[]{:S(2)}) collective-permute-start(bf16[8,120,640]{2,1,0:T(8,128)(2,1)} %bitcast.91), channel_id=1, source_target_pairs={{0,1},{1,0},{2,3},{3,2},{4,5},{5,4},{6,7},{7,6},{8,9},{9,8},{10,11... | collective-permute-start | bytes 3686408 | tf_op jit(solution)/shard_map/ppermute | solution.py:35
  181.6 117.0 %collective-permute-start.18 = (bf16[16,240,640]{2,1,0:T(8,128)(2,1)}, bf16[16,240,640]{2,1,0:T(8,128)(2,1)}, u32[]{:S(2)}, u32[]{:S(2)}) collective-permute-start(bf16[16,240,640]{2,1,0:T(8,128)(2,1)} %bitcast.72), channel_id=1, source_target_pairs={{0,8},{8,0},{16,24},{24,16},{1,9},{9,1},{17,25},{25,17},{2,10},{10... | collective-permute-start | bytes 14745608 | tf_op jit(solution)/shard_map/ppermute | solution.py:35
  222.9 65.0 %collective-permute-start.23 = (bf16[16,120,640]{2,1,0:T(8,128)(2,1)}, bf16[16,120,640]{2,1,0:T(8,128)(2,1)}, u32[]{:S(2)}, u32[]{:S(2)}) collective-permute-start(bf16[16,120,640]{2,1,0:T(8,128)(2,1)} %bitcast.95), channel_id=1, source_target_pairs={{0,8},{8,0},{16,24},{24,16},{1,9},{9,1},{17,25},{25,17},{2,10},{10... | collective-permute-start | bytes 7372808 | tf_op jit(solution)/shard_map/ppermute | solution.py:35
  246.8 16.9 %collective-permute-start.6 = (bf16[656,384]{1,0:T(8,128)(2,1)}, bf16[656,384]{1,0:T(8,128)(2,1)S(1)}, u32[]{:S(2)}, u32[]{:S(2)}) collective-permute-start(bf16[656,384]{1,0:T(8,128)(2,1)} %get-tuple-element.123), channel_id=1, source_target_pairs={{0,1},{1,0},{2,3},{3,2},{4,5},{5,4},{6,7},{7,6},{8,9},{9,8},{10,11... | collective-permute-start | bytes 1511432 | tf_op jit(solution)/shard_map/ppermute | solution.py:35
  247.3 22.7 %collective-permute-start.8 = (bf16[656,384]{1,0:T(8,128)(2,1)}, bf16[656,384]{1,0:T(8,128)(2,1)S(1)}, u32[]{:S(2)}, u32[]{:S(2)}) collective-permute-start(bf16[656,384]{1,0:T(8,128)(2,1)} %get-tuple-element.122), channel_id=1, source_target_pairs={{0,1},{1,0},{2,3},{3,2},{4,5},{5,4},{6,7},{7,6},{8,9},{9,8},{10,11... | collective-permute-start | bytes 1511432 | tf_op jit(solution)/shard_map/ppermute | solution.py:35
  445.7 113.4 %collective-permute-start.25 = (bf16[2,320,384]{2,1,0:T(8,128)(2,1)}, bf16[2,320,384]{2,1,0:T(8,128)(2,1)}, u32[]{:S(2)}, u32[]{:S(2)}) collective-permute-start(bf16[2,320,384]{2,1,0:T(8,128)(2,1)} %get-tuple-element.25), channel_id=1, source_target_pairs={{0,1},{1,0},{2,3},{3,2},{4,5},{5,4},{6,7},{7,6},{8,9},{9,8},{10,11... | collective-permute-start | bytes 1474568 | tf_op jit(solution)/shard_map/ppermute | solution.py:35
  455.1 107.5 %collective-permute-start.33 = (bf16[2,8,120,240]{3,2,1,0:T(8,128)(2,1)}, bf16[2,8,120,240]{3,2,1,0:T(8,128)(2,1)}, u32[]{:S(2)}, u32[]{:S(2)}) collective-permute-start(bf16[2,8,120,240]{3,2,1,0:T(8,128)(2,1)} %dynamic-slice_bitcast_fusion.6), channel_id=1, source_target_pairs={{0,8},{8,0},{16,24},{24,16},{1,9},{9,1},{17,25},{25,17},{2,10},{10... | collective-permute-start | bytes 2764808 | tf_op jit(solution)/shard_map/ppermute | solution.py:35
  534.3 107.2 %collective-permute-start.38 = (bf16[16,1,240,640]{3,2,0,1:T(8,128)(2,1)}, bf16[16,1,240,640]{3,2,0,1:T(8,128)(2,1)}, u32[]{:S(2)}, u32[]{:S(2)}) collective-permute-start(bf16[16,1,240,640]{3,2,0,1:T(8,128)(2,1)} %dynamic-slice_bitcast_fusion), channel_id=1, source_target_pairs={{0,8},{8,0},{16,24},{24,16},{1,9},{9,1},{17,25},{25,17},{2,10},{10... | collective-permute-start | bytes 14745608 | tf_op jit(solution)/shard_map/ppermute | solution.py:35
  542.3 24.4 %collective-permute-start.24 = (bf16[2,320,384]{2,1,0:T(8,128)(2,1)S(1)}, bf16[2,320,384]{2,1,0:T(8,128)(2,1)}, u32[]{:S(2)}, u32[]{:S(2)}) collective-permute-start(bf16[2,320,384]{2,1,0:T(8,128)(2,1)S(1)} %copy-done.9), channel_id=1, source_target_pairs={{0,1},{1,0},{2,3},{3,2},{4,5},{5,4},{6,7},{7,6},{8,9},{9,8},{10,11... | collective-permute-start | bytes 1474568 | tf_op jit(solution)/shard_map/ppermute | solution.py:35
  559.2 91.9 %collective-permute-start.43 = (bf16[2,8,120,640]{3,2,1,0:T(8,128)(2,1)}, bf16[2,8,120,640]{3,2,1,0:T(8,128)(2,1)}, u32[]{:S(2)}, u32[]{:S(2)}) collective-permute-start(bf16[2,8,120,640]{3,2,1,0:T(8,128)(2,1)} %dynamic-slice_bitcast_fusion.1), channel_id=1, source_target_pairs={{0,8},{8,0},{16,24},{24,16},{1,9},{9,1},{17,25},{25,17},{2,10},{10... | collective-permute-start | bytes 7372808 | tf_op jit(solution)/shard_map/ppermute | solution.py:35
  561.2 16.7 %collective-permute-start.26 = (bf16[2,320,384]{2,1,0:T(8,128)(2,1)}, bf16[2,320,384]{2,1,0:T(8,128)(2,1)}, u32[]{:S(2)}, u32[]{:S(2)}) collective-permute-start(bf16[2,320,384]{2,1,0:T(8,128)(2,1)} %fusion.21), channel_id=1, source_target_pairs={{2,0},{3,1},{4,2},{5,3},{6,4},{7,5},{10,8},{11,9},{12,10},{13,11},... | collective-permute-start | bytes 1474568 | tf_op jit(solution)/shard_map/ppermute | solution.py:80
  583.2 55.0 %collective-permute-start.35 = (bf16[4,1,120,240]{3,2,0,1:T(8,128)(2,1)}, bf16[4,1,120,240]{3,2,0,1:T(8,128)(2,1)}, u32[]{:S(2)}, u32[]{:S(2)}) collective-permute-start(bf16[4,1,120,240]{3,2,0,1:T(8,128)(2,1)} %dynamic-slice_bitcast_fusion.12), channel_id=1, source_target_pairs={{0,1},{1,0},{2,3},{3,2},{4,5},{5,4},{6,7},{7,6},{8,9},{9,8},{10,11... | collective-permute-start | bytes 691208 | tf_op jit(solution)/shard_map/ppermute | solution.py:35
  637.7 18.3 %collective-permute-start.28 = (bf16[2,8,208,240]{3,2,1,0:T(8,128)(2,1)S(1)}, bf16[2,8,208,240]{3,2,1,0:T(8,128)(2,1)S(1)}, u32[]{:S(2)}, u32[]{:S(2)}) collective-permute-start(bf16[2,8,208,240]{3,2,1,0:T(8,128)(2,1)S(1)} %dynamic-slice_bitcast_fusion.3), channel_id=1, source_target_pairs={{0,8},{8,0},{16,24},{24,16},{1,9},{9,1},{17,25},{25,17},{2,10},{10... | collective-permute-start | bytes 4792328 | tf_op jit(solution)/shard_map/ppermute | solution.py:35
  649.6 56.6 %collective-permute-start.39 = (bf16[8,1,240,640]{3,2,0,1:T(8,128)(2,1)}, bf16[8,1,240,640]{3,2,0,1:T(8,128)(2,1)}, u32[]{:S(2)}, u32[]{:S(2)}) collective-permute-start(bf16[8,1,240,640]{3,2,0,1:T(8,128)(2,1)} %dynamic-slice_bitcast_fusion.2), channel_id=1, source_target_pairs={{0,16},{8,24},{16,0},{24,8},{1,17},{9,25},{17,1},{25,9},{2,18},{10... | collective-permute-start | bytes 7372808 | tf_op jit(solution)/shard_map/ppermute | solution.py:35
  654.7 30.3 %collective-permute-start.44 = (bf16[8,1,120,640]{3,2,0,1:T(8,128)(2,1)}, bf16[8,1,120,640]{3,2,0,1:T(8,128)(2,1)}, u32[]{:S(2)}, u32[]{:S(2)}) collective-permute-start(bf16[8,1,120,640]{3,2,0,1:T(8,128)(2,1)} %dynamic-slice_bitcast_fusion.4), channel_id=1, source_target_pairs={{0,1},{1,0},{2,3},{3,2},{4,5},{5,4},{6,7},{7,6},{8,9},{9,8},{10,11... | collective-permute-start | bytes 3686408 | tf_op jit(solution)/shard_map/ppermute | solution.py:35
  657.5 43.6 %collective-permute-start.29 = (bf16[8,1,208,240]{3,2,0,1:T(8,128)(2,1)}, bf16[8,1,208,240]{3,2,0,1:T(8,128)(2,1)}, u32[]{:S(2)}, u32[]{:S(2)}) collective-permute-start(bf16[8,1,208,240]{3,2,0,1:T(8,128)(2,1)} %dynamic-slice_bitcast_fusion.7), channel_id=1, source_target_pairs={{0,1},{1,0},{2,3},{3,2},{4,5},{5,4},{6,7},{7,6},{8,9},{9,8},{10,11... | collective-permute-start | bytes 2396168 | tf_op jit(solution)/shard_map/ppermute | solution.py:35
  686.7 40.5 %collective-permute-start.45 = (bf16[1,4,120,640]{3,2,1,0:T(8,128)(2,1)S(1)}, bf16[1,4,120,640]{3,2,1,0:T(8,128)(2,1)S(1)}, u32[]{:S(2)}, u32[]{:S(2)}) collective-permute-start(bf16[1,4,120,640]{3,2,1,0:T(8,128)(2,1)S(1)} %dynamic-slice_bitcast_fusion.8), channel_id=1, source_target_pairs={{0,16},{8,24},{16,0},{24,8},{1,17},{9,25},{17,1},{25,9},{2,18},{10... | collective-permute-start | bytes 1843208 | tf_op jit(solution)/shard_map/ppermute | solution.py:35
  702.7 23.7 %collective-permute-start.30 = (bf16[1,4,208,240]{3,2,1,0:T(8,128)(2,1)S(1)}, bf16[1,4,208,240]{3,2,1,0:T(8,128)(2,1)S(1)}, u32[]{:S(2)}, u32[]{:S(2)}) collective-permute-start(bf16[1,4,208,240]{3,2,1,0:T(8,128)(2,1)S(1)} %dynamic-slice_bitcast_fusion.10), channel_id=1, source_target_pairs={{0,16},{8,24},{16,0},{24,8},{1,17},{9,25},{17,1},{25,9},{2,18},{10... | collective-permute-start | bytes 1198088 | tf_op jit(solution)/shard_map/ppermute | solution.py:35
  708.7 30.8 %collective-permute-start.40 = (bf16[4,1,240,640]{3,2,0,1:T(8,128)(2,1)S(1)}, bf16[4,1,240,640]{3,2,0,1:T(8,128)(2,1)S(1)}, u32[]{:S(2)}, u32[]{:S(2)}) collective-permute-start(bf16[4,1,240,640]{3,2,0,1:T(8,128)(2,1)S(1)} %dynamic-slice_bitcast_fusion.5), channel_id=1, source_target_pairs={{0,1},{1,0},{2,3},{3,2},{4,5},{5,4},{6,7},{7,6},{8,9},{9,8},{10,11... | collective-permute-start | bytes 3686408 | tf_op jit(solution)/shard_map/ppermute | solution.py:35
  739.8 18.4 %collective-permute-start.41 = (bf16[2,1,240,640]{3,2,0,1:T(8,128)(2,1)S(1)}, bf16[2,1,240,640]{3,2,0,1:T(8,128)(2,1)S(1)}, u32[]{:S(2)}, u32[]{:S(2)}) collective-permute-start(bf16[2,1,240,640]{3,2,0,1:T(8,128)(2,1)S(1)} %dynamic-slice_bitcast_fusion.9), channel_id=1, source_target_pairs={{0,2},{1,3},{2,0},{3,1},{4,6},{5,7},{6,4},{7,5},{8,10},{9,11},{10,... | collective-permute-start | bytes 1843208 | tf_op jit(solution)/shard_map/ppermute | solution.py:35
  (94 other events, 1104.8 us)

commit v2 on v1

--- a/solution.py
+++ b/solution.py
@@ -39,40 +39,58 @@
     return (lax.axis_index(axis) // mask) % 2
 
 
-def gather(block, order, major):
-    rows, cols = block.shape
-    have = []
-    buf = block[None]
-    for step in order:
-        got = swap(buf, *step)
-        before = [b for b in have if major.index(b) < major.index(step)]
-        pre = 2 ** len(before)
-        shape = (pre, buf.shape[0] // pre, rows, cols)
-        mine, theirs = buf.reshape(shape), got.reshape(shape)
-        upper = bit(*step) == 1
-        buf = jnp.stack(
-            [jnp.where(upper, theirs, mine), jnp.where(upper, mine, theirs)], axis=1
-        ).reshape(-1, rows, cols)
-        have.append(step)
-    return buf
-
-
-def scatter(buf, order, major):
-    count, rows, cols = buf.shape
-    have = list(major)
-    for index, step in enumerate(order):
-        pre = 2 ** have.index(step)
-        shape = (pre, 2, buf.shape[0] // (2 * pre), rows, cols)
-        parts = buf.reshape(shape)
-        own = bit(*step)
-        send = lax.dynamic_index_in_dim(parts, 1 - own, 1, keepdims=False)
-        keep = lax.dynamic_index_in_dim(parts, own, 1, keepdims=False)
-        got = swap(send, *step)
-        buf = (keep.astype(f32) + got.astype(f32)).reshape(-1, rows, cols)
-        if index < len(order) - 1:
-            buf = buf.astype(b16)
-        have.remove(step)
-    return buf[0]
+def gather(block, order):
+    bufs = [block[None]]
+    for index, (axis, mask) in enumerate(order):
+        got = [swap(b, axis, mask) for b in bufs]
+        if axis == "dp":
+            bufs = bufs + got
+            continue
+        upper = bit(axis, mask) == 1
+        pre = 1
+        for earlier in order[:index]:
+            pre *= 2 if earlier[0] == "ctx" else 1
+        merged = []
+        for mine, theirs in zip(bufs, got, strict=True):
+            shape = (pre, 1) + mine.shape[1:]
+            mine, theirs = mine.reshape(shape), theirs.reshape(shape)
+            both = jnp.concatenate(
+                [jnp.where(upper, theirs, mine), jnp.where(upper, mine, theirs)], axis=1
+            )
+            merged.append(both.reshape((2 * pre,) + shape[2:]))
+        bufs = merged
+    dp_masks = [mask for axis, mask in order if axis == "dp"]
+    out = [None] * len(bufs)
+    for i, b in enumerate(bufs):
+        out[sum(m for j, m in enumerate(dp_masks) if (i >> j) & 1)] = b
+    return out
+
+
+def scatter(bufs, order):
+    bufs = dict(enumerate(bufs))
+    for index, (axis, mask) in enumerate(order):
+        last = index == len(order) - 1
+        if axis == "dp":
+            keep = {r: b for r, b in bufs.items() if not r & mask}
+            send = {r: bufs[r ^ mask] for r in keep}
+        else:
+            own = bit(axis, mask)
+            keep, send = {}, {}
+            for r, b in bufs.items():
+                parts = b.reshape((b.shape[0] // 2, 2) + b.shape[1:])
+                send[r] = lax.dynamic_index_in_dim(parts, 1 - own, 1, keepdims=False)
+                keep[r] = lax.dynamic_index_in_dim(parts, own, 1, keepdims=False)
+        bufs = {}
+        for r in keep:
+            total = keep[r].astype(f32) + swap(send[r], axis, mask).astype(f32)
+            bufs[r] = total if last else total.astype(b16)
+    return bufs[0][0]
+
+
+def sum_everywhere(values, bits):
+    for axis, mask in bits:
+        values = values + swap(values, axis, mask)
+    return values
 
 
 def shift_outer(values, by):
@@ -224,6 +242,204 @@
     )(place, q_rot, datt, lse, *pieces, *pieces, *pieces)
 
 
+def turned(low, high, cosine, sine, sign):
+    return low * cosine - sign * high * sine, high * cosine + sign * low * sine
+
+
+def project_kernel(parts, q_cols, kv_cols, ctx, scale, *refs):
+    n_ref = refs[0]
+    w_refs = refs[1 : 1 + parts]
+    seg_ref, cos_ref, sin_ref, q_ref, own_ref, blocks, flat = refs[1 + parts :]
+    acc = dot(w_refs[0][...], n_ref[0], ((1,), (0,)))
+    for r in range(1, parts):
+        acc = acc + dot(w_refs[r][...], n_ref[r], ((1,), (0,)))
+    blocks[...] = acc
+    rows = blocks.shape[0] // ctx
+    width, kv_width = QUERY_HEADS * HEAD_DIM, KEY_VALUE_HEADS * HEAD_DIM
+    for c in range(ctx):
+        base = c * rows
+        flat[c * q_cols : (c + 1) * q_cols] = blocks[base : base + q_cols]
+        base += q_cols
+        at = width + c * kv_cols
+        flat[at : at + kv_cols] = blocks[base : base + kv_cols]
+        base += kv_cols
+        at += kv_width
+        flat[at : at + kv_cols] = blocks[base : base + kv_cols]
+    cosine, sine = cos_ref[...], sin_ref[...]
+    for h in range(QUERY_HEADS + KEY_VALUE_HEADS):
+        at = h * HEAD_DIM
+        pair = turned(flat[at : at + HALF], flat[at + HALF : at + HEAD_DIM], cosine, sine, 1.0)
+        for i, half in enumerate(pair):
+            if h < QUERY_HEADS:
+                q_ref[at + i * HALF : at + (i + 1) * HALF] = (half * scale).astype(b16)
+            else:
+                to = at - width + i * HALF
+                own_ref[to : to + HALF] = half.astype(b16)
+    own_ref[kv_width : 2 * kv_width] = flat[width + kv_width : width + 2 * kv_width].astype(b16)
+    own_ref[2 * kv_width : 2 * kv_width + 16] = seg_ref[...]
+
+
+def project_back_kernel(parts, q_cols, kv_cols, ctx, scale, *refs):
+    dq_ref, dkv_ref, cos_ref, sin_ref, n_ref = refs[:5]
+    w_refs = refs[5 : 5 + parts]
+    dn_ref = refs[5 + parts]
+    g_refs = refs[6 + parts : 6 + 2 * parts]
+    flat, blocks = refs[6 + 2 * parts :]
+    cosine, sine = cos_ref[...], sin_ref[...]
+    width, kv_width = QUERY_HEADS * HEAD_DIM, KEY_VALUE_HEADS * HEAD_DIM
+    for h in range(QUERY_HEADS + KEY_VALUE_HEADS):
+        at = h * HEAD_DIM
+        if h < QUERY_HEADS:
+            low, high = dq_ref[at : at + HALF] * scale, dq_ref[at + HALF : at + HEAD_DIM] * scale
+        else:
+            to = at - width
+            low, high = dkv_ref[0, to : to + HALF], dkv_ref[0, to + HALF : to + HEAD_DIM]
+        pair = turned(low, high, cosine, sine, -1.0)
+        for i, half in enumerate(pair):
+            flat[at + i * HALF : at + (i + 1) * HALF] = half
+    flat[width + kv_width : width + 2 * kv_width] = dkv_ref[1]
+    rows = blocks.shape[0] // ctx
+    tail = rows - q_cols - 2 * kv_cols
+    for c in range(ctx):
+        at = width + c * kv_cols
+        pieces = [
+            flat[c * q_cols : (c + 1) * q_cols],
+            flat[at : at + kv_cols],
+            flat[at + kv_width : at + kv_width + kv_cols],
+            jnp.zeros((tail, flat.shape[1]), f32),
+        ]
+        blocks[c * rows : (c + 1) * rows] = jnp.concatenate(pieces, axis=0).astype(b16)
+    for r in range(parts):
+        g_refs[r][...] = dot(blocks[...], n_ref[r], ((1,), (1,))).astype(b16)
+        dn_ref[r] = dot(w_refs[r][...], blocks[...], ((0,), (0,)))
+
+
+def mix_kernel(parts, me_ref, att_ref, x_ref, gain_ref, *refs):
+    w_refs = refs[:parts]
+    mid_ref, inv_ref, normed_ref = refs[parts:]
+    mid = x_ref[...].astype(f32)
+    for r in range(parts):
+        mid = mid + dot(att_ref[me_ref[0] ^ r], w_refs[r][...], ((0,), (1,)))
+    mid_ref[...] = mid
+    inv = lax.rsqrt(jnp.mean(mid * mid, axis=-1, keepdims=True) + epsilon)
+    inv_ref[...] = inv
+    normed_ref[...] = (mid * inv * gain_ref[...]).astype(b16)
+
+
+def mix_back_kernel(parts, me_ref, att_ref, grad_ref, *refs):
+    w_refs = refs[:parts]
+    datt_ref = refs[parts]
+    g_refs = refs[1 + parts :]
+    flipped = grad_ref[...].T.astype(b16)
+    for r in range(parts):
+        at = me_ref[0] ^ r
+        g_refs[r][...] = dot(flipped, att_ref[at], ((1,), (1,))).astype(b16)
+        datt_ref[at] = dot(w_refs[r][...], flipped, ((0,), (0,))).astype(b16)
+
+
+def ffn_kernel(parts, per, me_ref, n_ref, nt_ref, cot_ref, cot_t_ref, mid_ref, *refs):
+    f_refs = refs[:parts]
+    d_refs = refs[parts : 2 * parts]
+    out_ref, dn_ref = refs[2 * parts : 2 * parts + 2]
+    gf_refs = refs[2 * parts + 2 : 3 * parts + 2]
+    gd_refs = refs[3 * parts + 2 : 4 * parts + 2]
+    acc, down, g_down, hidden = refs[4 * parts + 2 :]
+    step = pl.program_id(0)
+    for r in range(parts):
+
+        @pl.when(step == r)
+        def _(r=r):
+            down[...] = d_refs[r][...]
+
+    @pl.when(step == 0)
+    def _():
+        acc[...] = jnp.zeros_like(acc)
+        dn_ref[...] = jnp.zeros_like(dn_ref)
+
+    ff = f_refs[0].shape[2] // 2
+    d_hidden = dot(cot_ref[...], down[...], ((1,), (0,)))
+    for i in range(per):
+        both = dot(n_ref[0], f_refs[0][i], ((1,), (0,)))
+        for r in range(1, parts):
+            both = both + dot(n_ref[r], f_refs[r][i], ((1,), (0,)))
+        gate, up = both[:, :ff], both[:, ff:]
+        grad = d_hidden[:, i * ff : (i + 1) * ff]
+        sigma = jax.nn.sigmoid(gate)
+        silu = gate * sigma
+        hidden[:, i * ff : (i + 1) * ff] = (silu * up).astype(b16)
+        d_gate = grad * up * (sigma * (1.0 + gate * (1.0 - sigma)))
+        d_both = jnp.concatenate([d_gate, grad * silu], axis=1).astype(b16)
+        for r in range(parts):
+            gf_refs[r][i] = dot(nt_ref[r], d_both, ((1,), (0,))).astype(b16)
+            dn_ref[r] += dot(d_both, f_refs[r][i], ((1,), (1,)))
+    acc[...] += dot(hidden[...], down[...], ((1,), (1,)))
+    g_down[...] = dot(cot_t_ref[...], hidden[...], ((1,), (0,))).astype(b16)
+    for r in range(parts):
+
+        @pl.when(step == r)
+        def _(r=r):
+            gd_refs[r][...] = g_down[...]
+
+    @pl.when(step == parts - 1)
+    def _():
+        out_ref[...] = (mid_ref[...] + acc[...]).astype(b16)
+
+
+def ffn(me, n_rel, nt_rel, cot, cot_t, mid, f_list, d_list):
+    parts = len(f_list)
+    ctx, rows, wide = f_list[0].shape
+    per = ctx // parts
+    tokens, width = mid.shape
+    down_shape = d_list[0].shape
+
+    def whole(a):
+        return pl.BlockSpec(a.shape, lambda i, me: (0,) * a.ndim, pipeline_mode=pl.Buffered(1))
+
+    f_spec = pl.BlockSpec((per, rows, wide), lambda i, me: (me[0] ^ i, 0, 0))
+    out_shape = [
+        jax.ShapeDtypeStruct((tokens, width), b16),
+        jax.ShapeDtypeStruct((parts, tokens, rows), f32),
+    ]
+    out_shape += [jax.ShapeDtypeStruct((ctx, rows, wide), b16)] * parts
+    out_shape += [jax.ShapeDtypeStruct(down_shape, b16)] * parts
+    return pl.pallas_call(
+        functools.partial(ffn_kernel, parts, per),
+        grid_spec=pltpu.PrefetchScalarGridSpec(
+            num_scalar_prefetch=1,
+            grid=(parts,),
+            in_specs=[whole(a) for a in (n_rel, nt_rel, cot, cot_t, mid)]
+            + [f_spec] * parts
+            + [whole(a) for a in d_list],
+            out_specs=[whole(a) for a in out_shape[:2]]
+            + [f_spec] * parts
+            + [whole(a) for a in d_list],
+            scratch_shapes=[
+                pltpu.VMEM((tokens, width), f32),
+                pltpu.VMEM(down_shape, b16),
+                pltpu.VMEM(down_shape, b16),
+                pltpu.VMEM((tokens, per * wide // 2), b16),
+            ],
+        ),
+        out_shape=out_shape,
+        compiler_params=pltpu.CompilerParams(vmem_limit_bytes=58 << 20),
+        name="ffn",
+    )(me, n_rel, nt_rel, cot, cot_t, mid, *f_list, *d_list)
+
+
+def in_vmem(kernel, name, out_shape, scratch, *args, scalars=0):
+    vmem = pl.BlockSpec(memory_space=pltpu.VMEM)
+    smem = pl.BlockSpec(memory_space=pltpu.SMEM)
+    return pl.pallas_call(
+        kernel,
+        in_specs=[smem] * scalars + [vmem] * (len(args) - scalars),
+        out_specs=[vmem] * len(out_shape),
+        out_shape=out_shape,
+        scratch_shapes=scratch,
+        compiler_params=pltpu.CompilerParams(vmem_limit_bytes=48 << 20),
+        name=name,
+    )(*args)
+
+
 def per_device(
     inputs,
     gain_one,
@@ -244,69 +460,71 @@
     rows = query_weight.shape[0]
     q_cols, kv_cols = query_weight.shape[1], key_weight.shape[1]
     ff_cols = gate_weight.shape[1]
-    ff = ff_cols * ctx
     down_rows, out_cols = down_weight.shape
     kv_width = KEY_VALUE_HEADS * HEAD_DIM
+    shape_of = jax.ShapeDtypeStruct
 
     dp_bits, ctx_bits = bits_of("dp", dp), bits_of("ctx", ctx)
-    dp_major = dp_bits + ctx_bits
-    ctx_major = ctx_bits + dp_bits
     x_last = ctx_bits + dp_bits
     y_last = ctx_bits[:-1] + dp_bits[:-1] + ctx_bits[-1:] + dp_bits[-1:]
 
     place = lax.axis_index("ctx")
-
-    gains = jnp.stack([gain_one, gain_two])
+    me = lax.axis_index("dp")
+    me_arg = me.reshape(1).astype(jnp.int32)
+    place_arg = place.reshape(1).astype(jnp.int32)
+
+    def relative(stacked):
+        return jnp.stack(
+            [lax.dynamic_index_in_dim(stacked, me ^ r, 0, keepdims=False) for r in range(dp)]
+        )
+
+    gains = jnp.concatenate([gain_one, gain_two])
     gain_rows = -(-gains.size // rows)
-    gains = jnp.pad(gains.reshape(-1), (0, gain_rows * rows - gains.size)).reshape(gain_rows, rows)
+    gains = jnp.pad(gains, (0, gain_rows * rows - gains.size)).reshape(gain_rows, rows)
     pad_rows = -(q_cols + 2 * kv_cols + gain_rows) % 16
     qkv_block = jnp.concatenate(
         [query_weight.T, key_weight.T, value_weight.T, gains, jnp.zeros((pad_rows, rows), b16)]
     )
-    qkv_all = gather(qkv_block, y_last, dp_major).reshape(dp, ctx, -1, rows)
-    out_all = gather(output_weight.T, x_last, dp_major).reshape(dp, ctx, -1, rows)
-    gu_all = gather(jnp.concatenate([gate_weight, up_weight], axis=1), x_last, ctx_major).reshape(
-        ctx, dp, rows, 2 * ff_cols
-    )
-    down_all = gather(down_weight.T, y_last, dp_major).reshape(dp, ctx, out_cols, down_rows)
-
-    def columns(piece):
-        return jnp.transpose(piece, (1, 2, 0, 3)).reshape(-1, dp * rows)
-
-    wq = columns(qkv_all[:, :, :q_cols])
-    wk = columns(qkv_all[:, :, q_cols : q_cols + kv_cols])
-    wv = columns(qkv_all[:, :, q_cols + kv_cols : q_cols + 2 * kv_cols])
-    w_qkv = jnp.concatenate([wq, wk, wv])
+    qkv_all = gather(qkv_block, y_last)
+    out_all = gather(output_weight.T, x_last)
+    gu_all = gather(jnp.concatenate([gate_weight, up_weight], axis=1), x_last)
+    down_all = gather(down_weight.T, y_last)
+
     first_gain = q_cols + 2 * kv_cols
-    gain_all = qkv_all[0, :, first_gain : first_gain + gain_rows].reshape(ctx, -1)
+    gain_all = qkv_all[0][:, first_gain : first_gain + gain_rows].reshape(ctx, -1)
     gain_part = gain_one.shape[0]
-    gain_a = gain_all[:, :gain_part].reshape(width).astype(f32)
-    gain_b = gain_all[:, gain_part : 2 * gain_part].reshape(width).astype(f32)
-    wo = columns(out_all)
-
-    x = inputs.reshape(total, width).astype(f32)
+    gain_a = gain_all[:, :gain_part].reshape(1, width).astype(f32)
+    gain_b = gain_all[:, gain_part : 2 * gain_part].reshape(1, width).astype(f32)
+    qkv_all = [a.reshape(-1, rows) for a in qkv_all]
+    out_all = [a.reshape(-1, rows) for a in out_all]
+    down_all = [a.reshape(-1, down_rows) for a in down_all]
+
+    cot = cotangent.reshape(total, width)
+    cot_t = cot.T
+    x_low = inputs.reshape(total, width)
+    x = x_low.astype(f32)
     inv_one = lax.rsqrt(jnp.mean(x * x, axis=-1, keepdims=True) + epsilon)
     normed_one = (x * inv_one * gain_a).astype(b16)
-    qkv = dot(w_qkv, normed_one, ((1,), (1,)))
+    one_t = relative(normed_one.T.reshape(dp, rows, total))
     positions = (place * tokens + jnp.arange(tokens, dtype=jnp.int32)).astype(f32)
     positions = jnp.tile(positions, sequences)
     frequency = jnp.exp(jnp.arange(HALF, dtype=f32) * (-2.0 * math.log(rope_base) / HEAD_DIM))
     angles = frequency[:, None] * positions[None, :]
     cosine, sine = jnp.cos(angles), jnp.sin(angles)
-
-    def turn(values, sign):
-        parts = values.reshape(-1, 2, HALF, total)
-        low, high = parts[:, 0], parts[:, 1]
-        return jnp.stack(
-            [low * cosine - sign * high * sine, high * cosine + sign * low * sine], axis=1
-        ).reshape(-1, total)
-
     score_scale = HEAD_DIM ** (-0.5)
-    q_rot = (turn(qkv[:width], 1.0) * score_scale).astype(b16)
-    k_rot = turn(qkv[width : width + kv_width], 1.0).astype(b16)
-    v_low = qkv[width + kv_width :].astype(b16)
     seg_row = jnp.pad(segment_ids.reshape(1, total).astype(b16), ((0, 15), (0, 0)))
-    own = jnp.concatenate([k_rot, v_low, seg_row])
+    block_rows = qkv_all[0].shape[0]
+    q_rot, own = in_vmem(
+        functools.partial(project_kernel, dp, q_cols, kv_cols, ctx, score_scale),
+        "project",
+        [shape_of((width, total), b16), shape_of((2 * kv_width + 16, total), b16)],
+        [pltpu.VMEM((block_rows, total), f32), pltpu.VMEM((width + 2 * kv_width, total), f32)],
+        one_t,
+        *qkv_all,
+        seg_row,
+        cosine,
+        sine,
+    )
 
     steps = ctx // 4
     inner = bit("ctx", 1)
@@ -321,41 +539,27 @@
         pieces += [straight[k], crossed[k]]
     pieces.append(straight[steps])
 
-    place_arg = place.reshape(1).astype(jnp.int32)
     att, lse = attend(place_arg, q_rot, pieces, sequences, tokens)
-
-    mid = x + dot(att, wo, ((0,), (1,)))
-    inv_two = lax.rsqrt(jnp.mean(mid * mid, axis=-1, keepdims=True) + epsilon)
-    normed_two = (mid * inv_two * gain_b).astype(b16)
-    w_gate = jnp.transpose(gu_all[..., :ff_cols], (1, 2, 0, 3)).reshape(width, ff)
-    w_up = jnp.transpose(gu_all[..., ff_cols:], (1, 2, 0, 3)).reshape(width, ff)
-    w_down = jnp.transpose(down_all, (1, 2, 0, 3)).reshape(width, ff)
-    gate = dot(normed_two, w_gate, ((1,), (0,)))
-    up = dot(normed_two, w_up, ((1,), (0,)))
-    sigma = jax.nn.sigmoid(gate)
-    hidden = (gate * sigma * up).astype(b16)
-    output = (mid + dot(hidden, w_down, ((1,), (1,)))).astype(b16)
-
-    cot = cotangent.reshape(total, width)
-    d_hidden = dot(cot, w_down, ((1,), (0,)))
-    d_up = (d_hidden * gate * sigma).astype(b16)
-    d_gate = (d_hidden * up * sigma * (1.0 + gate * (1.0 - sigma))).astype(b16)
-    g_down = dot(cot, hidden, ((0,), (0,))).astype(b16)
-    g_down = jnp.transpose(g_down.reshape(ctx, out_cols, dp, down_rows), (2, 0, 1, 3))
-    g_down = scatter(
-        g_down.reshape(dp * ctx, out_cols, down_rows), y_last[::-1], dp_major
-    )
-    g_gate = dot(normed_two, d_gate, ((0,), (0,))).astype(b16)
-    g_up = dot(normed_two, d_up, ((0,), (0,))).astype(b16)
-    g_gu = jnp.concatenate(
-        [
-            jnp.transpose(g.reshape(dp, rows, ctx, ff_cols), (2, 0, 1, 3))
-            for g in (g_gate, g_up)
-        ],
-        axis=-1,
-    )
-    g_gu = scatter(g_gu.reshape(ctx * dp, rows, 2 * ff_cols), x_last[::-1], ctx_major)
-    d_normed_two = dot(d_gate, w_gate, ((1,), (1,))) + dot(d_up, w_up, ((1,), (1,)))
+    att_3 = att.reshape(dp, rows, total)
+
+    mid, inv_two, normed_two = in_vmem(
+        functools.partial(mix_kernel, dp),
+        "mix",
+        [shape_of((total, width), f32), shape_of((total, 1), f32), shape_of((total, width), b16)],
+        [],
+        me_arg,
+        att_3,
+        x_low,
+        gain_b,
+        *out_all,
+        scalars=1,
+    )
+    two_t = relative(normed_two.T.reshape(dp, rows, total))
+    two = jnp.transpose(two_t, (0, 2, 1))
+    output, d_two, *grads = ffn(me_arg, two, two_t, cot, cot_t, mid, gu_all, down_all)
+    g_gu = scatter(grads[:dp], x_last[::-1])
+    g_down = scatter([g.reshape(ctx, out_cols, down_rows) for g in grads[dp:]], y_last[::-1])
+    d_normed_two = jnp.transpose(relative(d_two), (1, 0, 2)).reshape(total, width)
     g_gain_two = jnp.sum(d_normed_two * mid * inv_two, axis=0)
     scaled_two = gain_b * d_normed_two
     d_mid = (
@@ -363,16 +567,19 @@
         + inv_two * scaled_two
         - mid * inv_two**3 * jnp.mean(scaled_two * mid, axis=-1, keepdims=True)
     )
-    d_mid_low = d_mid.astype(b16)
-
-    def to_blocks(grad, n):
-        return jnp.transpose(grad.reshape(ctx, n, dp, rows), (2, 0, 1, 3))
-
-    g_out = dot(d_mid_low, att, ((0,), (1,))).astype(b16)
-    g_out = scatter(
-        to_blocks(g_out, out_cols).reshape(dp * ctx, out_cols, rows), x_last[::-1], dp_major
-    )
-    d_att = dot(wo, d_mid_low, ((0,), (1,))).astype(b16)
+    d_att, *g_out = in_vmem(
+        functools.partial(mix_back_kernel, dp),
+        "mix_back",
+        [shape_of(att_3.shape, b16)] + [shape_of((width, rows), b16)] * dp,
+        [],
+        me_arg,
+        att_3,
+        d_mid,
+        *out_all,
+        scalars=1,
+    )
+    g_out = scatter([g.reshape(ctx, out_cols, rows) for g in g_out], x_last[::-1])
+    d_att = d_att.reshape(width, total)
     dq_rot, *parts = attend_back(place_arg, q_rot, d_att, lse, pieces, sequences, tokens)
 
     returned = [swap(parts[2 * k + 1], "ctx", 1).astype(f32) for k in range(steps)]
@@ -388,12 +595,23 @@
     for k in range(steps, 0, -1):
         carried = here[k - 1] + shift_outer(carried.astype(b16), -1).astype(f32)
 
-    d_q = (turn(dq_rot, -1.0) * score_scale).astype(b16)
-    d_k = turn(carried[0], -1.0).astype(b16)
-    d_v = carried[1].astype(b16)
-    d_qkv = jnp.concatenate([d_q, d_k, d_v])
-    g_qkv = dot(d_qkv, normed_one, ((1,), (0,))).astype(b16)
-    d_normed_one = dot(d_qkv, w_qkv, ((0,), (0,)))
+    d_one_t, *g_qkv = in_vmem(
+        functools.partial(project_back_kernel, dp, q_cols, kv_cols, ctx, score_scale),
+        "project_back",
+        [shape_of((dp, rows, total), f32)] + [shape_of((block_rows, rows), b16)] * dp,
+        [
+            pltpu.VMEM((width + 2 * kv_width, total), f32),
+            pltpu.VMEM((block_rows, total), b16),
+        ],
+        dq_rot,
+        carried,
+        cosine,
+        sine,
+        one_t,
+        *qkv_all,
+    )
+    g_qkv = scatter([g.reshape(ctx, -1, rows) for g in g_qkv], y_last[::-1])
+    d_normed_one = relative(d_one_t).reshape(width, total).T
     g_gain_one = jnp.sum(d_normed_one * x * inv_one, axis=0)
     scaled_one = gain_a * d_normed_one
     input_grad = (
@@ -401,33 +619,17 @@
         + inv_one * scaled_one
         - x * inv_one**3 * jnp.mean(scaled_one * x, axis=-1, keepdims=True)
     ).astype(b16)
-
-    g_gains = jnp.concatenate(
-        [g_gain_one.reshape(ctx, gain_part), g_gain_two.reshape(ctx, gain_part)], axis=1
-    ).astype(b16)
-    g_gains = jnp.pad(g_gains, ((0, 0), (0, gain_rows * rows - 2 * gain_part)))
-    g_gains = jnp.broadcast_to(g_gains.reshape(1, ctx, gain_rows, rows), (dp, ctx, gain_rows, rows))
-    g_block = jnp.concatenate(
-        [
-            to_blocks(g_qkv[:width], q_cols),
-            to_blocks(g_qkv[width : width + kv_width], kv_cols),
-            to_blocks(g_qkv[width + kv_width :], kv_cols),
-            g_gains,
-            jnp.zeros((dp, ctx, pad_rows, rows), b16),
-        ],
-        axis=2,
-    )
-    g_block = scatter(g_block.reshape(dp * ctx, -1, rows), y_last[::-1], dp_major)
-    g_gains = g_block[first_gain : first_gain + gain_rows].reshape(-1)
+    g_gains = sum_everywhere(jnp.stack([g_gain_one, g_gain_two]), dp_bits + ctx_bits)
+    g_gains = lax.dynamic_slice_in_dim(g_gains, place * gain_part, gain_part, 1)
     return (
         output.reshape(sequences, tokens, width),
         input_grad.reshape(sequences, tokens, width),
-        g_gains[:gain_part],
-        g_block[:q_cols].T,
-        g_block[q_cols : q_cols + kv_cols].T,
-        g_block[q_cols + kv_cols : first_gain].T,
+        g_gains[0],
+        g_qkv[:q_cols].T,
+        g_qkv[q_cols : q_cols + kv_cols].T,
+        g_qkv[q_cols + kv_cols : first_gain].T,
         g_out.T,
-        g_gains[gain_part : 2 * gain_part],
+        g_gains[1],
         g_gu[:, :ff_cols],
         g_gu[:, ff_cols:],
         g_down.T,

time: 786 us -> 525 us (0.67)
  local copies, waits for them, and re-layouts: 268 us -> 62.7 us
  matrix products: 58.3 us -> 0 us
  Pallas kernels: 38.9 us -> 96.7 us
  other arithmetic: 91.9 us -> 51.5 us
  waiting for transfers between devices: 261 us -> 231 us
  starting transfers between devices: 53.3 us -> 71.9 us
    reshape x22 -> x3, local copies, waits for them, and re-layouts: 106 us -> 6.09 us  [the longest x1 3.09 us: per_device(): jnp.transpose(relative(d_two), (1, 0, 2)).reshape(total, width)]
    dot_general x15 -> x0, matrix products: 58.3 us -> none  [dot(): return lax.dot_general(a, b, (dims, ((), ())), preferred_element_type=f32)]
    pallas_call x0 -> x5, Pallas kernels: none -> 57.9 us  [the longest x1 40.3 us: ffn(): pl.pallas_call(functools.partial(ffn_kernel, parts, per), grid_spec=pltpu...]
    transpose x14 -> x7, local copies, waits for them, and re-layouts: 52 us -> 12.8 us  [the longest x1 3 us: per_device(): jnp.transpose(relative(d_two), (1, 0, 2)).reshape(total, width)]
    concatenate x5 -> x6, local copies, waits for them, and re-layouts: 36.9 us -> 4.23 us  [gather(): jnp.concatenate([jnp.where(upper, theirs, mine), jnp.where(upper, mine, t...]
    another operation x37 -> x4, other arithmetic: 31 us -> 2.59 us  [the longest x3 2.58 us: relative(): jnp.stack([lax.dynamic_index_in_dim(stacked, me ^ r, 0, keepdims=False) f...]
    ppermute x4, waiting for transfers between devices: 35.8 us -> 13.8 us  [shift_outer(): lax.ppermute(values, 'ctx', [(i, i + 2 * by) for i in range(size) if 0 <=...]
    ppermute x44 -> x61, starting transfers between devices: 41.8 us -> 62.2 us  [swap(): return lax.ppermute(values, axis, [(i, i ^ mask) for i in range(size)])]
  transfers between devices with their start and end apart: 48 -> 65, of which waited for: 21 -> 30; matrix products, arithmetic and copies ran while one was open for 36% -> 17% of each run, Pallas kernels for 2% -> 10%
where the time goes in v2:
time: 525 us; the launch traced here: 516 us
  waiting for transfers between devices  231 us (44%)
  Pallas kernels  96.7 us (18%)
  starting transfers between devices  71.9 us (14%)
  local copies, waits for them, and re-layouts  62.7 us (12%)
  other arithmetic  51.5 us (10%)
    ppermute x61, waiting for transfers between devices, swap(): return lax.ppermute(values, axis, [(i, i ^ mask) for i in range(size)])  217 us
    ppermute x61, starting transfers between devices, swap(): return lax.ppermute(values, axis, [(i, i ^ mask) for i in range(size)])  62.2 us
    pallas_call x1, Pallas kernels, ffn(): pl.pallas_call(functools.partial(ffn_kernel, parts, per), grid_spec=pltpu...  40.3 us
    unnamed x98, local copies, waits for them, and re-layouts  23.9 us
    pallas_call x1, Pallas kernels, attend_back(): pl.pallas_call(functools.partial(backward_kernel, blocks, tokens), grid_s...  23.6 us
    convert_element_type x18, other arithmetic, scatter(): bufs[r] = total if last else total.astype(b16)  18.9 us
    pallas_call x4, Pallas kernels, in_vmem(): pl.pallas_call(kernel, in_specs=[smem] * scalars + [vmem] * (len(args) -...  17.6 us
    pallas_call x1, Pallas kernels, attend(): pl.pallas_call(functools.partial(forward_kernel, blocks, tokens), grid_sp...  15.2 us
  transfers between devices with their start and end apart: 65, of which 30 were waited for; matrix products, arithmetic and copies ran while one was open for 17% of the time, Pallas kernels for 10%

profile of v2, /device:TPU:0, one launch (start us, length us, event | category | flops | bytes accessed | tf_op | source)
XLA Modules:
  0.0 516.0 jit_solution(12640199203666685311)
XLA Ops:
  2.3 4.0 collective-permute-start.11
  8.0 3.9 concatenate.96
  17.7 21.8 %collective-permute-done.17 = bf16[1,240,640]{2,1,0:T(8,128)(2,1)S(1)} collective-permute-done((bf16[1,240,640]{2,1,0:T(8,128)(2,1)S(1)}, bf16[1,240,640]{2,1,0:T(8,128)(2,1)S(1)}, u32[]{:S(2)}, u32[]{:S(2)}) %collective-permute-start.17) | collective-permute-done | bytes 307232 | tf_op jit(solution)/shard_map/ppermute | solution.py:35
  46.5 10.1 %collective-permute-done.18 = bf16[2,240,640]{2,1,0:T(8,128)(2,1)S(1)} collective-permute-done((bf16[2,240,640]{2,1,0:T(8,128)(2,1)S(1)}, bf16[2,240,640]{2,1,0:T(8,128)(2,1)S(1)}, u32[]{:S(2)}, u32[]{:S(2)}) %collective-permute-start.18) | collective-permute-done | bytes 614432 | tf_op jit(solution)/shard_map/ppermute | solution.py:35
  70.7 16.2 %collective-permute-done.19 = bf16[4,240,640]{2,1,0:T(8,128)(2,1)S(1)} collective-permute-done((bf16[4,240,640]{2,1,0:T(8,128)(2,1)S(1)}, bf16[4,240,640]{2,1,0:T(8,128)(2,1)S(1)}, u32[]{:S(2)}, u32[]{:S(2)}) %collective-permute-start.19) | collective-permute-done | bytes 1228832 | tf_op jit(solution)/shard_map/ppermute | solution.py:35
  90.8 4.7 collective-permute-done.2
  96.0 4.1 collective-permute-done.5
  117.3 8.7 %collective-permute-done.7.refs_3_.refs_8_.refs_13_.refs_5_.refs_10_.refs_15_ = bf16[656,384]{1,0:T(8,128)(2,1)S(1)} collective-permute-done((bf16[656,384]{1,0:T(8,128)(2,1)S(1)}, bf16[656,384]{1,0:T(8,128)(2,1)S(1)}, u32[]{:S(2)}, u32[]{:S(2)}) %collective-permute-start.7) | collective-permute-done | bytes 503840 | tf_op jit(solution)/shard_map/ppermute | solution.py:98
  126.0 4.4 collective-permute-start.9
  130.4 5.8 %collective-permute-done.13 = bf16[4,120,240]{2,1,0:T(8,128)(2,1)S(1)} collective-permute-done((bf16[4,120,240]{2,1,0:T(8,128)(2,1)S(1)}, bf16[4,120,240]{2,1,0:T(8,128)(2,1)S(1)}, u32[]{:S(2)}, u32[]{:S(2)}) %collective-permute-start.13) | collective-permute-done | bytes 230432 | tf_op jit(solution)/shard_map/ppermute | solution.py:35
  136.3 11.8 %collective-permute-done.27 = bf16[4,120,640]{2,1,0:T(8,128)(2,1)} collective-permute-done((bf16[4,120,640]{2,1,0:T(8,128)(2,1)}, bf16[4,120,640]{2,1,0:T(8,128)(2,1)}, u32[]{:S(2)}, u32[]{:S(2)}) %collective-permute-start.27) | collective-permute-done | bytes 614432 | tf_op jit(solution)/shard_map/ppermute | solution.py:35
  153.2 7.3 %collective-permute-done.28 = bf16[4,120,640]{2,1,0:T(8,128)(2,1)S(1)} collective-permute-done((bf16[4,120,640]{2,1,0:T(8,128)(2,1)}, bf16[4,120,640]{2,1,0:T(8,128)(2,1)S(1)}, u32[]{:S(2)}, u32[]{:S(2)}) %collective-permute-start.28) | collective-permute-done | bytes 614432 | tf_op jit(solution)/shard_map/ppermute | solution.py:35
  167.5 6.8 %collective-permute-done.10.refs_4_.refs_9_.refs_14_.refs_6_.refs_11_.refs_16_ = bf16[656,384]{1,0:T(8,128)(2,1)S(1)} collective-permute-done((bf16[656,384]{1,0:T(8,128)(2,1)S(1)}, bf16[656,384]{1,0:T(8,128)(2,1)S(1)}, u32[]{:S(2)}, u32[]{:S(2)}) %collective-permute-start.10) | collective-permute-done | bytes 503840 | tf_op jit(solution)/shard_map/ppermute | solution.py:35
  174.3 6.2 %collective-permute-done.8.refs_2_.refs_7_.refs_12_.refs_4_.refs_9_.refs_14_ = bf16[656,384]{1,0:T(8,128)(2,1)S(1)} collective-permute-done((bf16[656,384]{1,0:T(8,128)(2,1)S(1)}, bf16[656,384]{1,0:T(8,128)(2,1)S(1)}, u32[]{:S(2)}, u32[]{:S(2)}) %collective-permute-start.8) | collective-permute-done | bytes 503840 | tf_op jit(solution)/shard_map/ppermute | solution.py:35
  186.5 15.2 %attend.1 = (bf16[960,384]{1,0:T(8,128)(2,1)S(1)}, f32[5,8,384]{2,1,0:T(8,128)S(1)}) custom-call(s32[1]{0:T(128)} %bitcast.1.place_ref, bf16[960,384]{1,0:T(8,128)(2,1)S(1)} %copy-done.13, bf16[656,384]{1,0:T(8,128)(2,1)S(1)} %get-tuple-element.45.refs_1_.refs_6_.refs_11_.refs_3_.refs_8_.refs_13_, ...), custom_call_target="tpu_custom_call" | custom-call | tf_op jit(solution)/shard_map/attend/pallas_call | solution.py:201
  215.3 40.3 %ffn.1 = (bf16[384,960]{1,0:T(8,128)(2,1)}, f32[4,384,240]{2,1,0:T(8,128)}, bf16[8,240,640]{2,1,0:T(8,128)(2,1)}, bf16[8,240,640]{2,1,0:T(8,128)(2,1)}, bf16[8,2...) custom-call(s32[1]{0:T(128)} %bitcast.me_ref, ...), custom_call_target="tpu_custom_call" | custom-call | tf_op jit(solution)/shard_map/ffn/pallas_call | solution.py:405
  270.3 4.1 mix_back.1
  275.8 23.6 %attend_back.1 = (f32[960,384]{1,0:T(8,128)}, bf16[2,320,384]{2,1,0:T(8,128)(2,1)S(1)}, bf16[2,320,384]{2,1,0:T(8,128)(2,1)}, bf16[2,320,384]{2,1,0:T(8,128)(2,1...) custom-call(s32[1]{0:T(128)} %bitcast.1.place_ref, bf16[960,384]{1,0:T(8,128)(2,1)S(1)} %copy-done.14, ...), custom_call_target="tpu_custom_call" | custom-call | tf_op jit(solution)/shard_map/attend_back/pallas_call | solution.py:225
  306.4 8.6 %collective-permute-done.31 = bf16[2,320,384]{2,1,0:T(8,128)(2,1)S(1)} collective-permute-done((bf16[2,320,384]{2,1,0:T(8,128)(2,1)S(1)}, bf16[2,320,384]{2,1,0:T(8,128)(2,1)S(1)}, u32[]{:S(2)}, u32[]{:S(2)}) %collective-permute-start.31) | collective-permute-done | bytes 491552 | tf_op jit(solution)/shard_map/ppermute | solution.py:35
  320.4 4.3 collective-permute-done.30
  324.7 5.1 collective-permute-done.32
  337.7 5.1 collective-permute-start.50
  346.9 6.3 %collective-permute-done.50 = bf16[2,120,240]{2,1,0:T(8,128)(2,1)S(1)} collective-permute-done((bf16[2,120,240]{2,1,0:T(8,128)(2,1)S(1)}, bf16[2,120,240]{2,1,0:T(8,128)(2,1)S(1)}, u32[]{:S(2)}, u32[]{:S(2)}) %collective-permute-start.50) | collective-permute-done | bytes 115232 | tf_op jit(solution)/shard_map/ppermute | solution.py:35
  355.0 7.3 %project_back.1 = (f32[4,240,384]{2,1,0:T(8,128)}, bf16[1664,240]{1,0:T(8,128)(2,1)S(1)}, bf16[1664,240]{1,0:T(8,128)(2,1)S(1)}, bf16[1664,240]{1,0:T(8,128)(2,1)S(1)}, bf16[1664,240]{1,0:T(8,128)(2,1)S(1)}) custom-call(f32[960,384]{1,0:T(8,128)} %get-tuple-element.54.refs_0_, f32[2,320,384]{2,1,0:T(8,128)} %fusion.17.refs_1_, ...), custom_call_target="tpu_custom_call" | custom-call | tf_op jit(solution)/shard_map/project_back/pallas_call | solution.py:432
  375.0 3.9 add_convert_fusion.1
  389.4 9.4 %collective-permute-done.38 = f32[2,960]{1,0:T(2,128)S(1)} collective-permute-done((f32[2,960]{1,0:T(2,128)S(1)}, f32[2,960]{1,0:T(2,128)S(1)}, u32[]{:S(2)}, u32[]{:S(2)}) %collective-permute-start.38) | collective-permute-done | bytes 7712 | tf_op jit(solution)/shard_map/ppermute | solution.py:35
  412.0 9.2 %collective-permute-done.59 = bf16[4,120,640]{2,1,0:T(8,128)(2,1)S(1)} collective-permute-done((bf16[4,120,640]{2,1,0:T(8,128)(2,1)}, bf16[4,120,640]{2,1,0:T(8,128)(2,1)S(1)}, u32[]{:S(2)}, u32[]{:S(2)}) %collective-permute-start.59) | collective-permute-done | bytes 614432 | tf_op jit(solution)/shard_map/ppermute | solution.py:35
  422.2 25.8 %collective-permute-done.62 = bf16[4,120,640]{2,1,0:T(8,128)(2,1)S(1)} collective-permute-done((bf16[4,120,640]{2,1,0:T(8,128)(2,1)S(1)}, bf16[4,120,640]{2,1,0:T(8,128)(2,1)S(1)}, u32[]{:S(2)}, u32[]{:S(2)}) %collective-permute-start.62) | collective-permute-done | bytes 614432 | tf_op jit(solution)/shard_map/ppermute | solution.py:35
  454.9 6.6 %collective-permute-done.63 = bf16[2,120,640]{2,1,0:T(8,128)(2,1)S(1)} collective-permute-done((bf16[2,120,640]{2,1,0:T(8,128)(2,1)S(1)}, bf16[2,120,640]{2,1,0:T(8,128)(2,1)S(1)}, u32[]{:S(2)}, u32[]{:S(2)}) %collective-permute-start.63) | collective-permute-done | bytes 307232 | tf_op jit(solution)/shard_map/ppermute | solution.py:35
  466.2 14.3 %collective-permute-done.55 = bf16[4,240,640]{2,1,0:T(8,128)(2,1)S(1)} collective-permute-done((bf16[4,240,640]{2,1,0:T(8,128)(2,1)S(1)}, bf16[4,240,640]{2,1,0:T(8,128)(2,1)S(1)}, u32[]{:S(2)}, u32[]{:S(2)}) %collective-permute-start.55) | collective-permute-done | bytes 1228832 | tf_op jit(solution)/shard_map/ppermute | solution.py:35
  483.7 11.8 %collective-permute-done.45 = bf16[1,208,240]{2,1,0:T(8,128)(2,1)S(1)} collective-permute-done((bf16[1,208,240]{2,1,0:T(8,128)(2,1)S(1)}, bf16[1,208,240]{2,1,0:T(8,128)(2,1)S(1)}, u32[]{:S(2)}, u32[]{:S(2)}) %collective-permute-start.45) | collective-permute-done | bytes 99872 | tf_op jit(solution)/shard_map/ppermute | solution.py:35
  500.6 12.9 %collective-permute-done.57 = bf16[1,240,640]{2,1,0:T(8,128)(2,1)S(1)} collective-permute-done((bf16[1,240,640]{2,1,0:T(8,128)(2,1)S(1)}, bf16[1,240,640]{2,1,0:T(8,128)(2,1)S(1)}, u32[]{:S(2)}, u32[]{:S(2)}) %collective-permute-start.57) | collective-permute-done | bytes 307232 | tf_op jit(solution)/shard_map/ppermute | solution.py:35
  (332 shorter events, 183.9 us)
Async XLA Ops:
  2.3 59.8 %collective-permute-start.11 = (bf16[1,120,240]{2,1,0:T(8,128)(2,1)}, bf16[1,120,240]{2,1,0:T(8,128)(2,1)}, u32[]{:S(2)}, u32[]{:S(2)}) collective-permute-start(bf16[1,120,240]{2,1,0:T(8,128)(2,1)} %bitcast.32), channel_id=1, source_target_pairs={{0,4},{1,5},{2,6},{3,7},{4,0},{5,1},{6,2},{7,3},{8,12},{9,13},{10,... | collective-permute-start | bytes 172808 | tf_op jit(solution)/shard_map/ppermute | solution.py:35
  11.9 31.6 %collective-permute-start = (bf16[1,208,240]{2,1,0:T(8,128)(2,1)}, bf16[1,208,240]{2,1,0:T(8,128)(2,1)}, u32[]{:S(2)}, u32[]{:S(2)}) collective-permute-start(bf16[1,208,240]{2,1,0:T(8,128)(2,1)} %bitcast.7), channel_id=1, source_target_pairs={{0,4},{1,5},{2,6},{3,7},{4,0},{5,1},{6,2},{7,3},{8,12},{9,13},{10,... | collective-permute-start | bytes 299528 | tf_op jit(solution)/shard_map/ppermute | solution.py:35
  11.9 46.6 %collective-permute-start.23 = (bf16[1,120,640]{2,1,0:T(8,128)(2,1)}, bf16[1,120,640]{2,1,0:T(8,128)(2,1)}, u32[]{:S(2)}, u32[]{:S(2)}) collective-permute-start(bf16[1,120,640]{2,1,0:T(8,128)(2,1)} %bitcast.377), channel_id=1, source_target_pairs={{0,4},{1,5},{2,6},{3,7},{4,0},{5,1},{6,2},{7,3},{8,12},{9,13},{10,... | collective-permute-start | bytes 460808 | tf_op jit(solution)/shard_map/ppermute | solution.py:35
  17.1 22.4 %collective-permute-start.17 = (bf16[1,240,640]{2,1,0:T(8,128)(2,1)S(1)}, bf16[1,240,640]{2,1,0:T(8,128)(2,1)S(1)}, u32[]{:S(2)}, u32[]{:S(2)}) collective-permute-start(bf16[1,240,640]{2,1,0:T(8,128)(2,1)S(1)} %maximum_bitcast_fusion.2), channel_id=1, source_target_pairs={{0,4},{1,5},{2,6},{3,7},{4,0},{5,1},{6,2},{7,3},{8,12},{9,13},{10,... | collective-permute-start | bytes 921608 | tf_op jit(solution)/shard_map/ppermute | solution.py:35
  56.9 30.0 %collective-permute-start.19 = (bf16[4,240,640]{2,1,0:T(8,128)(2,1)S(1)}, bf16[4,240,640]{2,1,0:T(8,128)(2,1)S(1)}, u32[]{:S(2)}, u32[]{:S(2)}) collective-permute-start(bf16[4,240,640]{2,1,0:T(8,128)(2,1)S(1)} %bitcast.345), channel_id=1, source_target_pairs={{0,1},{1,0},{2,3},{3,2},{4,5},{5,4},{6,7},{7,6},{8,9},{9,8},{10,11... | collective-permute-start | bytes 3686408 | tf_op jit(solution)/shard_map/ppermute | solution.py:35
  63.0 52.1 %collective-permute-start.12 = (bf16[2,120,240]{2,1,0:T(8,128)(2,1)S(1)}, bf16[2,120,240]{2,1,0:T(8,128)(2,1)S(1)}, u32[]{:S(2)}, u32[]{:S(2)}) collective-permute-start(bf16[2,120,240]{2,1,0:T(8,128)(2,1)S(1)} %maximum_bitcast_fusion.5), channel_id=1, source_target_pairs={{0,2},{1,3},{2,0},{3,1},{4,6},{5,7},{6,4},{7,5},{8,10},{9,11},{10,... | collective-permute-start | bytes 345608 | tf_op jit(solution)/shard_map/ppermute | solution.py:35
  64.3 31.3 %collective-permute-start.2 = (bf16[4,208,240]{2,1,0:T(8,128)(2,1)S(1)}, bf16[4,208,240]{2,1,0:T(8,128)(2,1)S(1)}, u32[]{:S(2)}, u32[]{:S(2)}) collective-permute-start(bf16[4,208,240]{2,1,0:T(8,128)(2,1)S(1)} %bitcast.364), channel_id=1, source_target_pairs={{0,1},{1,0},{2,3},{3,2},{4,5},{5,4},{6,7},{7,6},{8,9},{9,8},{10,11... | collective-permute-start | bytes 1198088 | tf_op jit(solution)/shard_map/ppermute | solution.py:35
  69.1 31.0 %collective-permute-start.5 = (bf16[4,208,240]{2,1,0:T(8,128)(2,1)S(1)}, bf16[4,208,240]{2,1,0:T(8,128)(2,1)S(1)}, u32[]{:S(2)}, u32[]{:S(2)}) collective-permute-start(bf16[4,208,240]{2,1,0:T(8,128)(2,1)S(1)} %collective-permute-done.4), channel_id=1, source_target_pairs={{0,1},{1,0},{2,3},{3,2},{4,5},{5,4},{6,7},{7,6},{8,9},{9,8},{10,11... | collective-permute-start | bytes 1198088 | tf_op jit(solution)/shard_map/ppermute | solution.py:35
  89.3 60.2 %collective-permute-start.21 = (bf16[8,240,640]{2,1,0:T(8,128)(2,1)}, bf16[8,240,640]{2,1,0:T(8,128)(2,1)}, u32[]{:S(2)}, u32[]{:S(2)}) collective-permute-start(bf16[8,240,640]{2,1,0:T(8,128)(2,1)} %bitcast.64.refs_0_), channel_id=1, source_target_pairs={{0,16},{8,24},{16,0},{24,8},{1,17},{9,25},{17,1},{25,9},{2,18},{10... | collective-permute-start | bytes 7372808 | tf_op jit(solution)/shard_map/ppermute | solution.py:35
  101.5 46.5 %collective-permute-start.27 = (bf16[4,120,640]{2,1,0:T(8,128)(2,1)}, bf16[4,120,640]{2,1,0:T(8,128)(2,1)}, u32[]{:S(2)}, u32[]{:S(2)}) collective-permute-start(bf16[4,120,640]{2,1,0:T(8,128)(2,1)} %bitcast.74), channel_id=1, source_target_pairs={{0,16},{8,24},{16,0},{24,8},{1,17},{9,25},{17,1},{25,9},{2,18},{10... | collective-permute-start | bytes 1843208 | tf_op jit(solution)/shard_map/ppermute | solution.py:35
  115.1 35.1 %collective-permute-start.25 = (bf16[4,120,640]{2,1,0:T(8,128)(2,1)}, bf16[4,120,640]{2,1,0:T(8,128)(2,1)S(1)}, u32[]{:S(2)}, u32[]{:S(2)}) collective-permute-start(bf16[4,120,640]{2,1,0:T(8,128)(2,1)} %bitcast.74), channel_id=1, source_target_pairs={{0,1},{1,0},{2,3},{3,2},{4,5},{5,4},{6,7},{7,6},{8,9},{9,8},{10,11... | collective-permute-start | bytes 1843208 | tf_op jit(solution)/shard_map/ppermute | solution.py:35
  116.7 19.5 %collective-permute-start.13 = (bf16[4,120,240]{2,1,0:T(8,128)(2,1)S(1)}, bf16[4,120,240]{2,1,0:T(8,128)(2,1)S(1)}, u32[]{:S(2)}, u32[]{:S(2)}) collective-permute-start(bf16[4,120,240]{2,1,0:T(8,128)(2,1)S(1)} %bitcast.373), channel_id=1, source_target_pairs={{0,1},{1,0},{2,3},{3,2},{4,5},{5,4},{6,7},{7,6},{8,9},{9,8},{10,11... | collective-permute-start | bytes 691208 | tf_op jit(solution)/shard_map/ppermute | solution.py:35
  126.0 27.0 %collective-permute-start.9 = (bf16[656,384]{1,0:T(8,128)(2,1)S(1)}, bf16[656,384]{1,0:T(8,128)(2,1)S(1)}, u32[]{:S(2)}, u32[]{:S(2)}) collective-permute-start(bf16[656,384]{1,0:T(8,128)(2,1)S(1)} %collective-permute-done.7.refs_3_.refs_8_.refs_13_.refs_5_.refs_10_.refs_15_), channel_id=1, source_target_pairs={{0,2},{1,3},{2,4},{3,5},{4,6},{5,7},{8,10},{9,11},{10,12},{11,13},... | collective-permute-start | bytes 1511432 | tf_op jit(solution)/shard_map/ppermute | solution.py:98
  149.5 65.8 %collective-permute-start.20 = (bf16[8,240,640]{2,1,0:T(8,128)(2,1)}, bf16[8,240,640]{2,1,0:T(8,128)(2,1)}, u32[]{:S(2)}, u32[]{:S(2)}) collective-permute-start(bf16[8,240,640]{2,1,0:T(8,128)(2,1)} %bitcast.64.refs_0_), channel_id=1, source_target_pairs={{0,8},{8,0},{16,24},{24,16},{1,9},{9,1},{17,25},{25,17},{2,10},{10... | collective-permute-start | bytes 7372808 | tf_op jit(solution)/shard_map/ppermute | solution.py:35
  149.5 65.8 %collective-permute-start.22 = (bf16[8,240,640]{2,1,0:T(8,128)(2,1)}, bf16[8,240,640]{2,1,0:T(8,128)(2,1)}, u32[]{:S(2)}, u32[]{:S(2)}) collective-permute-start(bf16[8,240,640]{2,1,0:T(8,128)(2,1)} %collective-permute-done.21.refs_2_), channel_id=1, source_target_pairs={{0,8},{8,0},{16,24},{24,16},{1,9},{9,1},{17,25},{25,17},{2,10},{10... | collective-permute-start | bytes 7372808 | tf_op jit(solution)/shard_map/ppermute | solution.py:35
  167.5 47.8 %collective-permute-start.26 = (bf16[8,120,640]{2,1,0:T(8,128)(2,1)}, bf16[8,120,640]{2,1,0:T(8,128)(2,1)}, u32[]{:S(2)}, u32[]{:S(2)}) collective-permute-start(bf16[8,120,640]{2,1,0:T(8,128)(2,1)} %bitcast.78), channel_id=1, source_target_pairs={{0,8},{8,0},{16,24},{24,16},{1,9},{9,1},{17,25},{25,17},{2,10},{10... | collective-permute-start | bytes 3686408 | tf_op jit(solution)/shard_map/ppermute | solution.py:35
  174.3 41.0 %collective-permute-start.29 = (bf16[8,120,640]{2,1,0:T(8,128)(2,1)}, bf16[8,120,640]{2,1,0:T(8,128)(2,1)}, u32[]{:S(2)}, u32[]{:S(2)}) collective-permute-start(bf16[8,120,640]{2,1,0:T(8,128)(2,1)} %bitcast.83), channel_id=1, source_target_pairs={{0,8},{8,0},{16,24},{24,16},{1,9},{9,1},{17,25},{25,17},{2,10},{10... | collective-permute-start | bytes 3686408 | tf_op jit(solution)/shard_map/ppermute | solution.py:35
  180.6 21.1 %collective-permute-start.16 = (bf16[8,120,240]{2,1,0:T(8,128)(2,1)}, bf16[8,120,240]{2,1,0:T(8,128)(2,1)}, u32[]{:S(2)}, u32[]{:S(2)}) collective-permute-start(bf16[8,120,240]{2,1,0:T(8,128)(2,1)} %collective-permute-done.15), channel_id=1, source_target_pairs={{0,8},{8,0},{16,24},{24,16},{1,9},{9,1},{17,25},{25,17},{2,10},{10... | collective-permute-start | bytes 1382408 | tf_op jit(solution)/shard_map/ppermute | solution.py:35
  275.3 27.9 %collective-permute-start.47 = (bf16[8,120,240]{2,1,0:T(8,128)(2,1)S(1)}, bf16[8,120,240]{2,1,0:T(8,128)(2,1)S(1)}, u32[]{:S(2)}, u32[]{:S(2)}) collective-permute-start(bf16[8,120,240]{2,1,0:T(8,128)(2,1)S(1)} %bitcast.338), channel_id=1, source_target_pairs={{0,8},{8,0},{16,24},{24,16},{1,9},{9,1},{17,25},{25,17},{2,10},{10... | collective-permute-start | bytes 1382408 | tf_op jit(solution)/shard_map/ppermute | solution.py:35
  302.3 35.4 %collective-permute-start.58 = (bf16[8,120,640]{2,1,0:T(8,128)(2,1)}, bf16[8,120,640]{2,1,0:T(8,128)(2,1)}, u32[]{:S(2)}, u32[]{:S(2)}) collective-permute-start(bf16[8,120,640]{2,1,0:T(8,128)(2,1)} %bitcast.135), channel_id=1, source_target_pairs={{0,8},{8,0},{16,24},{24,16},{1,9},{9,1},{17,25},{25,17},{2,10},{10... | collective-permute-start | bytes 3686408 | tf_op jit(solution)/shard_map/ppermute | solution.py:35
  302.3 22.4 %collective-permute-start.30 = (bf16[2,320,384]{2,1,0:T(8,128)(2,1)}, bf16[2,320,384]{2,1,0:T(8,128)(2,1)S(1)}, u32[]{:S(2)}, u32[]{:S(2)}) collective-permute-start(bf16[2,320,384]{2,1,0:T(8,128)(2,1)} %get-tuple-element.56), channel_id=1, source_target_pairs={{0,1},{1,0},{2,3},{3,2},{4,5},{5,4},{6,7},{7,6},{8,9},{9,8},{10,11... | collective-permute-start | bytes 1474568 | tf_op jit(solution)/shard_map/ppermute | solution.py:35
  318.5 26.1 %collective-permute-start.60 = (bf16[8,120,640]{2,1,0:T(8,128)(2,1)}, bf16[8,120,640]{2,1,0:T(8,128)(2,1)S(1)}, u32[]{:S(2)}, u32[]{:S(2)}) collective-permute-start(bf16[8,120,640]{2,1,0:T(8,128)(2,1)} %bitcast.390), channel_id=1, source_target_pairs={{0,8},{8,0},{16,24},{24,16},{1,9},{9,1},{17,25},{25,17},{2,10},{10... | collective-permute-start | bytes 3686408 | tf_op jit(solution)/shard_map/ppermute | solution.py:35
  318.5 129.8 %collective-permute-start.52 = (bf16[8,240,640]{2,1,0:T(8,128)(2,1)}, bf16[8,240,640]{2,1,0:T(8,128)(2,1)}, u32[]{:S(2)}, u32[]{:S(2)}) collective-permute-start(bf16[8,240,640]{2,1,0:T(8,128)(2,1)} %get-tuple-element.70), channel_id=1, source_target_pairs={{0,8},{8,0},{16,24},{24,16},{1,9},{9,1},{17,25},{25,17},{2,10},{10... | collective-permute-start | bytes 7372808 | tf_op jit(solution)/shard_map/ppermute | solution.py:35
  324.7 50.2 %collective-permute-start.53 = (bf16[8,240,640]{2,1,0:T(8,128)(2,1)}, bf16[8,240,640]{2,1,0:T(8,128)(2,1)}, u32[]{:S(2)}, u32[]{:S(2)}) collective-permute-start(bf16[8,240,640]{2,1,0:T(8,128)(2,1)} %get-tuple-element.72), channel_id=1, source_target_pairs={{0,8},{8,0},{16,24},{24,16},{1,9},{9,1},{17,25},{25,17},{2,10},{10... | collective-permute-start | bytes 7372808 | tf_op jit(solution)/shard_map/ppermute | solution.py:35
  378.9 69.4 %collective-permute-start.54 = (bf16[8,240,640]{2,1,0:T(8,128)(2,1)}, bf16[8,240,640]{2,1,0:T(8,128)(2,1)}, u32[]{:S(2)}, u32[]{:S(2)}) collective-permute-start(bf16[8,240,640]{2,1,0:T(8,128)(2,1)} %add_convert_fusion.1), channel_id=1, source_target_pairs={{0,16},{8,24},{16,0},{24,8},{1,17},{9,25},{17,1},{25,9},{2,18},{10... | collective-permute-start | bytes 7372808 | tf_op jit(solution)/shard_map/ppermute | solution.py:35
  382.7 21.7 %collective-permute-start.61 = (bf16[4,120,640]{2,1,0:T(8,128)(2,1)}, bf16[4,120,640]{2,1,0:T(8,128)(2,1)}, u32[]{:S(2)}, u32[]{:S(2)}) collective-permute-start(bf16[4,120,640]{2,1,0:T(8,128)(2,1)} %dynamic-slice_bitcast_fusion.1), channel_id=1, source_target_pairs={{0,1},{1,0},{2,3},{3,2},{4,5},{5,4},{6,7},{7,6},{8,9},{9,8},{10,11... | collective-permute-start | bytes 1843208 | tf_op jit(solution)/shard_map/ppermute | solution.py:35
  387.0 19.8 %collective-permute-start.39 = (bf16[8,208,240]{2,1,0:T(8,128)(2,1)}, bf16[8,208,240]{2,1,0:T(8,128)(2,1)}, u32[]{:S(2)}, u32[]{:S(2)}) collective-permute-start(bf16[8,208,240]{2,1,0:T(8,128)(2,1)} %bitcast.337), channel_id=1, source_target_pairs={{0,8},{8,0},{16,24},{24,16},{1,9},{9,1},{17,25},{25,17},{2,10},{10... | collective-permute-start | bytes 2396168 | tf_op jit(solution)/shard_map/ppermute | solution.py:35
  406.7 41.3 %collective-permute-start.62 = (bf16[4,120,640]{2,1,0:T(8,128)(2,1)S(1)}, bf16[4,120,640]{2,1,0:T(8,128)(2,1)S(1)}, u32[]{:S(2)}, u32[]{:S(2)}) collective-permute-start(bf16[4,120,640]{2,1,0:T(8,128)(2,1)S(1)} %fusion.13), channel_id=1, source_target_pairs={{0,16},{8,24},{16,0},{24,8},{1,17},{9,25},{17,1},{25,9},{2,18},{10... | collective-permute-start | bytes 1843208 | tf_op jit(solution)/shard_map/ppermute | solution.py:35
  409.5 54.2 %collective-permute-start.40 = (bf16[4,208,240]{2,1,0:T(8,128)(2,1)S(1)}, bf16[4,208,240]{2,1,0:T(8,128)(2,1)S(1)}, u32[]{:S(2)}, u32[]{:S(2)}) collective-permute-start(bf16[4,208,240]{2,1,0:T(8,128)(2,1)S(1)} %dynamic-slice_bitcast_fusion.5), channel_id=1, source_target_pairs={{0,1},{1,0},{2,3},{3,2},{4,5},{5,4},{6,7},{7,6},{8,9},{9,8},{10,11... | collective-permute-start | bytes 1198088 | tf_op jit(solution)/shard_map/ppermute | solution.py:35
  421.3 31.6 %collective-permute-start.42 = (bf16[4,208,240]{2,1,0:T(8,128)(2,1)S(1)}, bf16[4,208,240]{2,1,0:T(8,128)(2,1)S(1)}, u32[]{:S(2)}, u32[]{:S(2)}) collective-permute-start(bf16[4,208,240]{2,1,0:T(8,128)(2,1)S(1)} %dynamic-slice_bitcast_fusion.4), channel_id=1, source_target_pairs={{0,1},{1,0},{2,3},{3,2},{4,5},{5,4},{6,7},{7,6},{8,9},{9,8},{10,11... | collective-permute-start | bytes 1198088 | tf_op jit(solution)/shard_map/ppermute | solution.py:35
  451.8 28.7 %collective-permute-start.55 = (bf16[4,240,640]{2,1,0:T(8,128)(2,1)S(1)}, bf16[4,240,640]{2,1,0:T(8,128)(2,1)S(1)}, u32[]{:S(2)}, u32[]{:S(2)}) collective-permute-start(bf16[4,240,640]{2,1,0:T(8,128)(2,1)S(1)} %dynamic-slice_bitcast_fusion), channel_id=1, source_target_pairs={{0,1},{1,0},{2,3},{3,2},{4,5},{5,4},{6,7},{7,6},{8,9},{9,8},{10,11... | collective-permute-start | bytes 3686408 | tf_op jit(solution)/shard_map/ppermute | solution.py:35
  461.5 21.4 %collective-permute-start.64 = (bf16[1,120,640]{2,1,0:T(8,128)(2,1)S(1)}, bf16[1,120,640]{2,1,0:T(8,128)(2,1)S(1)}, u32[]{:S(2)}, u32[]{:S(2)}) collective-permute-start(bf16[1,120,640]{2,1,0:T(8,128)(2,1)S(1)} %constant_dynamic-slice_fusion.1), channel_id=1, source_target_pairs={{0,4},{1,5},{2,6},{3,7},{4,0},{5,1},{6,2},{7,3},{8,12},{9,13},{10,... | collective-permute-start | bytes 460808 | tf_op jit(solution)/shard_map/ppermute | solution.py:35
  (75 other events, 738.9 us)

commit v3 on v2

v3 whole, which is shorter than its diff:
```python
import functools
import math

import jax
import jax.numpy as jnp
from jax import lax
from jax.experimental import pallas as pl
from jax.experimental.pallas import tpu as pltpu
from jax.sharding import PartitionSpec as P

QUERY_HEADS = 15
KEY_VALUE_HEADS = 5
HEAD_DIM = 64
GROUP = QUERY_HEADS // KEY_VALUE_HEADS
HALF = HEAD_DIM // 2

epsilon = 1e-05
rope_base = 10000.0
masked = -1e30
f32 = jnp.float32
b16 = jnp.bfloat16


def bits_of(axis, size):
    masks = []
    mask = size // 2
    while mask:
        masks.append((axis, mask))
        mask //= 2
    return masks


def swap(values, axis, mask):
    size = lax.axis_size(axis)
    return lax.ppermute(values, axis, [(i, i ^ mask) for i in range(size)])


def bit(axis, mask):
    return (lax.axis_index(axis) // mask) % 2


def after(values, *others):
    return lax.optimization_barrier((values, *others))[0]


def higher(order, mask):
    return 2 ** sum(1 for axis, m in order if axis == "ctx" and m > mask)


class Gather:
    def __init__(self, block, order):
        self.bufs = {0: block[None]}
        self.order = order
        self.done = 0

    def step(self, *others):
        axis, mask = self.order[self.done]
        sent = {r: after(b, *others) if others else b for r, b in self.bufs.items()}
        got = {r: swap(b, axis, mask) for r, b in sent.items()}
        if axis == "dp":
            self.bufs = {**self.bufs, **{r ^ mask: b for r, b in got.items()}}
        else:
            upper = bit(axis, mask) == 1
            pre = higher(self.order[: self.done], mask)
            for r, theirs in got.items():
                mine = self.bufs[r]
                shape = (pre, 1, mine.shape[0] // pre) + mine.shape[1:]
                mine, theirs = mine.reshape(shape), theirs.reshape(shape)
                both = jnp.concatenate(
                    [jnp.where(upper, theirs, mine), jnp.where(upper, mine, theirs)], axis=1
                )
                self.bufs[r] = both.reshape((-1,) + shape[3:])
        self.done += 1
        return list(got.values())

    def result(self):
        return [self.bufs[r] for r in sorted(self.bufs)]


class Scatter:
    def __init__(self, bufs, order):
        self.bufs = dict(enumerate(bufs))
        self.order = order
        self.done = 0

    def step(self, *others, pieces=1, hold=()):
        axis, mask = self.order[self.done]
        rest = self.order[self.done + 1 :]
        if axis == "dp":
            keep = {r: b for r, b in self.bufs.items() if not r & mask}
            send = {r: self.bufs[r ^ mask] for r in keep}
        else:
            own = bit(axis, mask)
            pre = higher(rest, mask)
            keep, send = {}, {}
            for r, b in self.bufs.items():
                parts = b.reshape((pre, 2, b.shape[0] // (2 * pre)) + b.shape[1:])
                send[r], keep[r] = (
                    lax.dynamic_index_in_dim(parts, i, 1, keepdims=False).reshape(
                        (-1,) + b.shape[1:]
                    )
                    for i in (1 - own, own)
                )
        got = {}
        first = []
        for r, b in send.items():
            b = after(b, *others) if others else b
            if pieces == 1:
                got[r] = swap(b, axis, mask)
                first.append(got[r])
                continue
            half = b.shape[0] // 2
            lower = swap(b[:half], axis, mask)
            upper = swap(after(b[half:], lower), axis, mask)
            got[r] = jnp.concatenate([lower, upper])
            first.append(lower)
        self.bufs = {}
        for r in keep:
            other = after(got[r], *hold) if hold else got[r]
            total = keep[r].astype(f32) + other.astype(f32)
            self.bufs[r] = total.astype(b16) if rest else total
        self.done += 1
        return first

    def finish(self):
        while self.done < len(self.order):
            self.step()
        return self.bufs[0][0]


def shift_outer(values, by):
    size = lax.axis_size("ctx")
    return lax.ppermute(
        values, "ctx", [(i, i + 2 * by) for i in range(size) if 0 <= i + 2 * by < size]
    )


def dot(a, b, dims):
    return lax.dot_general(a, b, (dims, ((), ())), preferred_element_type=f32)


def fill_bias(blocks, tokens, place, seg_refs, bias):
    queries = jnp.broadcast_to(seg_refs[0][0:1, :].astype(f32), (tokens, tokens))
    for j in range(blocks):
        keys = jnp.broadcast_to(seg_refs[j][0:1, :].astype(f32), (tokens, tokens)).T
        allowed = (keys == queries) & (place >= j)
        if j == 0:
            key_row = lax.broadcasted_iota(jnp.int32, (tokens, tokens), 0)
            query_col = lax.broadcasted_iota(jnp.int32, (tokens, tokens), 1)
            allowed = allowed & (key_row <= query_col)
        bias[j * tokens : (j + 1) * tokens, :] = jnp.where(allowed, 0.0, masked)


def heads_side(ref):
    return jnp.concatenate(
        [ref[h * HEAD_DIM : (h + 1) * HEAD_DIM, :] for h in range(GROUP)], axis=1
    )


def forward_kernel(blocks, tokens, place_ref, *refs):
    q_ref = refs[0]
    k_refs = refs[1 : 1 + blocks]
    v_refs = refs[1 + blocks : 1 + 2 * blocks]
    seg_refs = refs[1 + 2 * blocks : 1 + 3 * blocks]
    att_ref, lse_ref, bias = refs[1 + 3 * blocks :]

    @pl.when(pl.program_id(1) == 0)
    def _():
        fill_bias(blocks, tokens, place_ref[0], seg_refs, bias)

    keys = jnp.concatenate([r[...] for r in k_refs], axis=1)
    values = jnp.concatenate([r[...] for r in v_refs], axis=1)
    scores = dot(keys, heads_side(q_ref), ((0,), (0,)))
    for h in range(GROUP):
        own = scores[:, h * tokens : (h + 1) * tokens] + bias[...]
        top = jnp.max(own, axis=0, keepdims=True)
        probs = jnp.exp(own - top)
        total = jnp.sum(probs, axis=0, keepdims=True)
        out = dot(values, probs.astype(b16), ((1,), (0,)))
        att_ref[h * HEAD_DIM : (h + 1) * HEAD_DIM, :] = (out / total).astype(b16)
        lse_ref[0, h : h + 1, :] = top + jnp.log(total)


def backward_kernel(blocks, tokens, place_ref, *refs):
    q_ref, datt_ref, lse_ref = refs[:3]
    k_refs = refs[3 : 3 + blocks]
    v_refs = refs[3 + blocks : 3 + 2 * blocks]
    seg_refs = refs[3 + 2 * blocks : 3 + 3 * blocks]
    dq_ref = refs[3 + 3 * blocks]
    dkv_refs = refs[4 + 3 * blocks : 4 + 4 * blocks]
    bias, p_scr, ds_scr = refs[4 + 4 * blocks :]

    @pl.when(pl.program_id(1) == 0)
    def _():
        fill_bias(blocks, tokens, place_ref[0], seg_refs, bias)

    keys = jnp.concatenate([r[...] for r in k_refs], axis=1)
    values = jnp.concatenate([r[...] for r in v_refs], axis=1)
    queries = heads_side(q_ref)
    grads = heads_side(datt_ref)
    scores = dot(keys, queries, ((0,), (0,)))
    d_probs = dot(values, grads, ((0,), (0,)))
    for h in range(GROUP):
        lanes = slice(h * tokens, (h + 1) * tokens)
        probs = jnp.exp(scores[:, lanes] + bias[...] - lse_ref[0, h : h + 1, :])
        weighted = probs * d_probs[:, lanes]
        delta = jnp.sum(weighted, axis=0, keepdims=True)
        p_scr[:, lanes] = probs.astype(b16)
        ds_scr[:, lanes] = (weighted - probs * delta).astype(b16)
    d_scores = ds_scr[...]
    dq = dot(keys, d_scores, ((1,), (0,)))
    for h in range(GROUP):
        dq_ref[h * HEAD_DIM : (h + 1) * HEAD_DIM, :] = dq[:, h * tokens : (h + 1) * tokens]
    dk = dot(queries, d_scores, ((1,), (1,)))
    dv = dot(grads, p_scr[...], ((1,), (1,)))
    for j in range(blocks):
        lanes = slice(j * tokens, (j + 1) * tokens)
        dkv_refs[j][0] = dk[:, lanes].astype(b16)
        dkv_refs[j][1] = dv[:, lanes].astype(b16)


def kv_specs(blocks, tokens):
    per_group = (HEAD_DIM, tokens)
    key = pl.BlockSpec(per_group, lambda s, g, _: (g, s))
    value = pl.BlockSpec(per_group, lambda s, g, _: (KEY_VALUE_HEADS + g, s))
    seg_row = 2 * KEY_VALUE_HEADS * HEAD_DIM // 16
    seg = pl.BlockSpec((16, tokens), lambda s, g, _: (seg_row, s))
    return [key] * blocks + [value] * blocks + [seg] * blocks


def attend(place, q_rot, pieces, sequences, tokens):
    blocks = len(pieces)
    heads = pl.BlockSpec((GROUP * HEAD_DIM, tokens), lambda s, g, _: (g, s))
    stat = pl.BlockSpec((1, 8, tokens), lambda s, g, _: (g, 0, s))
    wide = sequences * tokens
    return pl.pallas_call(
        functools.partial(forward_kernel, blocks, tokens),
        grid_spec=pltpu.PrefetchScalarGridSpec(
            num_scalar_prefetch=1,
            grid=(sequences, KEY_VALUE_HEADS),
            in_specs=[heads] + kv_specs(blocks, tokens),
            out_specs=[heads, stat],
            scratch_shapes=[pltpu.VMEM((blocks * tokens, tokens), f32)],
        ),
        out_shape=[
            jax.ShapeDtypeStruct((QUERY_HEADS * HEAD_DIM, wide), b16),
            jax.ShapeDtypeStruct((KEY_VALUE_HEADS, 8, wide), f32),
        ],
        compiler_params=pltpu.CompilerParams(vmem_limit_bytes=40 << 20),
        cost_estimate=pl.CostEstimate(flops=1, bytes_accessed=1, transcendentals=0),
        name="attend",
    )(place, q_rot, *pieces, *pieces, *pieces)


def attend_back(place, q_rot, datt, lse, pieces, sequences, tokens):
    blocks = len(pieces)
    heads = pl.BlockSpec((GROUP * HEAD_DIM, tokens), lambda s, g, _: (g, s))
    stat = pl.BlockSpec((1, 8, tokens), lambda s, g, _: (g, 0, s))
    pair = pl.BlockSpec((2, HEAD_DIM, tokens), lambda s, g, _: (0, g, s))
    wide = sequences * tokens
    return pl.pallas_call(
        functools.partial(backward_kernel, blocks, tokens),
        grid_spec=pltpu.PrefetchScalarGridSpec(
            num_scalar_prefetch=1,
            grid=(sequences, KEY_VALUE_HEADS),
            in_specs=[heads, heads, stat] + kv_specs(blocks, tokens),
            out_specs=[heads] + [pair] * blocks,
            scratch_shapes=[
                pltpu.VMEM((blocks * tokens, tokens), f32),
                pltpu.VMEM((blocks * tokens, GROUP * tokens), b16),
                pltpu.VMEM((blocks * tokens, GROUP * tokens), b16),
            ],
        ),
        out_shape=[jax.ShapeDtypeStruct((QUERY_HEADS * HEAD_DIM, wide), f32)]
        + [jax.ShapeDtypeStruct((2, KEY_VALUE_HEADS * HEAD_DIM, wide), b16)] * blocks,
        compiler_params=pltpu.CompilerParams(vmem_limit_bytes=48 << 20),
        cost_estimate=pl.CostEstimate(flops=1, bytes_accessed=1, transcendentals=0),
        name="attend_back",
    )(place, q_rot, datt, lse, *pieces, *pieces, *pieces)


def turned(low, high, cosine, sine, sign):
    return low * cosine - sign * high * sine, high * cosine + sign * low * sine


def turn_rows(source, target, heads, cosine, sine, sign, scale):
    for h in range(heads):
        at = h * HEAD_DIM
        low, high = source[at : at + HALF], source[at + HALF : at + HEAD_DIM]
        pair = turned(low, high, cosine, sine, sign)
        for i, half in enumerate(pair):
            rows = slice(at + i * HALF, at + (i + 1) * HALF)
            target[rows] = (half * scale).astype(target.dtype)


def project_kv_kernel(parts, kv_cols, ctx, *refs):
    x_ref, inv_ref, gain_ref = refs[:3]
    w_refs = refs[3 : 3 + parts]
    seg_ref, cos_ref, sin_ref, normed_ref, own_ref, blocks, flat = refs[3 + parts :]
    for r in range(parts):
        normed = (x_ref[r].astype(f32) * inv_ref[...] * gain_ref[r]).astype(b16)
        normed_ref[r] = normed
        part = dot(w_refs[r][...], normed, ((1,), (0,)))
        if r == 0:
            blocks[...] = part
        else:
            blocks[...] += part
    rows = blocks.shape[0] // ctx
    kv_width = KEY_VALUE_HEADS * HEAD_DIM
    for c in range(ctx):
        base, at = c * rows, c * kv_cols
        flat[at : at + kv_cols] = blocks[base : base + kv_cols]
        at += kv_width
        flat[at : at + kv_cols] = blocks[base + kv_cols : base + 2 * kv_cols]
    turn_rows(flat, own_ref, KEY_VALUE_HEADS, cos_ref[...], sin_ref[...], 1.0, 1.0)
    own_ref[kv_width : 2 * kv_width] = flat[kv_width : 2 * kv_width].astype(b16)
    own_ref[2 * kv_width : 2 * kv_width + 16] = seg_ref[...]


def project_q_kernel(parts, scale, normed_ref, cos_ref, sin_ref, *refs):
    w_refs = refs[:parts]
    q_ref, flat = refs[parts:]
    acc = dot(w_refs[0][...], normed_ref[0], ((1,), (0,)))
    for r in range(1, parts):
        acc = acc + dot(w_refs[r][...], normed_ref[r], ((1,), (0,)))
    flat[...] = acc
    turn_rows(flat, q_ref, QUERY_HEADS, cos_ref[...], sin_ref[...], 1.0, scale)


def project_q_back_kernel(parts, scale, dq_ref, normed_ref, cos_ref, sin_ref, *refs):
    w_refs = refs[:parts]
    dn_ref = refs[parts]
    g_refs = refs[1 + parts : 1 + 2 * parts]
    flat = refs[1 + 2 * parts]
    turn_rows(dq_ref, flat, QUERY_HEADS, cos_ref[...], sin_ref[...], -1.0, scale)
    for r in range(parts):
        g_refs[r][...] = dot(flat[...], normed_ref[r], ((1,), (1,))).astype(b16)
    for r in range(parts):
        dn_ref[r] = dot(w_refs[r][...], flat[...], ((0,), (0,)))


def project_kv_back_kernel(parts, kv_cols, ctx, me_ref, *refs):
    dkv_ref, cos_ref, sin_ref, normed_ref, dn_q_ref, x_ref, inv_ref, gain_ref, d_mid_ref = refs[:9]
    w_refs = refs[9 : 9 + parts]
    out_ref, g_gain_ref = refs[9 + parts : 11 + parts]
    g_refs = refs[11 + parts : 11 + 2 * parts]
    flat, blocks, d_x = refs[11 + 2 * parts :]
    kv_width = KEY_VALUE_HEADS * HEAD_DIM
    turn_rows(dkv_ref.at[0], flat, KEY_VALUE_HEADS, cos_ref[...], sin_ref[...], -1.0, 1.0)
    rows = blocks.shape[0] // ctx
    for c in range(ctx):
        base, at = c * rows, c * kv_cols
        blocks[base : base + kv_cols] = flat[at : at + kv_cols]
        blocks[base + kv_cols : base + 2 * kv_cols] = dkv_ref[1, at : at + kv_cols]
        blocks[base + 2 * kv_cols : base + rows] = jnp.zeros(
            (rows - 2 * kv_cols, blocks.shape[1]), f32
        )
    low = blocks[...].astype(b16)
    for r in range(parts):
        g_refs[r][...] = dot(low, normed_ref[r], ((1,), (1,))).astype(b16)
    inv = inv_ref[...]
    mean = jnp.zeros_like(inv)
    for r in range(parts):
        d_normed = dn_q_ref[r] + dot(w_refs[r][...], low, ((0,), (0,)))
        x = x_ref[r].astype(f32)
        g_gain_ref[r] = jnp.sum(d_normed * (x * inv), axis=1, keepdims=True)
        scaled = d_normed * gain_ref[r]
        d_x[r] = scaled
        mean = mean + jnp.sum(scaled * x, axis=0, keepdims=True)
    mean = mean / (parts * x_ref.shape[1]) * (inv * inv * inv)
    pieces = []
    for d in range(parts):
        r = me_ref[0] ^ d
        total = d_mid_ref[d] + inv * d_x[r] - x_ref[r].astype(f32) * mean
        pieces.append(total.T)
    out_ref[...] = jnp.concatenate(pieces, axis=1).astype(b16)


def mix_kernel(parts, me_ref, att_ref, x_ref, gain_ref, *refs):
    w_refs = refs[:parts]
    mid_ref, inv_ref, normed_ref, normed_t_ref = refs[parts:]
    mid = x_ref[...].astype(f32)
    for r in range(parts):
        mid = mid + dot(att_ref[me_ref[0] ^ r], w_refs[r][...], ((0,), (1,)))
    mid_ref[...] = mid
    inv = lax.rsqrt(jnp.mean(mid * mid, axis=-1, keepdims=True) + epsilon)
    inv_ref[...] = inv
    normed = mid * inv * gain_ref[...]
    rows = normed_ref.shape[2]
    for d in range(parts):
        part = normed[:, d * rows : (d + 1) * rows]
        normed_ref[me_ref[0] ^ d] = part.astype(b16)
        normed_t_ref[me_ref[0] ^ d] = part.T.astype(b16)


def mix_back_kernel(parts, me_ref, att_ref, cot_ref, mid_ref, inv_ref, gain_ref, dn_ref, *refs):
    w_refs = refs[:parts]
    datt_ref, d_mid_ref, g_gain_ref = refs[parts : 3 + parts]
    g_refs = refs[3 + parts : 3 + 2 * parts]
    flipped = refs[3 + 2 * parts]
    rows = dn_ref.shape[2]
    inv = inv_ref[...]
    mean = jnp.zeros_like(inv)
    for d in range(parts):
        lanes = slice(d * rows, (d + 1) * rows)
        d_normed = dn_ref[me_ref[0] ^ d]
        mid = mid_ref[:, lanes]
        g_gain_ref[d] = jnp.sum(d_normed * (mid * inv), axis=0, keepdims=True)
        mean = mean + jnp.sum(d_normed * gain_ref[:, lanes] * mid, axis=-1, keepdims=True)
    mean = mean / (parts * rows) * (inv * inv * inv)
    for d in range(parts):
        lanes = slice(d * rows, (d + 1) * rows)
        scaled = dn_ref[me_ref[0] ^ d] * gain_ref[:, lanes]
        d_mid = cot_ref[:, lanes].astype(f32) + inv * scaled - mid_ref[:, lanes] * mean
        d_mid = d_mid.T
        d_mid_ref[d] = d_mid
        flipped[lanes] = d_mid.astype(b16)
    for r in range(parts):
        at = me_ref[0] ^ r
        g_refs[r][...] = dot(flipped[...], att_ref[at], ((1,), (1,))).astype(b16)
        datt_ref[at] = dot(w_refs[r][...], flipped[...], ((0,), (0,))).astype(b16)


def ffn_kernel(parts, per, me_ref, n_ref, nt_ref, cot_ref, mid_ref, *refs):
    f_refs = [refs[:parts], refs[parts : 2 * parts]]
    d_refs = refs[2 * parts : 3 * parts]
    out_ref, dn_ref = refs[3 * parts : 3 * parts + 2]
    rest = refs[3 * parts + 2 :]
    gf_refs = [rest[:parts], rest[parts : 2 * parts]]
    gd_refs = rest[2 * parts : 3 * parts]
    acc, down, g_down, hidden, cot_t = rest[3 * parts :]
    step = pl.program_id(0)
    for r in range(parts):

        @pl.when(step == r)
        def _(r=r):
            down[...] = d_refs[r][...]

    @pl.when(step == 0)
    def _():
        acc[...] = jnp.zeros_like(acc)
        cot_t[...] = cot_ref[...].T
        dn_ref[...] = jnp.zeros_like(dn_ref)

    cut = f_refs[0][0].shape[2]
    ff = (cut + f_refs[1][0].shape[2]) // 2
    d_hidden = dot(cot_ref[...], down[...], ((1,), (0,)))
    for i in range(per):
        both = []
        for side in f_refs:
            part = dot(n_ref[0], side[0][i], ((1,), (0,)))
            for r in range(1, parts):
                part = part + dot(n_ref[r], side[r][i], ((1,), (0,)))
            both.append(part)
        both = jnp.concatenate(both, axis=1)
        gate, up = both[:, :ff], both[:, ff:]
        grad = d_hidden[:, i * ff : (i + 1) * ff]
        sigma = jax.nn.sigmoid(gate)
        silu = gate * sigma
        hidden[:, i * ff : (i + 1) * ff] = (silu * up).astype(b16)
        d_gate = grad * up * (sigma * (1.0 + gate * (1.0 - sigma)))
        d_both = jnp.concatenate([d_gate, grad * silu], axis=1).astype(b16)
        sides = (d_both[:, :cut], d_both[:, cut:])
        for r in range(parts):
            for side in range(2):
                grad = dot(nt_ref[r], sides[side], ((1,), (0,)))
                gf_refs[side][r][i] = grad.astype(b16)
            dn_ref[r] += dot(sides[0], f_refs[0][r][i], ((1,), (1,))) + dot(
                sides[1], f_refs[1][r][i], ((1,), (1,))
            )
    acc[...] += dot(hidden[...], down[...], ((1,), (1,)))
    g_down[...] = dot(cot_t[...], hidden[...], ((1,), (0,))).astype(b16)
    for r in range(parts):

        @pl.when(step == r)
        def _(r=r):
            gd_refs[r][...] = g_down[...]

    @pl.when(step == parts - 1)
    def _():
        out_ref[...] = (mid_ref[...] + acc[...]).astype(b16)


def ffn(me, n_rel, nt_rel, cot, mid, f_one, f_two, d_list):
    parts = len(f_one)
    ctx, rows, cut = f_one[0].shape
    wide = cut + f_two[0].shape[2]
    per = ctx // parts
    tokens, width = mid.shape
    down_shape = d_list[0].shape

    def whole(a):
        return pl.BlockSpec(a.shape, lambda i, me: (0,) * a.ndim, pipeline_mode=pl.Buffered(1))

    f_specs = [
        pl.BlockSpec((per, rows, n), lambda i, me: (me[0] ^ i, 0, 0))
        for n in [cut] * parts + [wide - cut] * parts
    ]
    out_shape = [
        jax.ShapeDtypeStruct((tokens, width), b16),
        jax.ShapeDtypeStruct((parts, tokens, rows), f32),
    ]
    out_shape += [jax.ShapeDtypeStruct(f.shape, b16) for f in f_one + f_two]
    out_shape += [jax.ShapeDtypeStruct(down_shape, b16)] * parts
    return pl.pallas_call(
        functools.partial(ffn_kernel, parts, per),
        grid_spec=pltpu.PrefetchScalarGridSpec(
            num_scalar_prefetch=1,
            grid=(parts,),
            in_specs=[whole(a) for a in (n_rel, nt_rel, cot, mid)]
            + f_specs
            + [whole(a) for a in d_list],
            out_specs=[whole(a) for a in out_shape[:2]]
            + f_specs
            + [whole(a) for a in d_list],
            scratch_shapes=[
                pltpu.VMEM((tokens, width), f32),
                pltpu.VMEM(down_shape, b16),
                pltpu.VMEM(down_shape, b16),
                pltpu.VMEM((tokens, per * wide // 2), b16),
                pltpu.VMEM((width, tokens), b16),
            ],
        ),
        out_shape=out_shape,
        compiler_params=pltpu.CompilerParams(vmem_limit_bytes=58 << 20),
        cost_estimate=pl.CostEstimate(flops=1, bytes_accessed=1, transcendentals=0),
        name="ffn",
    )(me, n_rel, nt_rel, cot, mid, *f_one, *f_two, *d_list)


def in_vmem(kernel, name, out_shape, scratch, *args, scalars=0):
    vmem = pl.BlockSpec(memory_space=pltpu.VMEM)
    smem = pl.BlockSpec(memory_space=pltpu.SMEM)
    return pl.pallas_call(
        kernel,
        in_specs=[smem] * scalars + [vmem] * (len(args) - scalars),
        out_specs=[vmem] * len(out_shape),
        out_shape=out_shape,
        scratch_shapes=scratch,
        compiler_params=pltpu.CompilerParams(vmem_limit_bytes=48 << 20),
        cost_estimate=pl.CostEstimate(flops=1, bytes_accessed=1, transcendentals=0),
        name=name,
    )(*args)


def per_device(
    inputs,
    gain_one,
    query_weight,
    key_weight,
    value_weight,
    output_weight,
    gain_two,
    gate_weight,
    up_weight,
    down_weight,
    segment_ids,
    cotangent,
):
    dp, ctx = lax.axis_size("dp"), lax.axis_size("ctx")
    sequences, tokens, width = inputs.shape
    total = sequences * tokens
    rows = query_weight.shape[0]
    q_cols, kv_cols = query_weight.shape[1], key_weight.shape[1]
    ff_cols = gate_weight.shape[1]
    down_rows, out_cols = down_weight.shape
    kv_width = KEY_VALUE_HEADS * HEAD_DIM
    shape_of = jax.ShapeDtypeStruct

    dp_bits, ctx_bits = bits_of("dp", dp), bits_of("ctx", ctx)
    x_last = ctx_bits + dp_bits
    y_last = ctx_bits[:-1] + dp_bits[:-1] + ctx_bits[-1:] + dp_bits[-1:]
    z_last = ctx_bits[:-2] + ctx_bits[-1:] + dp_bits[:-1] + ctx_bits[-2:-1] + dp_bits[-1:]

    place = lax.axis_index("ctx")
    me = lax.axis_index("dp")
    me_arg = me.reshape(1).astype(jnp.int32)
    place_arg = place.reshape(1).astype(jnp.int32)

    def relative(stacked):
        return jnp.stack(
            [lax.dynamic_index_in_dim(stacked, me ^ r, 0, keepdims=False) for r in range(dp)]
        )

    gains = jnp.concatenate([gain_one, gain_two])
    gain_rows = -(-gains.size // rows)
    gains = jnp.pad(gains, (0, gain_rows * rows - gains.size)).reshape(gain_rows, rows)
    pad_rows = -(2 * kv_cols + gain_rows) % 8
    kv_block = jnp.concatenate(
        [key_weight.T, value_weight.T, gains, jnp.zeros((pad_rows, rows), b16)]
    )
    kv_gather = Gather(kv_block, y_last)
    qo_gather = Gather(jnp.concatenate([query_weight.T, output_weight.T]), x_last)
    gate_up = jnp.concatenate([gate_weight, up_weight], axis=1)
    cut = max(2 * ff_cols * 3 // 5 // 128, 1) * 128
    one_gather = Gather(gate_up[:, :cut], x_last)
    two_gather = Gather(gate_up[:, cut:], y_last)
    down_gather = Gather(down_weight.T, z_last)
    outer = len(ctx_bits) - 1
    token = kv_gather.step()
    one_gather.step(*token)
    two_gather.step(*token)
    token = kv_gather.step()
    down_gather.step(*token)
    qo_gather.step(*token)
    while kv_gather.done < len(x_last) - 1:
        token = kv_gather.step()
    for _ in range(outer - 1):
        two_gather.step(*token)
        down_gather.step(*token)
        one_gather.step(*token)
        qo_gather.step(*token)
    kv_gather.step()
    kv_all = kv_gather.result()

    first_gain = 2 * kv_cols
    gain_all = kv_all[0][:, first_gain : first_gain + gain_rows].reshape(ctx, -1)
    gain_part = gain_one.shape[0]
    gain_a = relative(gain_all[:, :gain_part].reshape(dp, rows, 1).astype(f32))
    gain_b = gain_all[:, gain_part : 2 * gain_part].reshape(1, width).astype(f32)
    kv_all = [a.reshape(-1, rows) for a in kv_all]

    cot = cotangent.reshape(total, width)
    x_low = inputs.reshape(total, width)
    x = x_low.astype(f32)
    inv_one = lax.rsqrt(jnp.mean(x * x, axis=-1) + epsilon).reshape(1, total)
    x_t = relative(x_low.T.reshape(dp, rows, total))
    positions = (place * tokens + jnp.arange(tokens, dtype=jnp.int32)).astype(f32)
    positions = jnp.tile(positions, sequences)
    frequency = jnp.exp(jnp.arange(HALF, dtype=f32) * (-2.0 * math.log(rope_base) / HEAD_DIM))
    angles = frequency[:, None] * positions[None, :]
    cosine, sine = jnp.cos(angles), jnp.sin(angles)
    score_scale = HEAD_DIM ** (-0.5)
    seg_row = jnp.pad(segment_ids.reshape(1, total).astype(b16), ((0, 15), (0, 0)))
    block_rows = kv_all[0].shape[0]
    one_t, own = in_vmem(
        functools.partial(project_kv_kernel, dp, kv_cols, ctx),
        "project_kv",
        [shape_of((dp, rows, total), b16), shape_of((2 * kv_width + 16, total), b16)],
        [pltpu.VMEM((block_rows, total), f32), pltpu.VMEM((2 * kv_width, total), f32)],
        x_t,
        inv_one,
        gain_a,
        *kv_all,
        seg_row,
        cosine,
        sine,
    )

    steps = ctx // 4
    inner = bit("ctx", 1)
    straight = [own]
    for _ in range(steps):
        straight.append(shift_outer(straight[-1], 1))
    crossed = [
        swap(jnp.where(inner == 0, straight[k], straight[k + 1]), "ctx", 1) for k in range(steps)
    ]
    while two_gather.done < len(x_last) - 2:
        spread = two_gather.step()
    while down_gather.done < len(x_last) - 2:
        spread += down_gather.step()
    while one_gather.done < outer + 1:
        one_gather.step()
    while qo_gather.done < outer + 1:
        qo_gather.step()
    ahead = qo_gather.step(*spread)
    while qo_gather.done < len(x_last):
        qo_gather.step()
    q_all = [a[:, :q_cols].reshape(-1, rows) for a in qo_gather.result()]
    out_all = [a[:, q_cols:].reshape(-1, rows) for a in qo_gather.result()]
    (q_rot,) = in_vmem(
        functools.partial(project_q_kernel, dp, score_scale),
        "project_q",
        [shape_of((width, total), b16)],
        [pltpu.VMEM((width, total), f32)],
        after(one_t, straight[1]),
        cosine,
        sine,
        *q_all,
    )
    one_gather.step(*ahead, straight[1])
    down_gather.step(straight[steps])
    two_gather.step(*crossed)
    pieces = []
    for k in range(steps):
        pieces += [straight[k], crossed[k]]
    pieces.append(straight[steps])

    att, lse = attend(place_arg, q_rot, pieces, sequences, tokens)
    for g in (one_gather, two_gather, down_gather):
        while g.done < len(x_last):
            g.step(lse)
    down_all = [a.reshape(-1, down_rows) for a in down_gather.result()]
    att_3 = att.reshape(dp, rows, total)

    mid, inv_two, two, two_t = in_vmem(
        functools.partial(mix_kernel, dp),
        "mix",
        [
            shape_of((total, width), f32),
            shape_of((total, 1), f32),
            shape_of((dp, total, rows), b16),
            shape_of((dp, rows, total), b16),
        ],
        [],
        me_arg,
        att_3,
        x_low,
        gain_b,
        *out_all,
        scalars=1,
    )
    output, d_two, *grads = ffn(me_arg, two, two_t, cot, mid, one_gather.result(), two_gather.result(), down_all)
    g_one = Scatter(grads[:dp], x_last[::-1])
    g_two = Scatter(grads[dp : 2 * dp], y_last[::-1])
    g_down = Scatter([g.reshape(ctx, out_cols, down_rows) for g in grads[2 * dp :]], z_last[::-1])
    d_att, d_mid, g_gain_two, *g_out = in_vmem(
        functools.partial(mix_back_kernel, dp),
        "mix_back",
        [
            shape_of(att_3.shape, b16),
            shape_of((dp, rows, total), f32),
            shape_of((dp, 1, rows), f32),
        ]
        + [shape_of((width, rows), b16)] * dp,
        [pltpu.VMEM((width, total), b16)],
        me_arg,
        att_3,
        cot,
        mid,
        inv_two,
        gain_b,
        d_two,
        *out_all,
        scalars=1,
    )
    folded = g_one.step(hold=(d_att,))
    folded += [t for g in (g_two, g_down) for t in g.step(hold=(d_att, *folded[:1]))]
    d_att = after(d_att.reshape(width, total), *folded)
    under_x, under_y, under_z = g_one.step(), g_two.step(), g_down.step()
    dq_rot, *parts = attend_back(place_arg, q_rot, d_att, lse, pieces, sequences, tokens)
    dq_rot = after(dq_rot, *under_x, *under_y, *under_z)
    parts = [after(p, *under_y) for p in parts]
    dn_q, *g_q = in_vmem(
        functools.partial(project_q_back_kernel, dp, score_scale),
        "project_q_back",
        [shape_of((dp, rows, total), f32)] + [shape_of((width, rows), b16)] * dp,
        [pltpu.VMEM((width, total), b16)],
        dq_rot,
        one_t,
        cosine,
        sine,
        *q_all,
    )

    returned = [swap(parts[2 * k + 1], "ctx", 1).astype(f32) for k in range(steps)]
    here = []
    for k in range(steps + 1):
        value = parts[2 * k].astype(f32)
        if k < steps:
            value = value + jnp.where(inner == 0, returned[k], 0.0)
        if k > 0:
            value = value + jnp.where(inner == 1, returned[k - 1], 0.0)
        here.append(value)
    carried = here[steps]
    for k in range(steps, 0, -1):
        moved = shift_outer(carried.astype(b16), -1)
        if k == steps:
            first_moved = moved
        carried = here[k - 1] + moved.astype(f32)
    g_qo = [
        jnp.concatenate([q.reshape(ctx, q_cols, rows), o.reshape(ctx, out_cols, rows)], axis=1)
        for q, o in zip(g_q, g_out, strict=True)
    ]
    g_qo = Scatter(g_qo, x_last[::-1])
    g_qo.step(parts[0])
    beside = g_two.step() + g_down.step() + g_one.step(*returned)
    beside += g_qo.step(*beside[:2])
    for g in (g_two, g_down, g_one):
        g.step(first_moved)
    while g_one.done < len(x_last):
        for g in (g_two, g_down, g_one):
            g.step(carried)

    carried = after(carried, *beside)
    input_grad, g_gain_one, *g_kv = in_vmem(
        functools.partial(project_kv_back_kernel, dp, kv_cols, ctx),
        "project_kv_back",
        [shape_of((total, width), b16), shape_of((dp, rows, 1), f32)]
        + [shape_of((block_rows, rows), b16)] * dp,
        [
            pltpu.VMEM((kv_width, total), f32),
            pltpu.VMEM((block_rows, total), f32),
            pltpu.VMEM((dp, rows, total), f32),
        ],
        me_arg,
        carried,
        cosine,
        sine,
        one_t,
        dn_q,
        x_t,
        inv_one,
        gain_a,
        d_mid,
        *kv_all,
        scalars=1,
    )
    g_gains = jnp.concatenate(
        [relative(g_gain_one).reshape(ctx, gain_part), g_gain_two.reshape(ctx, gain_part)], axis=1
    ).astype(b16)
    g_gains = jnp.pad(g_gains, ((0, 0), (0, gain_rows * rows - 2 * gain_part)))
    g_gains = jnp.pad(g_gains.reshape(ctx, gain_rows, rows), ((0, 0), (0, pad_rows), (0, 0)))
    g_kv = [
        jnp.concatenate([g.reshape(ctx, -1, rows)[:, :first_gain], g_gains], axis=1) for g in g_kv
    ]
    g_kv = Scatter(g_kv, x_last[::-1])
    token = g_kv.step()
    early = g_qo.step()
    while g_kv.done < len(x_last):
        token = g_kv.step(*token)
        if g_qo.done < min(g_kv.done, len(x_last)):
            g_qo.step(*token)
    g_kv, g_qo, g_down = g_kv.finish(), g_qo.finish(), g_down.finish()
    g_gu = jnp.concatenate([g_one.finish(), g_two.finish()], axis=1)
    g_gains = g_kv[first_gain : first_gain + gain_rows].reshape(-1)
    return (
        output.reshape(sequences, tokens, width),
        input_grad.reshape(sequences, tokens, width),
        g_gains[:gain_part],
        g_qo[:q_cols].T,
        g_kv[:kv_cols].T,
        g_kv[kv_cols : 2 * kv_cols].T,
        g_qo[q_cols:].T,
        g_gains[gain_part : 2 * gain_part],
        g_gu[:, :ff_cols],
        g_gu[:, ff_cols:],
        g_down.T,
    )


def solution(mesh):
    act = P("dp", "ctx", None)
    weight = P("dp", "ctx")
    gain = P("ctx")
    return jax.shard_map(
        per_device,
        mesh=mesh,
        in_specs=(
            act, gain, weight, weight, weight, weight, gain, weight, weight, weight, P("dp", "ctx"), act,
        ),
        out_specs=(
            act, act, gain, weight, weight, weight, weight, gain, weight, weight, weight,
        ),
        check_vma=False,
    )
```

time: 525 us -> 402 us (0.77)
  waiting for transfers between devices: 231 us -> 138 us
  other arithmetic: 51.5 us -> 34.4 us
  local copies, waits for them, and re-layouts: 62.7 us -> 45.8 us
    ppermute x61 -> x69, waiting for transfers between devices: 217 us -> 130 us  [swap(): return lax.ppermute(values, axis, [(i, i ^ mask) for i in range(size)])]
    transpose x7 -> x3, local copies, waits for them, and re-layouts: 12.8 us -> 1.03 us  [the longest x1 0.64 us: per_device(): g_kv[kv_cols:2 * kv_cols]]
    unnamed x98 -> x190, local copies, waits for them, and re-layouts: 23.9 us -> 32.8 us
    convert_element_type x21 -> x24, other arithmetic: 24.5 us -> 16.4 us  [the longest x22 15.9 us: step(): self.bufs[r] = total.astype(b16) if rest else total]
    concatenate x9 -> x11, local copies, waits for them, and re-layouts: 10.1 us -> 3.88 us  [the longest x7 3.63 us: step(): jnp.concatenate([jnp.where(upper, theirs, mine), jnp.where(upper, mine, t...]
    ppermute x4, waiting for transfers between devices: 13.8 us -> 7.77 us  [shift_outer(): lax.ppermute(values, 'ctx', [(i, i + 2 * by) for i in range(size) if 0 <=...]
    dynamic_slice x4 -> x2, local copies, waits for them, and re-layouts: 5.73 us -> 0.12 us  [relative(): lax.dynamic_index_in_dim(stacked, me ^ r, 0, keepdims=False)]
    pallas_call x4 -> x6, Pallas kernels: 17.6 us -> 22.8 us  [in_vmem(): pl.pallas_call(kernel, in_specs=[smem] * scalars + [vmem] * (len(args) -...]
  transfers between devices with their start and end apart: 65 -> 73, of which waited for: 30 -> 25; matrix products, arithmetic and copies ran while one was open for 17% -> 14% of each run, Pallas kernels for 10% -> 16%
where the time goes in v3:
time: 402 us; the launch traced here: 396 us
  waiting for transfers between devices  138 us (34%)
  Pallas kernels  100 us (25%)
  starting transfers between devices  74.9 us (19%)
  local copies, waits for them, and re-layouts  45.8 us (11%)
  other arithmetic  34.4 us (9%)
    ppermute x69, waiting for transfers between devices, swap(): return lax.ppermute(values, axis, [(i, i ^ mask) for i in range(size)])  130 us
    ppermute x69, starting transfers between devices, swap(): return lax.ppermute(values, axis, [(i, i ^ mask) for i in range(size)])  65.6 us
    pallas_call x1, Pallas kernels, ffn(): pl.pallas_call(functools.partial(ffn_kernel, parts, per), grid_spec=pltpu...  38.8 us
    unnamed x190, local copies, waits for them, and re-layouts  32.8 us
    pallas_call x1, Pallas kernels, attend_back(): pl.pallas_call(functools.partial(backward_kernel, blocks, tokens), grid_s...  23.5 us
    pallas_call x6, Pallas kernels, in_vmem(): pl.pallas_call(kernel, in_specs=[smem] * scalars + [vmem] * (len(args) -...  22.8 us
    convert_element_type x22, other arithmetic, step(): self.bufs[r] = total.astype(b16) if rest else total  15.9 us
    pallas_call x1, Pallas kernels, attend(): pl.pallas_call(functools.partial(forward_kernel, blocks, tokens), grid_sp...  15.1 us
  transfers between devices with their start and end apart: 73, of which 25 were waited for; matrix products, arithmetic and copies ran while one was open for 14% of the time, Pallas kernels for 16%

profile of v3, /device:TPU:0, one launch (start us, length us, event | category | flops | bytes accessed | tf_op | source)
XLA Modules:
  0.0 395.8 jit_solution(8315642822282626206)
XLA Ops:
  2.4 4.1 %collective-permute-start = (bf16[1,88,240]{2,1,0:T(8,128)(2,1)S(1)}, bf16[1,88,240]{2,1,0:T(8,128)(2,1)S(1)}, u32[]{:S(2)}, u32[]{:S(2)}) collective-permute-start(bf16[1,88,240]{2,1,0:T(8,128)(2,1)S(1)} %maximum_bitcast_fusion.6), channel_id=1, source_target_pairs={{0,4},{1,5},{2,6},{3,7},{4,0},{5,1},{6,2},{7,3},{8,12},{9,13},{10,... | collective-permute-start | bytes 126728 | tf_op jit(solution)/shard_map/ppermute | solution.py:35
  20.5 9.2 %collective-permute-done.12 = bf16[1,240,256]{2,1,0:T(8,128)(2,1)S(1)} collective-permute-done((bf16[1,240,256]{2,1,0:T(8,128)(2,1)S(1)}, bf16[1,240,256]{2,1,0:T(8,128)(2,1)S(1)}, u32[]{:S(2)}, u32[]{:S(2)}) %collective-permute-start.12) | collective-permute-done | bytes 122912 | tf_op jit(solution)/shard_map/ppermute | solution.py:35
  30.6 4.4 %collective-permute-done.23 = bf16[1,240,384]{2,1,0:T(8,128)(2,1)S(1)} collective-permute-done((bf16[1,240,384]{2,1,0:T(8,128)(2,1)S(1)}, bf16[1,240,384]{2,1,0:T(8,128)(2,1)S(1)}, u32[]{:S(2)}, u32[]{:S(2)}) %collective-permute-start.23) | collective-permute-done | bytes 184352 | tf_op jit(solution)/shard_map/ppermute | solution.py:35
  36.0 4.9 %collective-permute-done.8 = bf16[1,240,240]{2,1,0:T(8,128)(2,1)S(1)} collective-permute-done((bf16[1,240,240]{2,1,0:T(8,128)(2,1)S(1)}, bf16[1,240,240]{2,1,0:T(8,128)(2,1)S(1)}, u32[]{:S(2)}, u32[]{:S(2)}) %collective-permute-start.8) | collective-permute-done | bytes 115232 | tf_op jit(solution)/shard_map/ppermute | solution.py:35
  45.7 5.4 %collective-permute-done.5 = bf16[4,88,240]{2,1,0:T(8,128)(2,1)S(1)} collective-permute-done((bf16[4,88,240]{2,1,0:T(8,128)(2,1)}, bf16[4,88,240]{2,1,0:T(8,128)(2,1)S(1)}, u32[]{:S(2)}, u32[]{:S(2)}) %collective-permute-start.5) | collective-permute-done | bytes 168992 | tf_op jit(solution)/shard_map/ppermute | solution.py:35
  55.9 5.8 %collective-permute-done.9 = bf16[2,240,240]{2,1,0:T(8,128)(2,1)S(1)} collective-permute-done((bf16[2,240,240]{2,1,0:T(8,128)(2,1)}, bf16[2,240,240]{2,1,0:T(8,128)(2,1)S(1)}, u32[]{:S(2)}, u32[]{:S(2)}) %collective-permute-start.9) | collective-permute-done | bytes 230432 | tf_op jit(solution)/shard_map/ppermute | solution.py:35
  62.8 4.1 %collective-permute-done.13 = bf16[2,240,256]{2,1,0:T(8,128)(2,1)S(1)} collective-permute-done((bf16[2,240,256]{2,1,0:T(8,128)(2,1)}, bf16[2,240,256]{2,1,0:T(8,128)(2,1)S(1)}, u32[]{:S(2)}, u32[]{:S(2)}) %collective-permute-start.13) | collective-permute-done | bytes 245792 | tf_op jit(solution)/shard_map/ppermute | solution.py:35
  76.4 6.3 %collective-permute-done.7.refs_3_.refs_8_.refs_13_.refs_5_.refs_10_.refs_15_ = bf16[656,384]{1,0:T(8,128)(2,1)S(1)} collective-permute-done((bf16[656,384]{1,0:T(8,128)(2,1)S(1)}, bf16[656,384]{1,0:T(8,128)(2,1)S(1)}, u32[]{:S(2)}, u32[]{:S(2)}) %collective-permute-start.7) | collective-permute-done | bytes 503840 | tf_op jit(solution)/shard_map/ppermute | solution.py:133
  82.7 4.6 %collective-permute-start.21 = (bf16[656,384]{1,0:T(8,128)(2,1)S(1)}, bf16[656,384]{1,0:T(8,128)(2,1)S(1)}, u32[]{:S(2)}, u32[]{:S(2)}) collective-permute-start(bf16[656,384]{1,0:T(8,128)(2,1)S(1)} %collective-permute-done.7.refs_3_.refs_8_.refs_13_.refs_5_.refs_10_.refs_15_), channel_id=1, source_target_pairs={{0,2},{1,3},{2,4},{3,5},{4,6},{5,7},{8,10},{9,11},{10,12},{11,13},... | collective-permute-start | bytes 1511432 | tf_op jit(solution)/shard_map/ppermute | solution.py:133
  88.6 2.7 collective-permute-done.17
  97.1 2.5 collective-permute-start.33
  101.9 11.1 %collective-permute-done.18 = bf16[8,240,240]{2,1,0:T(8,128)(2,1)S(1)} collective-permute-done((bf16[8,240,240]{2,1,0:T(8,128)(2,1)S(1)}, bf16[8,240,240]{2,1,0:T(8,128)(2,1)S(1)}, u32[]{:S(2)}, u32[]{:S(2)}) %collective-permute-start.18) | collective-permute-done | bytes 921632 | tf_op jit(solution)/shard_map/ppermute | solution.py:35
  118.0 11.0 %collective-permute-done.31 = bf16[4,240,256]{2,1,0:T(8,128)(2,1)S(1)} collective-permute-done((bf16[4,240,256]{2,1,0:T(8,128)(2,1)S(1)}, bf16[4,240,256]{2,1,0:T(8,128)(2,1)S(1)}, u32[]{:S(2)}, u32[]{:S(2)}) %collective-permute-start.31) | collective-permute-done | bytes 491552 | tf_op jit(solution)/shard_map/ppermute | solution.py:35
  131.4 15.1 %attend.1 = (bf16[960,384]{1,0:T(8,128)(2,1)S(1)}, f32[5,8,384]{2,1,0:T(8,128)S(1)}) custom-call(s32[1]{0:T(128)} %bitcast.1.place_ref, bf16[960,384]{1,0:T(8,128)(2,1)S(1)} %project_q.1.refs_0_, bf16[656,384]{1,0:T(8,128)(2,1)S(1)} %get-tuple-element.109.refs_1_.refs_6_.refs_11_.refs_3_.refs_8_.refs_13_, ...), custom_call_target="tpu_custom_call" | custom-call | flops 1 | bytes 1 | tf_op jit(solution)/shard_map/attend/pallas_call | solution.py:236
  160.8 2.5 mix.1
  165.8 38.8 %ffn.1 = (bf16[384,960]{1,0:T(8,128)(2,1)}, f32[4,384,240]{2,1,0:T(8,128)}, bf16[8,240,384]{2,1,0:T(8,128)(2,1)}, bf16[8,240,384]{2,1,0:T(8,128)(2,1)}, bf16[8,2...) custom-call(s32[1]{0:T(128)} %bitcast.me_ref, ...), custom_call_target="tpu_custom_call" | custom-call | flops 1 | bytes 1 | tf_op jit(solution)/shard_map/ffn/pallas_call | solution.py:505
  210.0 7.8 %mix_back.1 = (bf16[4,240,384]{2,1,0:T(8,128)(2,1)S(1)}, f32[4,240,384]{2,1,0:T(8,128)}, f32[4,1,240]{2,1,0:T(1,128)S(1)}, bf16[960,240]{1,0:T(8,128)(2,1)S(1)},...) custom-call(s32[1]{0:T(128)} %bitcast.me_ref, ...), custom_call_target="tpu_custom_call" | custom-call | flops 1 | bytes 1 | tf_op jit(solution)/shard_map/mix_back/pallas_call | solution.py:534
  226.7 2.5 collective-permute-start.50
  239.6 23.5 %attend_back.1 = (f32[960,384]{1,0:T(8,128)}, bf16[2,320,384]{2,1,0:T(8,128)(2,1)S(1)}, bf16[2,320,384]{2,1,0:T(8,128)(2,1)S(1)}, bf16[2,320,384]{2,1,0:T(8,128)...) custom-call(s32[1]{0:T(128)} %bitcast.1.place_ref, bf16[960,384]{1,0:T(8,128)(2,1)S(1)} %copy-done.5, ...), custom_call_target="tpu_custom_call" | custom-call | flops 1 | bytes 1 | tf_op jit(solution)/shard_map/attend_back/pallas_call | solution.py:261
  267.8 9.5 %collective-permute-done.46 = bf16[2,320,384]{2,1,0:T(8,128)(2,1)S(1)} collective-permute-done((bf16[2,320,384]{2,1,0:T(8,128)(2,1)S(1)}, bf16[2,320,384]{2,1,0:T(8,128)(2,1)S(1)}, u32[]{:S(2)}, u32[]{:S(2)}) %collective-permute-start.46) | collective-permute-done | bytes 491552 | tf_op jit(solution)/shard_map/ppermute | solution.py:35
  278.7 5.9 %collective-permute-done.49 = bf16[4,240,256]{2,1,0:T(8,128)(2,1)S(1)} collective-permute-done((bf16[4,240,256]{2,1,0:T(8,128)(2,1)S(1)}, bf16[4,240,256]{2,1,0:T(8,128)(2,1)S(1)}, u32[]{:S(2)}, u32[]{:S(2)}) %collective-permute-start.49) | collective-permute-done | bytes 491552 | tf_op jit(solution)/shard_map/ppermute | solution.py:35
  287.1 8.8 %collective-permute-done.51 = bf16[4,120,640]{2,1,0:T(8,128)(2,1)S(1)} collective-permute-done((bf16[4,120,640]{2,1,0:T(8,128)(2,1)S(1)}, bf16[4,120,640]{2,1,0:T(8,128)(2,1)S(1)}, u32[]{:S(2)}, u32[]{:S(2)}) %collective-permute-start.51) | collective-permute-done | bytes 614432 | tf_op jit(solution)/shard_map/ppermute | solution.py:35
  298.5 2.7 collective-permute-start.69
  305.3 4.8 %project_q_back.1 = (f32[4,240,384]{2,1,0:T(8,128)}, bf16[960,240]{1,0:T(8,128)(2,1)S(1)}, bf16[960,240]{1,0:T(8,128)(2,1)S(1)}, bf16[960,240]{1,0:T(8,128)(2,1)S(1)}, bf16[960,240]{1,0:T(8,128)(2,1)S(1)}) custom-call(f32[960,384]{1,0:T(8,128)} %get-tuple-element.171.dq_ref, bf16[4,240,384]{2,1,0:T(8,128)(2,1)S(1)} %copy-done.1, f32[32,384]{1,0:T(8,128)S(1)} %copy-done.37, ...), custom_call_target="tpu_custom_call" | custom-call | flops 1 | bytes 1 | tf_op jit(solution)/shard_map/project_q_back/pallas_call | solution.py:534
  311.5 4.0 %collective-permute-done.69 = bf16[2,240,256]{2,1,0:T(8,128)(2,1)S(1)} collective-permute-done((bf16[2,240,256]{2,1,0:T(8,128)(2,1)S(1)}, bf16[2,240,256]{2,1,0:T(8,128)(2,1)S(1)}, u32[]{:S(2)}, u32[]{:S(2)}) %collective-permute-start.69) | collective-permute-done | bytes 245792 | tf_op jit(solution)/shard_map/ppermute | solution.py:35
  325.1 10.1 %collective-permute-done.67 = bf16[2,240,384]{2,1,0:T(8,128)(2,1)S(1)} collective-permute-done((bf16[2,240,384]{2,1,0:T(8,128)(2,1)S(1)}, bf16[2,240,384]{2,1,0:T(8,128)(2,1)S(1)}, u32[]{:S(2)}, u32[]{:S(2)}) %collective-permute-start.67) | collective-permute-done | bytes 368672 | tf_op jit(solution)/shard_map/ppermute | solution.py:35
  335.4 8.3 %collective-permute-done.56 = bf16[8,240,240]{2,1,0:T(8,128)(2,1)S(1)} collective-permute-done((bf16[8,240,240]{2,1,0:T(8,128)(2,1)S(1)}, bf16[8,240,240]{2,1,0:T(8,128)(2,1)S(1)}, u32[]{:S(2)}, u32[]{:S(2)}) %collective-permute-start.56) | collective-permute-done | bytes 921632 | tf_op jit(solution)/shard_map/ppermute | solution.py:35
  344.8 5.5 %project_kv_back.1 = (bf16[384,960]{1,0:T(8,128)(2,1)}, f32[4,240,1]{2,1,0:T(8,128)S(1)}, bf16[704,240]{1,0:T(8,128)(2,1)S(1)}, bf16[704,240]{1,0:T(8,128)(2,1)S...) custom-call(s32[1]{0:T(128)} %bitcast.me_ref, f32[2,320,384]{2,1,0:T(8,128)} %convert_add_fusion.8.refs_0_, ...), custom_call_target="tpu_custom_call" | custom-call | flops 1 | bytes 1 | tf_op jit(solution)/shard_map/project_kv_back/pallas_call | solution.py:534
  358.3 7.2 %collective-permute-done.59 = bf16[8,88,240]{2,1,0:T(8,128)(2,1)S(1)} collective-permute-done((bf16[8,88,240]{2,1,0:T(8,128)(2,1)S(1)}, bf16[8,88,240]{2,1,0:T(8,128)(2,1)S(1)}, u32[]{:S(2)}, u32[]{:S(2)}) %collective-permute-start.59) | collective-permute-done | bytes 337952 | tf_op jit(solution)/shard_map/ppermute | solution.py:35
  370.8 3.8 collective-permute-done.60
  381.9 2.6 collective-permute-done.62
  389.4 4.7 %collective-permute-done.66 = bf16[1,240,240]{2,1,0:T(8,128)(2,1)S(1)} collective-permute-done((bf16[1,240,240]{2,1,0:T(8,128)(2,1)S(1)}, bf16[1,240,240]{2,1,0:T(8,128)(2,1)S(1)}, u32[]{:S(2)}, u32[]{:S(2)}) %collective-permute-start.66) | collective-permute-done | bytes 115232 | tf_op jit(solution)/shard_map/ppermute | solution.py:35
  (456 shorter events, 149.1 us)
Async XLA Ops:
  13.7 21.3 %collective-permute-start.23 = (bf16[1,240,384]{2,1,0:T(8,128)(2,1)S(1)}, bf16[1,240,384]{2,1,0:T(8,128)(2,1)S(1)}, u32[]{:S(2)}, u32[]{:S(2)}) collective-permute-start(bf16[1,240,384]{2,1,0:T(8,128)(2,1)S(1)} %fusion.25), channel_id=1, source_target_pairs={{0,4},{1,5},{2,6},{3,7},{4,0},{5,1},{6,2},{7,3},{8,12},{9,13},{10,... | collective-permute-start | bytes 552968 | tf_op jit(solution)/shard_map/ppermute | solution.py:35
  16.9 27.0 %collective-permute-start.4 = (bf16[4,88,240]{2,1,0:T(8,128)(2,1)}, bf16[4,88,240]{2,1,0:T(8,128)(2,1)}, u32[]{:S(2)}, u32[]{:S(2)}) collective-permute-start(bf16[4,88,240]{2,1,0:T(8,128)(2,1)} %bitcast.16), channel_id=1, source_target_pairs={{0,16},{8,24},{16,0},{24,8},{1,17},{9,25},{17,1},{25,9},{2,18},{10... | collective-permute-start | bytes 506888 | tf_op jit(solution)/shard_map/ppermute | solution.py:35
  18.4 24.2 %collective-permute-start.2 = (bf16[4,88,240]{2,1,0:T(8,128)(2,1)}, bf16[4,88,240]{2,1,0:T(8,128)(2,1)S(1)}, u32[]{:S(2)}, u32[]{:S(2)}) collective-permute-start(bf16[4,88,240]{2,1,0:T(8,128)(2,1)} %bitcast.16), channel_id=1, source_target_pairs={{0,1},{1,0},{2,3},{3,2},{4,5},{5,4},{6,7},{7,6},{8,9},{9,8},{10,11... | collective-permute-start | bytes 506888 | tf_op jit(solution)/shard_map/ppermute | solution.py:35
  19.9 21.8 %collective-permute-start.15 = (bf16[1,120,640]{2,1,0:T(8,128)(2,1)S(1)}, bf16[1,120,640]{2,1,0:T(8,128)(2,1)S(1)}, u32[]{:S(2)}, u32[]{:S(2)}) collective-permute-start(bf16[1,120,640]{2,1,0:T(8,128)(2,1)S(1)} %bitcast.462), channel_id=1, source_target_pairs={{0,4},{1,5},{2,6},{3,7},{4,0},{5,1},{6,2},{7,3},{8,12},{9,13},{10,... | collective-permute-start | bytes 460808 | tf_op jit(solution)/shard_map/ppermute | solution.py:35
  43.7 25.7 %collective-permute-start.3 = (bf16[8,88,240]{2,1,0:T(8,128)(2,1)S(1)}, bf16[8,88,240]{2,1,0:T(8,128)(2,1)S(1)}, u32[]{:S(2)}, u32[]{:S(2)}) collective-permute-start(bf16[8,88,240]{2,1,0:T(8,128)(2,1)S(1)} %bitcast.386), channel_id=1, source_target_pairs={{0,8},{8,0},{16,24},{24,16},{1,9},{9,1},{17,25},{25,17},{2,10},{10... | collective-permute-start | bytes 1013768 | tf_op jit(solution)/shard_map/ppermute | solution.py:35
  67.0 20.3 %collective-permute-start.10 = (bf16[4,240,240]{2,1,0:T(8,128)(2,1)S(1)}, bf16[4,240,240]{2,1,0:T(8,128)(2,1)S(1)}, u32[]{:S(2)}, u32[]{:S(2)}) collective-permute-start(bf16[4,240,240]{2,1,0:T(8,128)(2,1)S(1)} %bitcast.442), channel_id=1, source_target_pairs={{0,1},{1,0},{2,3},{3,2},{4,5},{5,4},{6,7},{7,6},{8,9},{9,8},{10,11... | collective-permute-start | bytes 1382408 | tf_op jit(solution)/shard_map/ppermute | solution.py:35
  67.7 20.9 %collective-permute-start.14 = (bf16[4,240,256]{2,1,0:T(8,128)(2,1)S(1)}, bf16[4,240,256]{2,1,0:T(8,128)(2,1)S(1)}, u32[]{:S(2)}, u32[]{:S(2)}) collective-permute-start(bf16[4,240,256]{2,1,0:T(8,128)(2,1)S(1)} %bitcast.438), channel_id=1, source_target_pairs={{0,16},{8,24},{16,0},{24,8},{1,17},{9,25},{17,1},{25,9},{2,18},{10... | collective-permute-start | bytes 1474568 | tf_op jit(solution)/shard_map/ppermute | solution.py:35
  75.1 21.8 %collective-permute-start.25 = (bf16[4,240,384]{2,1,0:T(8,128)(2,1)S(1)}, bf16[4,240,384]{2,1,0:T(8,128)(2,1)S(1)}, u32[]{:S(2)}, u32[]{:S(2)}) collective-permute-start(bf16[4,240,384]{2,1,0:T(8,128)(2,1)S(1)} %bitcast.432), channel_id=1, source_target_pairs={{0,1},{1,0},{2,3},{3,2},{4,5},{5,4},{6,7},{7,6},{8,9},{9,8},{10,11... | collective-permute-start | bytes 2211848 | tf_op jit(solution)/shard_map/ppermute | solution.py:35
  91.3 21.7 %collective-permute-start.18 = (bf16[8,240,240]{2,1,0:T(8,128)(2,1)S(1)}, bf16[8,240,240]{2,1,0:T(8,128)(2,1)S(1)}, u32[]{:S(2)}, u32[]{:S(2)}) collective-permute-start(bf16[8,240,240]{2,1,0:T(8,128)(2,1)S(1)} %bitcast.425), channel_id=1, source_target_pairs={{0,16},{8,24},{16,0},{24,8},{1,17},{9,25},{17,1},{25,9},{2,18},{10... | collective-permute-start | bytes 2764808 | tf_op jit(solution)/shard_map/ppermute | solution.py:35
  94.8 20.1 %collective-permute-start.20 = (bf16[656,384]{1,0:T(8,128)(2,1)S(1)}, bf16[656,384]{1,0:T(8,128)(2,1)S(1)}, u32[]{:S(2)}, u32[]{:S(2)}) collective-permute-start(bf16[656,384]{1,0:T(8,128)(2,1)S(1)} %get-tuple-element.295), channel_id=1, source_target_pairs={{0,1},{1,0},{2,3},{3,2},{4,5},{5,4},{6,7},{7,6},{8,9},{9,8},{10,11... | collective-permute-start | bytes 1511432 | tf_op jit(solution)/shard_map/ppermute | solution.py:35
  95.4 19.5 %collective-permute-start.22 = (bf16[656,384]{1,0:T(8,128)(2,1)S(1)}, bf16[656,384]{1,0:T(8,128)(2,1)S(1)}, u32[]{:S(2)}, u32[]{:S(2)}) collective-permute-start(bf16[656,384]{1,0:T(8,128)(2,1)S(1)} %get-tuple-element.294), channel_id=1, source_target_pairs={{0,1},{1,0},{2,3},{3,2},{4,5},{5,4},{6,7},{7,6},{8,9},{9,8},{10,11... | collective-permute-start | bytes 1511432 | tf_op jit(solution)/shard_map/ppermute | solution.py:35
  97.1 19.5 %collective-permute-start.33 = (bf16[4,120,640]{2,1,0:T(8,128)(2,1)S(1)}, bf16[4,120,640]{2,1,0:T(8,128)(2,1)S(1)}, u32[]{:S(2)}, u32[]{:S(2)}) collective-permute-start(bf16[4,120,640]{2,1,0:T(8,128)(2,1)S(1)} %bitcast.454), channel_id=1, source_target_pairs={{0,2},{1,3},{2,0},{3,1},{4,6},{5,7},{6,4},{7,5},{8,10},{9,11},{10,... | collective-permute-start | bytes 1843208 | tf_op jit(solution)/shard_map/ppermute | solution.py:35
  101.1 46.9 %collective-permute-start.35 = (bf16[4,120,640]{2,1,0:T(8,128)(2,1)S(1)}, bf16[4,120,640]{2,1,0:T(8,128)(2,1)S(1)}, u32[]{:S(2)}, u32[]{:S(2)}) collective-permute-start(bf16[4,120,640]{2,1,0:T(8,128)(2,1)S(1)} %collective-permute-done.17), channel_id=1, source_target_pairs={{0,2},{1,3},{2,0},{3,1},{4,6},{5,7},{6,4},{7,5},{8,10},{9,11},{10,... | collective-permute-start | bytes 1843208 | tf_op jit(solution)/shard_map/ppermute | solution.py:35
  113.0 35.6 %collective-permute-start.27 = (bf16[8,240,384]{2,1,0:T(8,128)(2,1)}, bf16[8,240,384]{2,1,0:T(8,128)(2,1)}, u32[]{:S(2)}, u32[]{:S(2)}) collective-permute-start(bf16[8,240,384]{2,1,0:T(8,128)(2,1)} %bitcast.86.refs_0_), channel_id=1, source_target_pairs={{0,16},{8,24},{16,0},{24,8},{1,17},{9,25},{17,1},{25,9},{2,18},{10... | collective-permute-start | bytes 4423688 | tf_op jit(solution)/shard_map/ppermute | solution.py:35
  116.5 33.9 %collective-permute-start.29 = (bf16[4,240,256]{2,1,0:T(8,128)(2,1)S(1)}, bf16[4,240,256]{2,1,0:T(8,128)(2,1)S(1)}, u32[]{:S(2)}, u32[]{:S(2)}) collective-permute-start(bf16[4,240,256]{2,1,0:T(8,128)(2,1)S(1)} %bitcast.439), channel_id=1, source_target_pairs={{0,1},{1,0},{2,3},{3,2},{4,5},{5,4},{6,7},{7,6},{8,9},{9,8},{10,11... | collective-permute-start | bytes 1474568 | tf_op jit(solution)/shard_map/ppermute | solution.py:35
  204.7 19.9 %collective-permute-start.37 = (bf16[8,240,384]{2,1,0:T(8,128)(2,1)}, bf16[8,240,384]{2,1,0:T(8,128)(2,1)}, u32[]{:S(2)}, u32[]{:S(2)}) collective-permute-start(bf16[8,240,384]{2,1,0:T(8,128)(2,1)} %get-tuple-element.140), channel_id=1, source_target_pairs={{0,8},{8,0},{16,24},{24,16},{1,9},{9,1},{17,25},{25,17},{2,10},{10... | collective-permute-start | bytes 4423688 | tf_op jit(solution)/shard_map/ppermute | solution.py:35
  204.8 19.4 %collective-permute-start.42 = (bf16[8,120,640]{2,1,0:T(8,128)(2,1)}, bf16[8,120,640]{2,1,0:T(8,128)(2,1)}, u32[]{:S(2)}, u32[]{:S(2)}) collective-permute-start(bf16[8,120,640]{2,1,0:T(8,128)(2,1)} %bitcast.470), channel_id=1, source_target_pairs={{0,8},{8,0},{16,24},{24,16},{1,9},{9,1},{17,25},{25,17},{2,10},{10... | collective-permute-start | bytes 3686408 | tf_op jit(solution)/shard_map/ppermute | solution.py:35
  205.3 21.3 %collective-permute-start.41 = (bf16[8,120,640]{2,1,0:T(8,128)(2,1)}, bf16[8,120,640]{2,1,0:T(8,128)(2,1)}, u32[]{:S(2)}, u32[]{:S(2)}) collective-permute-start(bf16[8,120,640]{2,1,0:T(8,128)(2,1)} %bitcast.469), channel_id=1, source_target_pairs={{0,8},{8,0},{16,24},{24,16},{1,9},{9,1},{17,25},{25,17},{2,10},{10... | collective-permute-start | bytes 3686408 | tf_op jit(solution)/shard_map/ppermute | solution.py:35
  205.4 23.9 %collective-permute-start.40 = (bf16[8,240,256]{2,1,0:T(8,128)(2,1)}, bf16[8,240,256]{2,1,0:T(8,128)(2,1)}, u32[]{:S(2)}, u32[]{:S(2)}) collective-permute-start(bf16[8,240,256]{2,1,0:T(8,128)(2,1)} %get-tuple-element.143), channel_id=1, source_target_pairs={{0,8},{8,0},{16,24},{24,16},{1,9},{9,1},{17,25},{25,17},{2,10},{10... | collective-permute-start | bytes 2949128 | tf_op jit(solution)/shard_map/ppermute | solution.py:35
  205.8 25.4 %collective-permute-start.39 = (bf16[8,240,256]{2,1,0:T(8,128)(2,1)}, bf16[8,240,256]{2,1,0:T(8,128)(2,1)}, u32[]{:S(2)}, u32[]{:S(2)}) collective-permute-start(bf16[8,240,256]{2,1,0:T(8,128)(2,1)} %get-tuple-element.142), channel_id=1, source_target_pairs={{0,8},{8,0},{16,24},{24,16},{1,9},{9,1},{17,25},{25,17},{2,10},{10... | collective-permute-start | bytes 2949128 | tf_op jit(solution)/shard_map/ppermute | solution.py:35
  226.7 39.6 %collective-permute-start.50 = (bf16[4,120,640]{2,1,0:T(8,128)(2,1)S(1)}, bf16[4,120,640]{2,1,0:T(8,128)(2,1)S(1)}, u32[]{:S(2)}, u32[]{:S(2)}) collective-permute-start(bf16[4,120,640]{2,1,0:T(8,128)(2,1)S(1)} %bitcast.455), channel_id=1, source_target_pairs={{0,2},{1,3},{2,0},{3,1},{4,6},{5,7},{6,4},{7,5},{8,10},{9,11},{10,... | collective-permute-start | bytes 1843208 | tf_op jit(solution)/shard_map/ppermute | solution.py:35
  230.9 32.2 %collective-permute-start.44 = (bf16[4,240,256]{2,1,0:T(8,128)(2,1)S(1)}, bf16[4,240,256]{2,1,0:T(8,128)(2,1)}, u32[]{:S(2)}, u32[]{:S(2)}) collective-permute-start(bf16[4,240,256]{2,1,0:T(8,128)(2,1)S(1)} %dynamic-slice_bitcast_fusion.2), channel_id=1, source_target_pairs={{0,1},{1,0},{2,3},{3,2},{4,5},{5,4},{6,7},{7,6},{8,9},{9,8},{10,11... | collective-permute-start | bytes 1474568 | tf_op jit(solution)/shard_map/ppermute | solution.py:35
  233.6 29.5 %collective-permute-start.43 = (bf16[4,240,256]{2,1,0:T(8,128)(2,1)}, bf16[4,240,256]{2,1,0:T(8,128)(2,1)}, u32[]{:S(2)}, u32[]{:S(2)}) collective-permute-start(bf16[4,240,256]{2,1,0:T(8,128)(2,1)} %dynamic-slice_bitcast_fusion.3), channel_id=1, source_target_pairs={{0,1},{1,0},{2,3},{3,2},{4,5},{5,4},{6,7},{7,6},{8,9},{9,8},{10,11... | collective-permute-start | bytes 1474568 | tf_op jit(solution)/shard_map/ppermute | solution.py:35
  237.1 50.0 %collective-permute-start.54 = (bf16[4,120,640]{2,1,0:T(8,128)(2,1)S(1)}, bf16[4,120,640]{2,1,0:T(8,128)(2,1)S(1)}, u32[]{:S(2)}, u32[]{:S(2)}) collective-permute-start(bf16[4,120,640]{2,1,0:T(8,128)(2,1)S(1)} %bitcast.456), channel_id=1, source_target_pairs={{0,2},{1,3},{2,0},{3,1},{4,6},{5,7},{6,4},{7,5},{8,10},{9,11},{10,... | collective-permute-start | bytes 1843208 | tf_op jit(solution)/shard_map/ppermute | solution.py:35
  238.8 62.4 %collective-permute-start.52 = (bf16[8,240,384]{2,1,0:T(8,128)(2,1)S(1)}, bf16[8,240,384]{2,1,0:T(8,128)(2,1)S(1)}, u32[]{:S(2)}, u32[]{:S(2)}) collective-permute-start(bf16[8,240,384]{2,1,0:T(8,128)(2,1)S(1)} %add_convert_fusion.1), channel_id=1, source_target_pairs={{0,16},{8,24},{16,0},{24,8},{1,17},{9,25},{17,1},{25,9},{2,18},{10... | collective-permute-start | bytes 4423688 | tf_op jit(solution)/shard_map/ppermute | solution.py:35
  263.6 33.1 %collective-permute-start.45 = (bf16[2,320,384]{2,1,0:T(8,128)(2,1)S(1)}, bf16[2,320,384]{2,1,0:T(8,128)(2,1)S(1)}, u32[]{:S(2)}, u32[]{:S(2)}) collective-permute-start(bf16[2,320,384]{2,1,0:T(8,128)(2,1)S(1)} %get-tuple-element.154), channel_id=1, source_target_pairs={{0,1},{1,0},{2,3},{3,2},{4,5},{5,4},{6,7},{7,6},{8,9},{9,8},{10,11... | collective-permute-start | bytes 1474568 | tf_op jit(solution)/shard_map/ppermute | solution.py:35
  277.3 18.7 %collective-permute-start.51 = (bf16[4,120,640]{2,1,0:T(8,128)(2,1)S(1)}, bf16[4,120,640]{2,1,0:T(8,128)(2,1)S(1)}, u32[]{:S(2)}, u32[]{:S(2)}) collective-permute-start(bf16[4,120,640]{2,1,0:T(8,128)(2,1)S(1)} %fusion.4), channel_id=1, source_target_pairs={{0,16},{8,24},{16,0},{24,8},{1,17},{9,25},{17,1},{25,9},{2,18},{10... | collective-permute-start | bytes 1843208 | tf_op jit(solution)/shard_map/ppermute | solution.py:35
  296.3 26.7 %collective-permute-start.71 = (bf16[2,120,640]{2,1,0:T(8,128)(2,1)S(1)}, bf16[2,120,640]{2,1,0:T(8,128)(2,1)S(1)}, u32[]{:S(2)}, u32[]{:S(2)}) collective-permute-start(bf16[2,120,640]{2,1,0:T(8,128)(2,1)S(1)} %dynamic-slice_bitcast_fusion.5), channel_id=1, source_target_pairs={{0,1},{1,0},{2,3},{3,2},{4,5},{5,4},{6,7},{7,6},{8,9},{9,8},{10,11... | collective-permute-start | bytes 921608 | tf_op jit(solution)/shard_map/ppermute | solution.py:35
  297.0 18.5 %collective-permute-start.48 = (bf16[2,320,384]{2,1,0:T(8,128)(2,1)S(1)}, bf16[2,320,384]{2,1,0:T(8,128)(2,1)S(1)}, u32[]{:S(2)}, u32[]{:S(2)}) collective-permute-start(bf16[2,320,384]{2,1,0:T(8,128)(2,1)S(1)} %add_convert_fusion.10), channel_id=1, source_target_pairs={{2,0},{3,1},{4,2},{5,3},{6,4},{7,5},{10,8},{11,9},{12,10},{13,11},... | collective-permute-start | bytes 1474568 | tf_op jit(solution)/shard_map/ppermute | solution.py:133
  311.3 44.5 %collective-permute-start.63 = (bf16[8,240,240]{2,1,0:T(8,128)(2,1)}, bf16[8,240,240]{2,1,0:T(8,128)(2,1)}, u32[]{:S(2)}, u32[]{:S(2)}) collective-permute-start(bf16[8,240,240]{2,1,0:T(8,128)(2,1)} %pad_maximum_fusion.7), channel_id=1, source_target_pairs={{0,8},{8,0},{16,24},{24,16},{1,9},{9,1},{17,25},{25,17},{2,10},{10... | collective-permute-start | bytes 2764808 | tf_op jit(solution)/shard_map/ppermute | solution.py:35
  321.9 21.8 %collective-permute-start.56 = (bf16[8,240,240]{2,1,0:T(8,128)(2,1)S(1)}, bf16[8,240,240]{2,1,0:T(8,128)(2,1)S(1)}, u32[]{:S(2)}, u32[]{:S(2)}) collective-permute-start(bf16[8,240,240]{2,1,0:T(8,128)(2,1)S(1)} %add_convert_fusion.5), channel_id=1, source_target_pairs={{0,16},{8,24},{16,0},{24,8},{1,17},{9,25},{17,1},{25,9},{2,18},{10... | collective-permute-start | bytes 2764808 | tf_op jit(solution)/shard_map/ppermute | solution.py:35
  323.8 27.5 %collective-permute-start.72 = (bf16[1,120,640]{2,1,0:T(8,128)(2,1)}, bf16[1,120,640]{2,1,0:T(8,128)(2,1)}, u32[]{:S(2)}, u32[]{:S(2)}) collective-permute-start(bf16[1,120,640]{2,1,0:T(8,128)(2,1)} %constant_dynamic-slice_fusion), channel_id=1, source_target_pairs={{0,4},{1,5},{2,6},{3,7},{4,0},{5,1},{6,2},{7,3},{8,12},{9,13},{10,... | collective-permute-start | bytes 460808 | tf_op jit(solution)/shard_map/ppermute | solution.py:35
  (128 other events, 1383.3 us)

commit v4 on v3

--- a/solution.py
+++ b/solution.py
@@ -53,10 +53,12 @@
         self.order = order
         self.done = 0
 
-    def step(self, *others):
+    def step(self, *others, hold=()):
         axis, mask = self.order[self.done]
         sent = {r: after(b, *others) if others else b for r, b in self.bufs.items()}
         got = {r: swap(b, axis, mask) for r, b in sent.items()}
+        if hold:
+            got = {r: after(b, *hold) for r, b in got.items()}
         if axis == "dp":
             self.bufs = {**self.bufs, **{r ^ mask: b for r, b in got.items()}}
         else:
@@ -368,12 +370,13 @@
         d_x[r] = scaled
         mean = mean + jnp.sum(scaled * x, axis=0, keepdims=True)
     mean = mean / (parts * x_ref.shape[1]) * (inv * inv * inv)
-    pieces = []
+    features, tokens = x_ref.shape[1], out_ref.shape[2]
     for d in range(parts):
         r = me_ref[0] ^ d
         total = d_mid_ref[d] + inv * d_x[r] - x_ref[r].astype(f32) * mean
-        pieces.append(total.T)
-    out_ref[...] = jnp.concatenate(pieces, axis=1).astype(b16)
+        for s in range(out_ref.shape[0]):
+            lanes = slice(s * tokens, (s + 1) * tokens)
+            out_ref[s, d * features : (d + 1) * features] = total[:, lanes].astype(b16)
 
 
 def mix_kernel(parts, me_ref, att_ref, x_ref, gain_ref, *refs):
@@ -411,8 +414,9 @@
     for d in range(parts):
         lanes = slice(d * rows, (d + 1) * rows)
         scaled = dn_ref[me_ref[0] ^ d] * gain_ref[:, lanes]
-        d_mid = cot_ref[:, lanes].astype(f32) + inv * scaled - mid_ref[:, lanes] * mean
-        d_mid = d_mid.T
+        d_mid = (inv * scaled - mid_ref[:, lanes] * mean).T
+        cot = [cot_ref[s, lanes].astype(f32) for s in range(cot_ref.shape[0])]
+        d_mid = d_mid + jnp.concatenate(cot, axis=1)
         d_mid_ref[d] = d_mid
         flipped[lanes] = d_mid.astype(b16)
     for r in range(parts):
@@ -428,7 +432,7 @@
     rest = refs[3 * parts + 2 :]
     gf_refs = [rest[:parts], rest[parts : 2 * parts]]
     gd_refs = rest[2 * parts : 3 * parts]
-    acc, down, g_down, hidden, cot_t = rest[3 * parts :]
+    acc, down, g_down, hidden, cot_t, cot = rest[3 * parts :]
     step = pl.program_id(0)
     for r in range(parts):
 
@@ -439,12 +443,15 @@
     @pl.when(step == 0)
     def _():
         acc[...] = jnp.zeros_like(acc)
-        cot_t[...] = cot_ref[...].T
+        length = cot_ref.shape[2]
+        for s in range(cot_ref.shape[0]):
+            cot_t[:, s * length : (s + 1) * length] = cot_ref[s]
+            cot[s * length : (s + 1) * length, :] = cot_ref[s].T
         dn_ref[...] = jnp.zeros_like(dn_ref)
 
     cut = f_refs[0][0].shape[2]
     ff = (cut + f_refs[1][0].shape[2]) // 2
-    d_hidden = dot(cot_ref[...], down[...], ((1,), (0,)))
+    d_hidden = dot(cot[...], down[...], ((1,), (0,)))
     for i in range(per):
         both = []
         for side in f_refs:
@@ -478,7 +485,10 @@
 
     @pl.when(step == parts - 1)
     def _():
-        out_ref[...] = (mid_ref[...] + acc[...]).astype(b16)
+        length = out_ref.shape[2]
+        for s in range(out_ref.shape[0]):
+            part = slice(s * length, (s + 1) * length)
+            out_ref[s] = (mid_ref[part] + acc[part]).T.astype(b16)
 
 
 def ffn(me, n_rel, nt_rel, cot, mid, f_one, f_two, d_list):
@@ -497,7 +507,7 @@
         for n in [cut] * parts + [wide - cut] * parts
     ]
     out_shape = [
-        jax.ShapeDtypeStruct((tokens, width), b16),
+        jax.ShapeDtypeStruct(cot.shape, b16),
         jax.ShapeDtypeStruct((parts, tokens, rows), f32),
     ]
     out_shape += [jax.ShapeDtypeStruct(f.shape, b16) for f in f_one + f_two]
@@ -519,6 +529,7 @@
                 pltpu.VMEM(down_shape, b16),
                 pltpu.VMEM((tokens, per * wide // 2), b16),
                 pltpu.VMEM((width, tokens), b16),
+                pltpu.VMEM((tokens, width), b16),
             ],
         ),
         out_shape=out_shape,
@@ -620,7 +631,7 @@
     gain_b = gain_all[:, gain_part : 2 * gain_part].reshape(1, width).astype(f32)
     kv_all = [a.reshape(-1, rows) for a in kv_all]
 
-    cot = cotangent.reshape(total, width)
+    cot = jnp.transpose(cotangent, (0, 2, 1))
     x_low = inputs.reshape(total, width)
     x = x_low.astype(f32)
     inv_one = lax.rsqrt(jnp.mean(x * x, axis=-1) + epsilon).reshape(1, total)
@@ -762,7 +773,7 @@
         if k > 0:
             value = value + jnp.where(inner == 1, returned[k - 1], 0.0)
         here.append(value)
-    carried = here[steps]
+    carried = after(here[steps], *under_x, *under_z)
     for k in range(steps, 0, -1):
         moved = shift_outer(carried.astype(b16), -1)
         if k == steps:
@@ -774,19 +785,16 @@
     ]
     g_qo = Scatter(g_qo, x_last[::-1])
     g_qo.step(parts[0])
-    beside = g_two.step() + g_down.step() + g_one.step(*returned)
-    beside += g_qo.step(*beside[:2])
-    for g in (g_two, g_down, g_one):
+    beside = g_two.step(hold=(first_moved,)) + g_down.step(hold=(first_moved,))
+    beside += g_one.step(*returned)
+    ahead = g_qo.step(*beside[:2])
+    for g in (g_two, g_down):
         g.step(first_moved)
-    while g_one.done < len(x_last):
-        for g in (g_two, g_down, g_one):
-            g.step(carried)
-
     carried = after(carried, *beside)
     input_grad, g_gain_one, *g_kv = in_vmem(
         functools.partial(project_kv_back_kernel, dp, kv_cols, ctx),
         "project_kv_back",
-        [shape_of((total, width), b16), shape_of((dp, rows, 1), f32)]
+        [shape_of((sequences, width, tokens), b16), shape_of((dp, rows, 1), f32)]
         + [shape_of((block_rows, rows), b16)] * dp,
         [
             pltpu.VMEM((kv_width, total), f32),
@@ -815,8 +823,12 @@
         jnp.concatenate([g.reshape(ctx, -1, rows)[:, :first_gain], g_gains], axis=1) for g in g_kv
     ]
     g_kv = Scatter(g_kv, x_last[::-1])
-    token = g_kv.step()
-    early = g_qo.step()
+    g_one.step(first_moved, hold=(input_grad,))
+    token = g_kv.step(*ahead)
+    g_qo.step()
+    for g in (g_two, g_down, g_one):
+        while g.done < len(x_last):
+            g.step(hold=(input_grad,))
     while g_kv.done < len(x_last):
         token = g_kv.step(*token)
         if g_qo.done < min(g_kv.done, len(x_last)):
@@ -825,8 +837,8 @@
     g_gu = jnp.concatenate([g_one.finish(), g_two.finish()], axis=1)
     g_gains = g_kv[first_gain : first_gain + gain_rows].reshape(-1)
     return (
-        output.reshape(sequences, tokens, width),
-        input_grad.reshape(sequences, tokens, width),
+        jnp.transpose(output, (0, 2, 1)),
+        jnp.transpose(input_grad, (0, 2, 1)),
         g_gains[:gain_part],
         g_qo[:q_cols].T,
         g_kv[:kv_cols].T,

time: 402 us -> 390 us (0.970)
  waiting for transfers between devices: 138 us -> 125 us
  local copies, waits for them, and re-layouts: 45.8 us -> 39.4 us
  other arithmetic: 34.4 us -> 40.6 us
    ppermute x69, waiting for transfers between devices: 130 us -> 117 us  [swap(): return lax.ppermute(values, axis, [(i, i ^ mask) for i in range(size)])]
    unnamed x190 -> x191, local copies, waits for them, and re-layouts: 32.8 us -> 24.9 us
    convert_element_type x22, other arithmetic: 15.9 us -> 20.6 us  [step(): self.bufs[r] = total.astype(b16) if rest else total]
  transfers between devices with their start and end apart: 73 -> 73, of which waited for: 25 -> 25; matrix products, arithmetic and copies ran while one was open for 14% -> 15% of each run, Pallas kernels for 16% -> 16%
where the time goes in v4:
time: 390 us; the launch traced here: 384 us
  waiting for transfers between devices  125 us (32%)
  Pallas kernels  99.4 us (25%)
  starting transfers between devices  76.5 us (20%)
  other arithmetic  40.6 us (10%)
  local copies, waits for them, and re-layouts  39.4 us (10%)
    ppermute x69, waiting for transfers between devices, swap(): return lax.ppermute(values, axis, [(i, i ^ mask) for i in range(size)])  117 us
    ppermute x69, starting transfers between devices, swap(): return lax.ppermute(values, axis, [(i, i ^ mask) for i in range(size)])  66.8 us
    pallas_call x1, Pallas kernels, ffn(): pl.pallas_call(functools.partial(ffn_kernel, parts, per), grid_spec=pltpu...  38.7 us
    unnamed x191, local copies, waits for them, and re-layouts  24.9 us
    pallas_call x1, Pallas kernels, attend_back(): pl.pallas_call(functools.partial(backward_kernel, blocks, tokens), grid_s...  23.4 us
    pallas_call x6, Pallas kernels, in_vmem(): pl.pallas_call(kernel, in_specs=[smem] * scalars + [vmem] * (len(args) -...  22.2 us
    convert_element_type x22, other arithmetic, step(): self.bufs[r] = total.astype(b16) if rest else total  20.6 us
    pallas_call x1, Pallas kernels, attend(): pl.pallas_call(functools.partial(forward_kernel, blocks, tokens), grid_sp...  15.1 us
  transfers between devices with their start and end apart: 73, of which 25 were waited for; matrix products, arithmetic and copies ran while one was open for 15% of the time, Pallas kernels for 16%

profile of v4, /device:TPU:0, one launch (start us, length us, event | category | flops | bytes accessed | tf_op | source)
XLA Modules:
  0.0 383.9 jit_solution(15144548440577880132)
XLA Ops:
  2.4 4.1 %collective-permute-start = (bf16[1,88,240]{2,1,0:T(8,128)(2,1)S(1)}, bf16[1,88,240]{2,1,0:T(8,128)(2,1)S(1)}, u32[]{:S(2)}, u32[]{:S(2)}) collective-permute-start(bf16[1,88,240]{2,1,0:T(8,128)(2,1)S(1)} %maximum_bitcast_fusion.6), channel_id=1, source_target_pairs={{0,4},{1,5},{2,6},{3,7},{4,0},{5,1},{6,2},{7,3},{8,12},{9,13},{10,... | collective-permute-start | bytes 126728 | tf_op jit(solution)/shard_map/ppermute | solution.py:35
  13.7 2.4 collective-permute-start.23
  20.5 9.2 %collective-permute-done.12 = bf16[1,240,256]{2,1,0:T(8,128)(2,1)S(1)} collective-permute-done((bf16[1,240,256]{2,1,0:T(8,128)(2,1)S(1)}, bf16[1,240,256]{2,1,0:T(8,128)(2,1)S(1)}, u32[]{:S(2)}, u32[]{:S(2)}) %collective-permute-start.12) | collective-permute-done | bytes 122912 | tf_op jit(solution)/shard_map/ppermute | solution.py:35
  30.6 4.4 %collective-permute-done.23 = bf16[1,240,384]{2,1,0:T(8,128)(2,1)S(1)} collective-permute-done((bf16[1,240,384]{2,1,0:T(8,128)(2,1)S(1)}, bf16[1,240,384]{2,1,0:T(8,128)(2,1)S(1)}, u32[]{:S(2)}, u32[]{:S(2)}) %collective-permute-start.23) | collective-permute-done | bytes 184352 | tf_op jit(solution)/shard_map/ppermute | solution.py:35
  36.0 4.9 %collective-permute-done.8 = bf16[1,240,240]{2,1,0:T(8,128)(2,1)S(1)} collective-permute-done((bf16[1,240,240]{2,1,0:T(8,128)(2,1)S(1)}, bf16[1,240,240]{2,1,0:T(8,128)(2,1)S(1)}, u32[]{:S(2)}, u32[]{:S(2)}) %collective-permute-start.8) | collective-permute-done | bytes 115232 | tf_op jit(solution)/shard_map/ppermute | solution.py:35
  45.7 5.4 %collective-permute-done.5 = bf16[4,88,240]{2,1,0:T(8,128)(2,1)S(1)} collective-permute-done((bf16[4,88,240]{2,1,0:T(8,128)(2,1)}, bf16[4,88,240]{2,1,0:T(8,128)(2,1)S(1)}, u32[]{:S(2)}, u32[]{:S(2)}) %collective-permute-start.5) | collective-permute-done | bytes 168992 | tf_op jit(solution)/shard_map/ppermute | solution.py:35
  55.9 5.8 %collective-permute-done.9 = bf16[2,240,240]{2,1,0:T(8,128)(2,1)S(1)} collective-permute-done((bf16[2,240,240]{2,1,0:T(8,128)(2,1)}, bf16[2,240,240]{2,1,0:T(8,128)(2,1)S(1)}, u32[]{:S(2)}, u32[]{:S(2)}) %collective-permute-start.9) | collective-permute-done | bytes 230432 | tf_op jit(solution)/shard_map/ppermute | solution.py:35
  62.8 4.1 %collective-permute-done.13 = bf16[2,240,256]{2,1,0:T(8,128)(2,1)S(1)} collective-permute-done((bf16[2,240,256]{2,1,0:T(8,128)(2,1)}, bf16[2,240,256]{2,1,0:T(8,128)(2,1)S(1)}, u32[]{:S(2)}, u32[]{:S(2)}) %collective-permute-start.13) | collective-permute-done | bytes 245792 | tf_op jit(solution)/shard_map/ppermute | solution.py:35
  76.4 6.2 %collective-permute-done.7.refs_3_.refs_8_.refs_13_.refs_5_.refs_10_.refs_15_ = bf16[656,384]{1,0:T(8,128)(2,1)S(1)} collective-permute-done((bf16[656,384]{1,0:T(8,128)(2,1)S(1)}, bf16[656,384]{1,0:T(8,128)(2,1)S(1)}, u32[]{:S(2)}, u32[]{:S(2)}) %collective-permute-start.7) | collective-permute-done | bytes 503840 | tf_op jit(solution)/shard_map/ppermute | solution.py:135
  82.7 4.9 %collective-permute-start.21 = (bf16[656,384]{1,0:T(8,128)(2,1)S(1)}, bf16[656,384]{1,0:T(8,128)(2,1)S(1)}, u32[]{:S(2)}, u32[]{:S(2)}) collective-permute-start(bf16[656,384]{1,0:T(8,128)(2,1)S(1)} %collective-permute-done.7.refs_3_.refs_8_.refs_13_.refs_5_.refs_10_.refs_15_), channel_id=1, source_target_pairs={{0,2},{1,3},{2,4},{3,5},{4,6},{5,7},{8,10},{9,11},{10,12},{11,13},... | collective-permute-start | bytes 1511432 | tf_op jit(solution)/shard_map/ppermute | solution.py:135
  97.0 2.5 collective-permute-start.33
  101.9 11.2 %collective-permute-done.18 = bf16[8,240,240]{2,1,0:T(8,128)(2,1)S(1)} collective-permute-done((bf16[8,240,240]{2,1,0:T(8,128)(2,1)S(1)}, bf16[8,240,240]{2,1,0:T(8,128)(2,1)S(1)}, u32[]{:S(2)}, u32[]{:S(2)}) %collective-permute-start.18) | collective-permute-done | bytes 921632 | tf_op jit(solution)/shard_map/ppermute | solution.py:35
  117.8 11.1 %collective-permute-done.31 = bf16[4,240,256]{2,1,0:T(8,128)(2,1)S(1)} collective-permute-done((bf16[4,240,256]{2,1,0:T(8,128)(2,1)S(1)}, bf16[4,240,256]{2,1,0:T(8,128)(2,1)S(1)}, u32[]{:S(2)}, u32[]{:S(2)}) %collective-permute-start.31) | collective-permute-done | bytes 491552 | tf_op jit(solution)/shard_map/ppermute | solution.py:35
  131.3 15.1 %attend.1 = (bf16[960,384]{1,0:T(8,128)(2,1)S(1)}, f32[5,8,384]{2,1,0:T(8,128)S(1)}) custom-call(s32[1]{0:T(128)} %bitcast.1.place_ref, bf16[960,384]{1,0:T(8,128)(2,1)S(1)} %project_q.1.refs_0_, bf16[656,384]{1,0:T(8,128)(2,1)S(1)} %get-tuple-element.115.refs_1_.refs_6_.refs_11_.refs_3_.refs_8_.refs_13_, ...), custom_call_target="tpu_custom_call" | custom-call | flops 1 | bytes 1 | tf_op jit(solution)/shard_map/attend/pallas_call | solution.py:238
  158.0 2.5 mix.1
  163.0 38.7 %ffn.1 = (bf16[3,960,128]{2,1,0:T(8,128)(2,1)}, f32[4,384,240]{2,1,0:T(8,128)}, bf16[8,240,384]{2,1,0:T(8,128)(2,1)}, bf16[8,240,384]{2,1,0:T(8,128)(2,1)}, bf16...) custom-call(s32[1]{0:T(128)} %bitcast.me_ref, ...), custom_call_target="tpu_custom_call" | custom-call | flops 1 | bytes 1 | tf_op jit(solution)/shard_map/ffn/pallas_call | solution.py:515
  207.3 7.4 %mix_back.1 = (bf16[4,240,384]{2,1,0:T(8,128)(2,1)S(1)}, f32[4,240,384]{2,1,0:T(8,128)}, f32[4,1,240]{2,1,0:T(1,128)S(1)}, bf16[960,240]{1,0:T(8,128)(2,1)S(1)},...) custom-call(s32[1]{0:T(128)} %bitcast.me_ref, ...), custom_call_target="tpu_custom_call" | custom-call | flops 1 | bytes 1 | tf_op jit(solution)/shard_map/mix_back/pallas_call | solution.py:545
  219.0 3.4 add_convert_fusion.2
  230.7 2.5 collective-permute-start.49
  235.6 23.4 %attend_back.1 = (f32[960,384]{1,0:T(8,128)}, bf16[2,320,384]{2,1,0:T(8,128)(2,1)S(1)}, bf16[2,320,384]{2,1,0:T(8,128)(2,1)S(1)}, bf16[2,320,384]{2,1,0:T(8,128)...) custom-call(s32[1]{0:T(128)} %bitcast.1.place_ref, bf16[960,384]{1,0:T(8,128)(2,1)S(1)} %copy-done.5, ...), custom_call_target="tpu_custom_call" | custom-call | flops 1 | bytes 1 | tf_op jit(solution)/shard_map/attend_back/pallas_call | solution.py:263
  264.2 9.0 %collective-permute-done.46 = bf16[2,320,384]{2,1,0:T(8,128)(2,1)S(1)} collective-permute-done((bf16[2,320,384]{2,1,0:T(8,128)(2,1)S(1)}, bf16[2,320,384]{2,1,0:T(8,128)(2,1)S(1)}, u32[]{:S(2)}, u32[]{:S(2)}) %collective-permute-start.46) | collective-permute-done | bytes 491552 | tf_op jit(solution)/shard_map/ppermute | solution.py:35
  278.9 4.8 %project_q_back.1 = (f32[4,240,384]{2,1,0:T(8,128)}, bf16[960,240]{1,0:T(8,128)(2,1)S(1)}, bf16[960,240]{1,0:T(8,128)(2,1)S(1)}, bf16[960,240]{1,0:T(8,128)(2,1)S(1)}, bf16[960,240]{1,0:T(8,128)(2,1)S(1)}) custom-call(f32[960,384]{1,0:T(8,128)} %get-tuple-element.179.dq_ref, bf16[4,240,384]{2,1,0:T(8,128)(2,1)S(1)} %copy-done.1, f32[32,384]{1,0:T(8,128)S(1)} %copy-done.37, ...), custom_call_target="tpu_custom_call" | custom-call | flops 1 | bytes 1 | tf_op jit(solution)/shard_map/project_q_back/pallas_call | solution.py:545
  294.7 7.3 %collective-permute-done.54 = bf16[4,240,384]{2,1,0:T(8,128)(2,1)S(1)} collective-permute-done((bf16[4,240,384]{2,1,0:T(8,128)(2,1)S(1)}, bf16[4,240,384]{2,1,0:T(8,128)(2,1)S(1)}, u32[]{:S(2)}, u32[]{:S(2)}) %collective-permute-start.54) | collective-permute-done | bytes 737312 | tf_op jit(solution)/shard_map/ppermute | solution.py:35
  305.4 6.6 %collective-permute-done.69 = bf16[2,240,256]{2,1,0:T(8,128)(2,1)S(1)} collective-permute-done((bf16[2,240,256]{2,1,0:T(8,128)(2,1)S(1)}, bf16[2,240,256]{2,1,0:T(8,128)(2,1)S(1)}, u32[]{:S(2)}, u32[]{:S(2)}) %collective-permute-start.69) | collective-permute-done | bytes 245792 | tf_op jit(solution)/shard_map/ppermute | solution.py:35
  320.1 5.3 %project_kv_back.1 = (bf16[3,960,128]{2,1,0:T(8,128)(2,1)}, f32[4,240,1]{2,1,0:T(8,128)S(1)}, bf16[704,240]{1,0:T(8,128)(2,1)S(1)}, bf16[704,240]{1,0:T(8,128)(2...) custom-call(s32[1]{0:T(128)} %bitcast.me_ref, f32[2,320,384]{2,1,0:T(8,128)} %convert_add_fusion.8.refs_0_, ...), custom_call_target="tpu_custom_call" | custom-call | flops 1 | bytes 1 | tf_op jit(solution)/shard_map/project_kv_back/pallas_call | solution.py:545
  328.7 2.4 collective-permute-start.68
  331.1 9.1 %collective-permute-done.56 = bf16[8,240,240]{2,1,0:T(8,128)(2,1)} collective-permute-done((bf16[8,240,240]{2,1,0:T(8,128)(2,1)}, bf16[8,240,240]{2,1,0:T(8,128)(2,1)}, u32[]{:S(2)}, u32[]{:S(2)}) %collective-permute-start.56) | collective-permute-done | bytes 921632 | tf_op jit(solution)/shard_map/ppermute | solution.py:35
  347.0 6.8 %collective-permute-done.59 = bf16[8,88,240]{2,1,0:T(8,128)(2,1)S(1)} collective-permute-done((bf16[8,88,240]{2,1,0:T(8,128)(2,1)S(1)}, bf16[8,88,240]{2,1,0:T(8,128)(2,1)S(1)}, u32[]{:S(2)}, u32[]{:S(2)}) %collective-permute-start.59) | collective-permute-done | bytes 337952 | tf_op jit(solution)/shard_map/ppermute | solution.py:35
  356.6 6.5 %collective-permute-done.60 = bf16[4,88,240]{2,1,0:T(8,128)(2,1)S(1)} collective-permute-done((bf16[4,88,240]{2,1,0:T(8,128)(2,1)S(1)}, bf16[4,88,240]{2,1,0:T(8,128)(2,1)S(1)}, u32[]{:S(2)}, u32[]{:S(2)}) %collective-permute-start.60) | collective-permute-done | bytes 168992 | tf_op jit(solution)/shard_map/ppermute | solution.py:35
  365.2 2.7 collective-permute-done.61
  373.7 2.5 collective-permute-done.65
  378.2 3.9 %collective-permute-done.66 = bf16[1,240,240]{2,1,0:T(8,128)(2,1)S(1)} collective-permute-done((bf16[1,240,240]{2,1,0:T(8,128)(2,1)S(1)}, bf16[1,240,240]{2,1,0:T(8,128)(2,1)S(1)}, u32[]{:S(2)}, u32[]{:S(2)}) %collective-permute-start.66) | collective-permute-done | bytes 115232 | tf_op jit(solution)/shard_map/ppermute | solution.py:35
  (457 shorter events, 145.2 us)
Async XLA Ops:
  13.7 21.3 %collective-permute-start.23 = (bf16[1,240,384]{2,1,0:T(8,128)(2,1)S(1)}, bf16[1,240,384]{2,1,0:T(8,128)(2,1)S(1)}, u32[]{:S(2)}, u32[]{:S(2)}) collective-permute-start(bf16[1,240,384]{2,1,0:T(8,128)(2,1)S(1)} %fusion.25), channel_id=1, source_target_pairs={{0,4},{1,5},{2,6},{3,7},{4,0},{5,1},{6,2},{7,3},{8,12},{9,13},{10,... | collective-permute-start | bytes 552968 | tf_op jit(solution)/shard_map/ppermute | solution.py:35
  16.9 27.1 %collective-permute-start.4 = (bf16[4,88,240]{2,1,0:T(8,128)(2,1)}, bf16[4,88,240]{2,1,0:T(8,128)(2,1)}, u32[]{:S(2)}, u32[]{:S(2)}) collective-permute-start(bf16[4,88,240]{2,1,0:T(8,128)(2,1)} %bitcast.16), channel_id=1, source_target_pairs={{0,16},{8,24},{16,0},{24,8},{1,17},{9,25},{17,1},{25,9},{2,18},{10... | collective-permute-start | bytes 506888 | tf_op jit(solution)/shard_map/ppermute | solution.py:35
  18.4 24.2 %collective-permute-start.2 = (bf16[4,88,240]{2,1,0:T(8,128)(2,1)}, bf16[4,88,240]{2,1,0:T(8,128)(2,1)S(1)}, u32[]{:S(2)}, u32[]{:S(2)}) collective-permute-start(bf16[4,88,240]{2,1,0:T(8,128)(2,1)} %bitcast.16), channel_id=1, source_target_pairs={{0,1},{1,0},{2,3},{3,2},{4,5},{5,4},{6,7},{7,6},{8,9},{9,8},{10,11... | collective-permute-start | bytes 506888 | tf_op jit(solution)/shard_map/ppermute | solution.py:35
  19.9 21.8 %collective-permute-start.15 = (bf16[1,120,640]{2,1,0:T(8,128)(2,1)S(1)}, bf16[1,120,640]{2,1,0:T(8,128)(2,1)S(1)}, u32[]{:S(2)}, u32[]{:S(2)}) collective-permute-start(bf16[1,120,640]{2,1,0:T(8,128)(2,1)S(1)} %bitcast.459), channel_id=1, source_target_pairs={{0,4},{1,5},{2,6},{3,7},{4,0},{5,1},{6,2},{7,3},{8,12},{9,13},{10,... | collective-permute-start | bytes 460808 | tf_op jit(solution)/shard_map/ppermute | solution.py:35
  43.7 25.7 %collective-permute-start.3 = (bf16[8,88,240]{2,1,0:T(8,128)(2,1)S(1)}, bf16[8,88,240]{2,1,0:T(8,128)(2,1)S(1)}, u32[]{:S(2)}, u32[]{:S(2)}) collective-permute-start(bf16[8,88,240]{2,1,0:T(8,128)(2,1)S(1)} %bitcast.386), channel_id=1, source_target_pairs={{0,8},{8,0},{16,24},{24,16},{1,9},{9,1},{17,25},{25,17},{2,10},{10... | collective-permute-start | bytes 1013768 | tf_op jit(solution)/shard_map/ppermute | solution.py:35
  67.0 20.6 %collective-permute-start.10 = (bf16[4,240,240]{2,1,0:T(8,128)(2,1)S(1)}, bf16[4,240,240]{2,1,0:T(8,128)(2,1)S(1)}, u32[]{:S(2)}, u32[]{:S(2)}) collective-permute-start(bf16[4,240,240]{2,1,0:T(8,128)(2,1)S(1)} %bitcast.440), channel_id=1, source_target_pairs={{0,1},{1,0},{2,3},{3,2},{4,5},{5,4},{6,7},{7,6},{8,9},{9,8},{10,11... | collective-permute-start | bytes 1382408 | tf_op jit(solution)/shard_map/ppermute | solution.py:35
  67.7 21.2 %collective-permute-start.14 = (bf16[4,240,256]{2,1,0:T(8,128)(2,1)S(1)}, bf16[4,240,256]{2,1,0:T(8,128)(2,1)S(1)}, u32[]{:S(2)}, u32[]{:S(2)}) collective-permute-start(bf16[4,240,256]{2,1,0:T(8,128)(2,1)S(1)} %bitcast.438), channel_id=1, source_target_pairs={{0,16},{8,24},{16,0},{24,8},{1,17},{9,25},{17,1},{25,9},{2,18},{10... | collective-permute-start | bytes 1474568 | tf_op jit(solution)/shard_map/ppermute | solution.py:35
  75.1 21.8 %collective-permute-start.25 = (bf16[4,240,384]{2,1,0:T(8,128)(2,1)S(1)}, bf16[4,240,384]{2,1,0:T(8,128)(2,1)S(1)}, u32[]{:S(2)}, u32[]{:S(2)}) collective-permute-start(bf16[4,240,384]{2,1,0:T(8,128)(2,1)S(1)} %bitcast.430), channel_id=1, source_target_pairs={{0,1},{1,0},{2,3},{3,2},{4,5},{5,4},{6,7},{7,6},{8,9},{9,8},{10,11... | collective-permute-start | bytes 2211848 | tf_op jit(solution)/shard_map/ppermute | solution.py:35
  91.3 21.9 %collective-permute-start.18 = (bf16[8,240,240]{2,1,0:T(8,128)(2,1)S(1)}, bf16[8,240,240]{2,1,0:T(8,128)(2,1)S(1)}, u32[]{:S(2)}, u32[]{:S(2)}) collective-permute-start(bf16[8,240,240]{2,1,0:T(8,128)(2,1)S(1)} %bitcast.421), channel_id=1, source_target_pairs={{0,16},{8,24},{16,0},{24,8},{1,17},{9,25},{17,1},{25,9},{2,18},{10... | collective-permute-start | bytes 2764808 | tf_op jit(solution)/shard_map/ppermute | solution.py:35
  94.7 19.4 %collective-permute-start.20 = (bf16[656,384]{1,0:T(8,128)(2,1)S(1)}, bf16[656,384]{1,0:T(8,128)(2,1)S(1)}, u32[]{:S(2)}, u32[]{:S(2)}) collective-permute-start(bf16[656,384]{1,0:T(8,128)(2,1)S(1)} %get-tuple-element.296), channel_id=1, source_target_pairs={{0,1},{1,0},{2,3},{3,2},{4,5},{5,4},{6,7},{7,6},{8,9},{9,8},{10,11... | collective-permute-start | bytes 1511432 | tf_op jit(solution)/shard_map/ppermute | solution.py:35
  95.4 19.4 %collective-permute-start.22 = (bf16[656,384]{1,0:T(8,128)(2,1)S(1)}, bf16[656,384]{1,0:T(8,128)(2,1)S(1)}, u32[]{:S(2)}, u32[]{:S(2)}) collective-permute-start(bf16[656,384]{1,0:T(8,128)(2,1)S(1)} %get-tuple-element.295), channel_id=1, source_target_pairs={{0,1},{1,0},{2,3},{3,2},{4,5},{5,4},{6,7},{7,6},{8,9},{9,8},{10,11... | collective-permute-start | bytes 1511432 | tf_op jit(solution)/shard_map/ppermute | solution.py:35
  97.0 19.4 %collective-permute-start.33 = (bf16[4,120,640]{2,1,0:T(8,128)(2,1)S(1)}, bf16[4,120,640]{2,1,0:T(8,128)(2,1)S(1)}, u32[]{:S(2)}, u32[]{:S(2)}) collective-permute-start(bf16[4,120,640]{2,1,0:T(8,128)(2,1)S(1)} %bitcast.452), channel_id=1, source_target_pairs={{0,2},{1,3},{2,0},{3,1},{4,6},{5,7},{6,4},{7,5},{8,10},{9,11},{10,... | collective-permute-start | bytes 1843208 | tf_op jit(solution)/shard_map/ppermute | solution.py:35
  101.0 46.8 %collective-permute-start.35 = (bf16[4,120,640]{2,1,0:T(8,128)(2,1)S(1)}, bf16[4,120,640]{2,1,0:T(8,128)(2,1)S(1)}, u32[]{:S(2)}, u32[]{:S(2)}) collective-permute-start(bf16[4,120,640]{2,1,0:T(8,128)(2,1)S(1)} %collective-permute-done.17), channel_id=1, source_target_pairs={{0,2},{1,3},{2,0},{3,1},{4,6},{5,7},{6,4},{7,5},{8,10},{9,11},{10,... | collective-permute-start | bytes 1843208 | tf_op jit(solution)/shard_map/ppermute | solution.py:35
  113.2 35.4 %collective-permute-start.27 = (bf16[8,240,384]{2,1,0:T(8,128)(2,1)}, bf16[8,240,384]{2,1,0:T(8,128)(2,1)}, u32[]{:S(2)}, u32[]{:S(2)}) collective-permute-start(bf16[8,240,384]{2,1,0:T(8,128)(2,1)} %bitcast.86.refs_0_), channel_id=1, source_target_pairs={{0,16},{8,24},{16,0},{24,8},{1,17},{9,25},{17,1},{25,9},{2,18},{10... | collective-permute-start | bytes 4423688 | tf_op jit(solution)/shard_map/ppermute | solution.py:35
  116.5 33.8 %collective-permute-start.29 = (bf16[4,240,256]{2,1,0:T(8,128)(2,1)S(1)}, bf16[4,240,256]{2,1,0:T(8,128)(2,1)S(1)}, u32[]{:S(2)}, u32[]{:S(2)}) collective-permute-start(bf16[4,240,256]{2,1,0:T(8,128)(2,1)S(1)} %bitcast.439), channel_id=1, source_target_pairs={{0,1},{1,0},{2,3},{3,2},{4,5},{5,4},{6,7},{7,6},{8,9},{9,8},{10,11... | collective-permute-start | bytes 1474568 | tf_op jit(solution)/shard_map/ppermute | solution.py:35
  201.6 17.3 %collective-permute-start.37 = (bf16[8,240,384]{2,1,0:T(8,128)(2,1)}, bf16[8,240,384]{2,1,0:T(8,128)(2,1)}, u32[]{:S(2)}, u32[]{:S(2)}) collective-permute-start(bf16[8,240,384]{2,1,0:T(8,128)(2,1)} %get-tuple-element.146), channel_id=1, source_target_pairs={{0,8},{8,0},{16,24},{24,16},{1,9},{9,1},{17,25},{25,17},{2,10},{10... | collective-permute-start | bytes 4423688 | tf_op jit(solution)/shard_map/ppermute | solution.py:35
  202.6 20.9 %collective-permute-start.40 = (bf16[8,240,256]{2,1,0:T(8,128)(2,1)}, bf16[8,240,256]{2,1,0:T(8,128)(2,1)}, u32[]{:S(2)}, u32[]{:S(2)}) collective-permute-start(bf16[8,240,256]{2,1,0:T(8,128)(2,1)} %get-tuple-element.149), channel_id=1, source_target_pairs={{0,8},{8,0},{16,24},{24,16},{1,9},{9,1},{17,25},{25,17},{2,10},{10... | collective-permute-start | bytes 2949128 | tf_op jit(solution)/shard_map/ppermute | solution.py:35
  202.7 23.7 %collective-permute-start.39 = (bf16[8,240,256]{2,1,0:T(8,128)(2,1)}, bf16[8,240,256]{2,1,0:T(8,128)(2,1)}, u32[]{:S(2)}, u32[]{:S(2)}) collective-permute-start(bf16[8,240,256]{2,1,0:T(8,128)(2,1)} %get-tuple-element.148), channel_id=1, source_target_pairs={{0,8},{8,0},{16,24},{24,16},{1,9},{9,1},{17,25},{25,17},{2,10},{10... | collective-permute-start | bytes 2949128 | tf_op jit(solution)/shard_map/ppermute | solution.py:35
  222.3 52.8 %collective-permute-start.47 = (bf16[8,240,384]{2,1,0:T(8,128)(2,1)}, bf16[8,240,384]{2,1,0:T(8,128)(2,1)S(1)}, u32[]{:S(2)}, u32[]{:S(2)}) collective-permute-start(bf16[8,240,384]{2,1,0:T(8,128)(2,1)} %add_convert_fusion.2), channel_id=1, source_target_pairs={{0,16},{8,24},{16,0},{24,8},{1,17},{9,25},{17,1},{25,9},{2,18},{10... | collective-permute-start | bytes 4423688 | tf_op jit(solution)/shard_map/ppermute | solution.py:35
  225.1 33.9 %collective-permute-start.44 = (bf16[4,240,256]{2,1,0:T(8,128)(2,1)S(1)}, bf16[4,240,256]{2,1,0:T(8,128)(2,1)}, u32[]{:S(2)}, u32[]{:S(2)}) collective-permute-start(bf16[4,240,256]{2,1,0:T(8,128)(2,1)S(1)} %dynamic-slice_bitcast_fusion.2), channel_id=1, source_target_pairs={{0,1},{1,0},{2,3},{3,2},{4,5},{5,4},{6,7},{7,6},{8,9},{9,8},{10,11... | collective-permute-start | bytes 1474568 | tf_op jit(solution)/shard_map/ppermute | solution.py:35
  228.1 30.9 %collective-permute-start.43 = (bf16[4,240,256]{2,1,0:T(8,128)(2,1)S(1)}, bf16[4,240,256]{2,1,0:T(8,128)(2,1)}, u32[]{:S(2)}, u32[]{:S(2)}) collective-permute-start(bf16[4,240,256]{2,1,0:T(8,128)(2,1)S(1)} %dynamic-slice_bitcast_fusion.3), channel_id=1, source_target_pairs={{0,1},{1,0},{2,3},{3,2},{4,5},{5,4},{6,7},{7,6},{8,9},{9,8},{10,11... | collective-permute-start | bytes 1474568 | tf_op jit(solution)/shard_map/ppermute | solution.py:35
  230.7 31.6 %collective-permute-start.49 = (bf16[4,120,640]{2,1,0:T(8,128)(2,1)S(1)}, bf16[4,120,640]{2,1,0:T(8,128)(2,1)S(1)}, u32[]{:S(2)}, u32[]{:S(2)}) collective-permute-start(bf16[4,120,640]{2,1,0:T(8,128)(2,1)S(1)} %bitcast.454), channel_id=1, source_target_pairs={{0,2},{1,3},{2,0},{3,1},{4,6},{5,7},{6,4},{7,5},{8,10},{9,11},{10,... | collective-permute-start | bytes 1843208 | tf_op jit(solution)/shard_map/ppermute | solution.py:35
  234.5 40.6 %collective-permute-start.48 = (bf16[4,120,640]{2,1,0:T(8,128)(2,1)}, bf16[4,120,640]{2,1,0:T(8,128)(2,1)S(1)}, u32[]{:S(2)}, u32[]{:S(2)}) collective-permute-start(bf16[4,120,640]{2,1,0:T(8,128)(2,1)} %bitcast.115), channel_id=1, source_target_pairs={{0,2},{1,3},{2,0},{3,1},{4,6},{5,7},{6,4},{7,5},{8,10},{9,11},{10,... | collective-permute-start | bytes 1843208 | tf_op jit(solution)/shard_map/ppermute | solution.py:35
  261.3 30.7 %collective-permute-start.52 = (bf16[4,240,256]{2,1,0:T(8,128)(2,1)}, bf16[4,240,256]{2,1,0:T(8,128)(2,1)}, u32[]{:S(2)}, u32[]{:S(2)}) collective-permute-start(bf16[4,240,256]{2,1,0:T(8,128)(2,1)} %fusion.7), channel_id=1, source_target_pairs={{0,16},{8,24},{16,0},{24,8},{1,17},{9,25},{17,1},{25,9},{2,18},{10... | collective-permute-start | bytes 1474568 | tf_op jit(solution)/shard_map/ppermute | solution.py:35
  262.3 26.6 %collective-permute-start.45 = (bf16[2,320,384]{2,1,0:T(8,128)(2,1)S(1)}, bf16[2,320,384]{2,1,0:T(8,128)(2,1)S(1)}, u32[]{:S(2)}, u32[]{:S(2)}) collective-permute-start(bf16[2,320,384]{2,1,0:T(8,128)(2,1)S(1)} %get-tuple-element.160), channel_id=1, source_target_pairs={{0,1},{1,0},{2,3},{3,2},{4,5},{5,4},{6,7},{7,6},{8,9},{9,8},{10,11... | collective-permute-start | bytes 1474568 | tf_op jit(solution)/shard_map/ppermute | solution.py:35
  283.8 18.3 %collective-permute-start.54 = (bf16[4,240,384]{2,1,0:T(8,128)(2,1)S(1)}, bf16[4,240,384]{2,1,0:T(8,128)(2,1)S(1)}, u32[]{:S(2)}, u32[]{:S(2)}) collective-permute-start(bf16[4,240,384]{2,1,0:T(8,128)(2,1)S(1)} %dynamic-slice_bitcast_fusion), channel_id=1, source_target_pairs={{0,1},{1,0},{2,3},{3,2},{4,5},{5,4},{6,7},{7,6},{8,9},{9,8},{10,11... | collective-permute-start | bytes 2211848 | tf_op jit(solution)/shard_map/ppermute | solution.py:35
  286.9 57.1 %collective-permute-start.63 = (bf16[8,240,240]{2,1,0:T(8,128)(2,1)}, bf16[8,240,240]{2,1,0:T(8,128)(2,1)}, u32[]{:S(2)}, u32[]{:S(2)}) collective-permute-start(bf16[8,240,240]{2,1,0:T(8,128)(2,1)} %pad_maximum_fusion.7), channel_id=1, source_target_pairs={{0,8},{8,0},{16,24},{24,16},{1,9},{9,1},{17,25},{25,17},{2,10},{10... | collective-permute-start | bytes 2764808 | tf_op jit(solution)/shard_map/ppermute | solution.py:35
  287.0 28.3 %collective-permute-start.55 = (bf16[8,240,240]{2,1,0:T(8,128)(2,1)S(1)}, bf16[8,240,240]{2,1,0:T(8,128)(2,1)S(1)}, u32[]{:S(2)}, u32[]{:S(2)}) collective-permute-start(bf16[8,240,240]{2,1,0:T(8,128)(2,1)S(1)} %pad_maximum_fusion.6), channel_id=1, source_target_pairs={{0,8},{8,0},{16,24},{24,16},{1,9},{9,1},{17,25},{25,17},{2,10},{10... | collective-permute-start | bytes 2764808 | tf_op jit(solution)/shard_map/ppermute | solution.py:35
  288.9 24.0 %collective-permute-start.71 = (bf16[2,120,640]{2,1,0:T(8,128)(2,1)S(1)}, bf16[2,120,640]{2,1,0:T(8,128)(2,1)S(1)}, u32[]{:S(2)}, u32[]{:S(2)}) collective-permute-start(bf16[2,120,640]{2,1,0:T(8,128)(2,1)S(1)} %dynamic-slice_bitcast_fusion.5), channel_id=1, source_target_pairs={{0,1},{1,0},{2,3},{3,2},{4,5},{5,4},{6,7},{7,6},{8,9},{9,8},{10,11... | collective-permute-start | bytes 921608 | tf_op jit(solution)/shard_map/ppermute | solution.py:35
  292.0 25.8 %collective-permute-start.51 = (bf16[2,320,384]{2,1,0:T(8,128)(2,1)S(1)}, bf16[2,320,384]{2,1,0:T(8,128)(2,1)S(1)}, u32[]{:S(2)}, u32[]{:S(2)}) collective-permute-start(bf16[2,320,384]{2,1,0:T(8,128)(2,1)S(1)} %add_convert_fusion.10), channel_id=1, source_target_pairs={{2,0},{3,1},{4,2},{5,3},{6,4},{7,5},{10,8},{11,9},{12,10},{13,11},... | collective-permute-start | bytes 1474568 | tf_op jit(solution)/shard_map/ppermute | solution.py:135
  317.8 22.3 %collective-permute-start.56 = (bf16[8,240,240]{2,1,0:T(8,128)(2,1)}, bf16[8,240,240]{2,1,0:T(8,128)(2,1)}, u32[]{:S(2)}, u32[]{:S(2)}) collective-permute-start(bf16[8,240,240]{2,1,0:T(8,128)(2,1)} %add_convert_fusion.5), channel_id=1, source_target_pairs={{0,16},{8,24},{16,0},{24,8},{1,17},{9,25},{17,1},{25,9},{2,18},{10... | collective-permute-start | bytes 2764808 | tf_op jit(solution)/shard_map/ppermute | solution.py:35
  346.0 19.0 %collective-permute-start.64 = (bf16[4,240,240]{2,1,0:T(8,128)(2,1)S(1)}, bf16[4,240,240]{2,1,0:T(8,128)(2,1)S(1)}, u32[]{:S(2)}, u32[]{:S(2)}) collective-permute-start(bf16[4,240,240]{2,1,0:T(8,128)(2,1)S(1)} %dynamic-slice_bitcast_fusion.1), channel_id=1, source_target_pairs={{0,1},{1,0},{2,3},{3,2},{4,5},{5,4},{6,7},{7,6},{8,9},{9,8},{10,11... | collective-permute-start | bytes 1382408 | tf_op jit(solution)/shard_map/ppermute | solution.py:35
  (130 other events, 1252.8 us)

commit v5 on v4

--- a/solution.py
+++ b/solution.py
@@ -824,7 +824,7 @@
     ]
     g_kv = Scatter(g_kv, x_last[::-1])
     g_one.step(first_moved, hold=(input_grad,))
-    token = g_kv.step(*ahead)
+    token = g_kv.step(hold=ahead)
     g_qo.step()
     for g in (g_two, g_down, g_one):
         while g.done < len(x_last):

time: 390 us -> 388 us (level)
  transfers between devices with their start and end apart: 73 -> 73, of which waited for: 25 -> 24; matrix products, arithmetic and copies ran while one was open for 15% -> 15% of each run, Pallas kernels for 16% -> 16%
where the time goes in v5:
time: 388 us; the launch traced here: 382 us
  waiting for transfers between devices  125 us (32%)
  Pallas kernels  99.4 us (26%)
  starting transfers between devices  75.3 us (19%)
  other arithmetic  40.6 us (10%)
  local copies, waits for them, and re-layouts  39.4 us (10%)
    ppermute x69, waiting for transfers between devices, swap(): return lax.ppermute(values, axis, [(i, i ^ mask) for i in range(size)])  117 us
    ppermute x69, starting transfers between devices, swap(): return lax.ppermute(values, axis, [(i, i ^ mask) for i in range(size)])  65.7 us
    pallas_call x1, Pallas kernels, ffn(): pl.pallas_call(functools.partial(ffn_kernel, parts, per), grid_spec=pltpu...  38.7 us
    unnamed x191, local copies, waits for them, and re-layouts  24.9 us
    pallas_call x1, Pallas kernels, attend_back(): pl.pallas_call(functools.partial(backward_kernel, blocks, tokens), grid_s...  23.4 us
    pallas_call x6, Pallas kernels, in_vmem(): pl.pallas_call(kernel, in_specs=[smem] * scalars + [vmem] * (len(args) -...  22.2 us
    convert_element_type x22, other arithmetic, step(): self.bufs[r] = total.astype(b16) if rest else total  20.6 us
    pallas_call x1, Pallas kernels, attend(): pl.pallas_call(functools.partial(forward_kernel, blocks, tokens), grid_sp...  15.1 us
  transfers between devices with their start and end apart: 73, of which 24 were waited for; matrix products, arithmetic and copies ran while one was open for 15% of the time, Pallas kernels for 16%

profile of v5, /device:TPU:0, one launch (start us, length us, event | category | flops | bytes accessed | tf_op | source)
XLA Modules:
  0.0 382.0 jit_solution(7945460460498673783)
XLA Ops:
  2.4 4.1 %collective-permute-start = (bf16[1,88,240]{2,1,0:T(8,128)(2,1)S(1)}, bf16[1,88,240]{2,1,0:T(8,128)(2,1)S(1)}, u32[]{:S(2)}, u32[]{:S(2)}) collective-permute-start(bf16[1,88,240]{2,1,0:T(8,128)(2,1)S(1)} %maximum_bitcast_fusion.6), channel_id=1, source_target_pairs={{0,4},{1,5},{2,6},{3,7},{4,0},{5,1},{6,2},{7,3},{8,12},{9,13},{10,... | collective-permute-start | bytes 126728 | tf_op jit(solution)/shard_map/ppermute | solution.py:35
  20.5 9.2 %collective-permute-done.12 = bf16[1,240,256]{2,1,0:T(8,128)(2,1)S(1)} collective-permute-done((bf16[1,240,256]{2,1,0:T(8,128)(2,1)S(1)}, bf16[1,240,256]{2,1,0:T(8,128)(2,1)S(1)}, u32[]{:S(2)}, u32[]{:S(2)}) %collective-permute-start.12) | collective-permute-done | bytes 122912 | tf_op jit(solution)/shard_map/ppermute | solution.py:35
  30.6 4.4 %collective-permute-done.23 = bf16[1,240,384]{2,1,0:T(8,128)(2,1)S(1)} collective-permute-done((bf16[1,240,384]{2,1,0:T(8,128)(2,1)S(1)}, bf16[1,240,384]{2,1,0:T(8,128)(2,1)S(1)}, u32[]{:S(2)}, u32[]{:S(2)}) %collective-permute-start.23) | collective-permute-done | bytes 184352 | tf_op jit(solution)/shard_map/ppermute | solution.py:35
  36.0 4.9 %collective-permute-done.8 = bf16[1,240,240]{2,1,0:T(8,128)(2,1)S(1)} collective-permute-done((bf16[1,240,240]{2,1,0:T(8,128)(2,1)S(1)}, bf16[1,240,240]{2,1,0:T(8,128)(2,1)S(1)}, u32[]{:S(2)}, u32[]{:S(2)}) %collective-permute-start.8) | collective-permute-done | bytes 115232 | tf_op jit(solution)/shard_map/ppermute | solution.py:35
  45.7 5.4 %collective-permute-done.5 = bf16[4,88,240]{2,1,0:T(8,128)(2,1)S(1)} collective-permute-done((bf16[4,88,240]{2,1,0:T(8,128)(2,1)}, bf16[4,88,240]{2,1,0:T(8,128)(2,1)S(1)}, u32[]{:S(2)}, u32[]{:S(2)}) %collective-permute-start.5) | collective-permute-done | bytes 168992 | tf_op jit(solution)/shard_map/ppermute | solution.py:35
  55.9 5.8 %collective-permute-done.9 = bf16[2,240,240]{2,1,0:T(8,128)(2,1)S(1)} collective-permute-done((bf16[2,240,240]{2,1,0:T(8,128)(2,1)}, bf16[2,240,240]{2,1,0:T(8,128)(2,1)S(1)}, u32[]{:S(2)}, u32[]{:S(2)}) %collective-permute-start.9) | collective-permute-done | bytes 230432 | tf_op jit(solution)/shard_map/ppermute | solution.py:35
  62.8 4.1 %collective-permute-done.13 = bf16[2,240,256]{2,1,0:T(8,128)(2,1)S(1)} collective-permute-done((bf16[2,240,256]{2,1,0:T(8,128)(2,1)}, bf16[2,240,256]{2,1,0:T(8,128)(2,1)S(1)}, u32[]{:S(2)}, u32[]{:S(2)}) %collective-permute-start.13) | collective-permute-done | bytes 245792 | tf_op jit(solution)/shard_map/ppermute | solution.py:35
  76.4 6.2 %collective-permute-done.7.refs_3_.refs_8_.refs_13_.refs_5_.refs_10_.refs_15_ = bf16[656,384]{1,0:T(8,128)(2,1)S(1)} collective-permute-done((bf16[656,384]{1,0:T(8,128)(2,1)S(1)}, bf16[656,384]{1,0:T(8,128)(2,1)S(1)}, u32[]{:S(2)}, u32[]{:S(2)}) %collective-permute-start.7) | collective-permute-done | bytes 503840 | tf_op jit(solution)/shard_map/ppermute | solution.py:135
  82.7 4.9 %collective-permute-start.21 = (bf16[656,384]{1,0:T(8,128)(2,1)S(1)}, bf16[656,384]{1,0:T(8,128)(2,1)S(1)}, u32[]{:S(2)}, u32[]{:S(2)}) collective-permute-start(bf16[656,384]{1,0:T(8,128)(2,1)S(1)} %collective-permute-done.7.refs_3_.refs_8_.refs_13_.refs_5_.refs_10_.refs_15_), channel_id=1, source_target_pairs={{0,2},{1,3},{2,4},{3,5},{4,6},{5,7},{8,10},{9,11},{10,12},{11,13},... | collective-permute-start | bytes 1511432 | tf_op jit(solution)/shard_map/ppermute | solution.py:135
  97.0 2.5 collective-permute-start.33
  101.9 11.2 %collective-permute-done.18 = bf16[8,240,240]{2,1,0:T(8,128)(2,1)S(1)} collective-permute-done((bf16[8,240,240]{2,1,0:T(8,128)(2,1)S(1)}, bf16[8,240,240]{2,1,0:T(8,128)(2,1)S(1)}, u32[]{:S(2)}, u32[]{:S(2)}) %collective-permute-start.18) | collective-permute-done | bytes 921632 | tf_op jit(solution)/shard_map/ppermute | solution.py:35
  117.8 11.1 %collective-permute-done.31 = bf16[4,240,256]{2,1,0:T(8,128)(2,1)S(1)} collective-permute-done((bf16[4,240,256]{2,1,0:T(8,128)(2,1)S(1)}, bf16[4,240,256]{2,1,0:T(8,128)(2,1)S(1)}, u32[]{:S(2)}, u32[]{:S(2)}) %collective-permute-start.31) | collective-permute-done | bytes 491552 | tf_op jit(solution)/shard_map/ppermute | solution.py:35
  131.3 15.1 %attend.1 = (bf16[960,384]{1,0:T(8,128)(2,1)S(1)}, f32[5,8,384]{2,1,0:T(8,128)S(1)}) custom-call(s32[1]{0:T(128)} %bitcast.1.place_ref, bf16[960,384]{1,0:T(8,128)(2,1)S(1)} %project_q.1.refs_0_, bf16[656,384]{1,0:T(8,128)(2,1)S(1)} %get-tuple-element.115.refs_1_.refs_6_.refs_11_.refs_3_.refs_8_.refs_13_, ...), custom_call_target="tpu_custom_call" | custom-call | flops 1 | bytes 1 | tf_op jit(solution)/shard_map/attend/pallas_call | solution.py:238
  158.0 2.5 mix.1
  163.0 38.7 %ffn.1 = (bf16[3,960,128]{2,1,0:T(8,128)(2,1)}, f32[4,384,240]{2,1,0:T(8,128)}, bf16[8,240,384]{2,1,0:T(8,128)(2,1)}, bf16[8,240,384]{2,1,0:T(8,128)(2,1)}, bf16...) custom-call(s32[1]{0:T(128)} %bitcast.me_ref, ...), custom_call_target="tpu_custom_call" | custom-call | flops 1 | bytes 1 | tf_op jit(solution)/shard_map/ffn/pallas_call | solution.py:515
  207.3 7.4 %mix_back.1 = (bf16[4,240,384]{2,1,0:T(8,128)(2,1)S(1)}, f32[4,240,384]{2,1,0:T(8,128)}, f32[4,1,240]{2,1,0:T(1,128)S(1)}, bf16[960,240]{1,0:T(8,128)(2,1)S(1)},...) custom-call(s32[1]{0:T(128)} %bitcast.me_ref, ...), custom_call_target="tpu_custom_call" | custom-call | flops 1 | bytes 1 | tf_op jit(solution)/shard_map/mix_back/pallas_call | solution.py:545
  219.0 3.4 add_convert_fusion.2
  230.7 2.5 collective-permute-start.49
  235.6 23.4 %attend_back.1 = (f32[960,384]{1,0:T(8,128)}, bf16[2,320,384]{2,1,0:T(8,128)(2,1)S(1)}, bf16[2,320,384]{2,1,0:T(8,128)(2,1)S(1)}, bf16[2,320,384]{2,1,0:T(8,128)...) custom-call(s32[1]{0:T(128)} %bitcast.1.place_ref, bf16[960,384]{1,0:T(8,128)(2,1)S(1)} %copy-done.5, ...), custom_call_target="tpu_custom_call" | custom-call | flops 1 | bytes 1 | tf_op jit(solution)/shard_map/attend_back/pallas_call | solution.py:263
  264.2 9.0 %collective-permute-done.46 = bf16[2,320,384]{2,1,0:T(8,128)(2,1)S(1)} collective-permute-done((bf16[2,320,384]{2,1,0:T(8,128)(2,1)S(1)}, bf16[2,320,384]{2,1,0:T(8,128)(2,1)S(1)}, u32[]{:S(2)}, u32[]{:S(2)}) %collective-permute-start.46) | collective-permute-done | bytes 491552 | tf_op jit(solution)/shard_map/ppermute | solution.py:35
  278.9 4.8 %project_q_back.1 = (f32[4,240,384]{2,1,0:T(8,128)}, bf16[960,240]{1,0:T(8,128)(2,1)S(1)}, bf16[960,240]{1,0:T(8,128)(2,1)S(1)}, bf16[960,240]{1,0:T(8,128)(2,1)S(1)}, bf16[960,240]{1,0:T(8,128)(2,1)S(1)}) custom-call(f32[960,384]{1,0:T(8,128)} %get-tuple-element.179.dq_ref, bf16[4,240,384]{2,1,0:T(8,128)(2,1)S(1)} %copy-done.1, f32[32,384]{1,0:T(8,128)S(1)} %copy-done.37, ...), custom_call_target="tpu_custom_call" | custom-call | flops 1 | bytes 1 | tf_op jit(solution)/shard_map/project_q_back/pallas_call | solution.py:545
  294.7 7.3 %collective-permute-done.54 = bf16[4,240,384]{2,1,0:T(8,128)(2,1)S(1)} collective-permute-done((bf16[4,240,384]{2,1,0:T(8,128)(2,1)S(1)}, bf16[4,240,384]{2,1,0:T(8,128)(2,1)S(1)}, u32[]{:S(2)}, u32[]{:S(2)}) %collective-permute-start.54) | collective-permute-done | bytes 737312 | tf_op jit(solution)/shard_map/ppermute | solution.py:35
  305.4 6.6 %collective-permute-done.69 = bf16[2,240,256]{2,1,0:T(8,128)(2,1)S(1)} collective-permute-done((bf16[2,240,256]{2,1,0:T(8,128)(2,1)S(1)}, bf16[2,240,256]{2,1,0:T(8,128)(2,1)S(1)}, u32[]{:S(2)}, u32[]{:S(2)}) %collective-permute-start.69) | collective-permute-done | bytes 245792 | tf_op jit(solution)/shard_map/ppermute | solution.py:35
  320.1 5.3 %project_kv_back.1 = (bf16[3,960,128]{2,1,0:T(8,128)(2,1)}, f32[4,240,1]{2,1,0:T(8,128)S(1)}, bf16[704,240]{1,0:T(8,128)(2,1)S(1)}, bf16[704,240]{1,0:T(8,128)(2...) custom-call(s32[1]{0:T(128)} %bitcast.me_ref, f32[2,320,384]{2,1,0:T(8,128)} %convert_add_fusion.8.refs_0_, ...), custom_call_target="tpu_custom_call" | custom-call | flops 1 | bytes 1 | tf_op jit(solution)/shard_map/project_kv_back/pallas_call | solution.py:545
  328.7 2.5 collective-permute-start.68
  332.3 8.0 %collective-permute-done.68 = bf16[1,240,384]{2,1,0:T(8,128)(2,1)S(1)} collective-permute-done((bf16[1,240,384]{2,1,0:T(8,128)(2,1)S(1)}, bf16[1,240,384]{2,1,0:T(8,128)(2,1)S(1)}, u32[]{:S(2)}, u32[]{:S(2)}) %collective-permute-start.68) | collective-permute-done | bytes 184352 | tf_op jit(solution)/shard_map/ppermute | solution.py:35
  344.4 5.7 %collective-permute-done.59 = bf16[8,88,240]{2,1,0:T(8,128)(2,1)S(1)} collective-permute-done((bf16[8,88,240]{2,1,0:T(8,128)(2,1)S(1)}, bf16[8,88,240]{2,1,0:T(8,128)(2,1)S(1)}, u32[]{:S(2)}, u32[]{:S(2)}) %collective-permute-start.59) | collective-permute-done | bytes 337952 | tf_op jit(solution)/shard_map/ppermute | solution.py:35
  352.9 6.8 %collective-permute-done.60 = bf16[4,88,240]{2,1,0:T(8,128)(2,1)S(1)} collective-permute-done((bf16[4,88,240]{2,1,0:T(8,128)(2,1)S(1)}, bf16[4,88,240]{2,1,0:T(8,128)(2,1)S(1)}, u32[]{:S(2)}, u32[]{:S(2)}) %collective-permute-start.60) | collective-permute-done | bytes 168992 | tf_op jit(solution)/shard_map/ppermute | solution.py:35
  361.3 3.1 collective-permute-done.61
  364.4 2.7 collective-permute-start.62
  370.2 4.1 %collective-permute-done.65 = bf16[2,240,240]{2,1,0:T(8,128)(2,1)S(1)} collective-permute-done((bf16[2,240,240]{2,1,0:T(8,128)(2,1)S(1)}, bf16[2,240,240]{2,1,0:T(8,128)(2,1)S(1)}, u32[]{:S(2)}, u32[]{:S(2)}) %collective-permute-start.65) | collective-permute-done | bytes 230432 | tf_op jit(solution)/shard_map/ppermute | solution.py:35
  375.0 5.2 %collective-permute-done.66 = bf16[1,240,240]{2,1,0:T(8,128)(2,1)S(1)} collective-permute-done((bf16[1,240,240]{2,1,0:T(8,128)(2,1)S(1)}, bf16[1,240,240]{2,1,0:T(8,128)(2,1)S(1)}, u32[]{:S(2)}, u32[]{:S(2)}) %collective-permute-start.66) | collective-permute-done | bytes 115232 | tf_op jit(solution)/shard_map/ppermute | solution.py:35
  (457 shorter events, 141.4 us)
Async XLA Ops:
  13.7 21.3 %collective-permute-start.23 = (bf16[1,240,384]{2,1,0:T(8,128)(2,1)S(1)}, bf16[1,240,384]{2,1,0:T(8,128)(2,1)S(1)}, u32[]{:S(2)}, u32[]{:S(2)}) collective-permute-start(bf16[1,240,384]{2,1,0:T(8,128)(2,1)S(1)} %fusion.25), channel_id=1, source_target_pairs={{0,4},{1,5},{2,6},{3,7},{4,0},{5,1},{6,2},{7,3},{8,12},{9,13},{10,... | collective-permute-start | bytes 552968 | tf_op jit(solution)/shard_map/ppermute | solution.py:35
  16.9 27.1 %collective-permute-start.4 = (bf16[4,88,240]{2,1,0:T(8,128)(2,1)}, bf16[4,88,240]{2,1,0:T(8,128)(2,1)}, u32[]{:S(2)}, u32[]{:S(2)}) collective-permute-start(bf16[4,88,240]{2,1,0:T(8,128)(2,1)} %bitcast.16), channel_id=1, source_target_pairs={{0,16},{8,24},{16,0},{24,8},{1,17},{9,25},{17,1},{25,9},{2,18},{10... | collective-permute-start | bytes 506888 | tf_op jit(solution)/shard_map/ppermute | solution.py:35
  18.4 24.2 %collective-permute-start.2 = (bf16[4,88,240]{2,1,0:T(8,128)(2,1)}, bf16[4,88,240]{2,1,0:T(8,128)(2,1)S(1)}, u32[]{:S(2)}, u32[]{:S(2)}) collective-permute-start(bf16[4,88,240]{2,1,0:T(8,128)(2,1)} %bitcast.16), channel_id=1, source_target_pairs={{0,1},{1,0},{2,3},{3,2},{4,5},{5,4},{6,7},{7,6},{8,9},{9,8},{10,11... | collective-permute-start | bytes 506888 | tf_op jit(solution)/shard_map/ppermute | solution.py:35
  19.9 21.8 %collective-permute-start.15 = (bf16[1,120,640]{2,1,0:T(8,128)(2,1)S(1)}, bf16[1,120,640]{2,1,0:T(8,128)(2,1)S(1)}, u32[]{:S(2)}, u32[]{:S(2)}) collective-permute-start(bf16[1,120,640]{2,1,0:T(8,128)(2,1)S(1)} %bitcast.459), channel_id=1, source_target_pairs={{0,4},{1,5},{2,6},{3,7},{4,0},{5,1},{6,2},{7,3},{8,12},{9,13},{10,... | collective-permute-start | bytes 460808 | tf_op jit(solution)/shard_map/ppermute | solution.py:35
  43.7 25.7 %collective-permute-start.3 = (bf16[8,88,240]{2,1,0:T(8,128)(2,1)S(1)}, bf16[8,88,240]{2,1,0:T(8,128)(2,1)S(1)}, u32[]{:S(2)}, u32[]{:S(2)}) collective-permute-start(bf16[8,88,240]{2,1,0:T(8,128)(2,1)S(1)} %bitcast.386), channel_id=1, source_target_pairs={{0,8},{8,0},{16,24},{24,16},{1,9},{9,1},{17,25},{25,17},{2,10},{10... | collective-permute-start | bytes 1013768 | tf_op jit(solution)/shard_map/ppermute | solution.py:35
  67.0 20.6 %collective-permute-start.10 = (bf16[4,240,240]{2,1,0:T(8,128)(2,1)S(1)}, bf16[4,240,240]{2,1,0:T(8,128)(2,1)S(1)}, u32[]{:S(2)}, u32[]{:S(2)}) collective-permute-start(bf16[4,240,240]{2,1,0:T(8,128)(2,1)S(1)} %bitcast.440), channel_id=1, source_target_pairs={{0,1},{1,0},{2,3},{3,2},{4,5},{5,4},{6,7},{7,6},{8,9},{9,8},{10,11... | collective-permute-start | bytes 1382408 | tf_op jit(solution)/shard_map/ppermute | solution.py:35
  67.7 21.2 %collective-permute-start.14 = (bf16[4,240,256]{2,1,0:T(8,128)(2,1)S(1)}, bf16[4,240,256]{2,1,0:T(8,128)(2,1)S(1)}, u32[]{:S(2)}, u32[]{:S(2)}) collective-permute-start(bf16[4,240,256]{2,1,0:T(8,128)(2,1)S(1)} %bitcast.438), channel_id=1, source_target_pairs={{0,16},{8,24},{16,0},{24,8},{1,17},{9,25},{17,1},{25,9},{2,18},{10... | collective-permute-start | bytes 1474568 | tf_op jit(solution)/shard_map/ppermute | solution.py:35
  75.1 21.8 %collective-permute-start.25 = (bf16[4,240,384]{2,1,0:T(8,128)(2,1)S(1)}, bf16[4,240,384]{2,1,0:T(8,128)(2,1)S(1)}, u32[]{:S(2)}, u32[]{:S(2)}) collective-permute-start(bf16[4,240,384]{2,1,0:T(8,128)(2,1)S(1)} %bitcast.430), channel_id=1, source_target_pairs={{0,1},{1,0},{2,3},{3,2},{4,5},{5,4},{6,7},{7,6},{8,9},{9,8},{10,11... | collective-permute-start | bytes 2211848 | tf_op jit(solution)/shard_map/ppermute | solution.py:35
  91.3 21.9 %collective-permute-start.18 = (bf16[8,240,240]{2,1,0:T(8,128)(2,1)S(1)}, bf16[8,240,240]{2,1,0:T(8,128)(2,1)S(1)}, u32[]{:S(2)}, u32[]{:S(2)}) collective-permute-start(bf16[8,240,240]{2,1,0:T(8,128)(2,1)S(1)} %bitcast.421), channel_id=1, source_target_pairs={{0,16},{8,24},{16,0},{24,8},{1,17},{9,25},{17,1},{25,9},{2,18},{10... | collective-permute-start | bytes 2764808 | tf_op jit(solution)/shard_map/ppermute | solution.py:35
  94.7 19.4 %collective-permute-start.20 = (bf16[656,384]{1,0:T(8,128)(2,1)S(1)}, bf16[656,384]{1,0:T(8,128)(2,1)S(1)}, u32[]{:S(2)}, u32[]{:S(2)}) collective-permute-start(bf16[656,384]{1,0:T(8,128)(2,1)S(1)} %get-tuple-element.296), channel_id=1, source_target_pairs={{0,1},{1,0},{2,3},{3,2},{4,5},{5,4},{6,7},{7,6},{8,9},{9,8},{10,11... | collective-permute-start | bytes 1511432 | tf_op jit(solution)/shard_map/ppermute | solution.py:35
  95.4 19.4 %collective-permute-start.22 = (bf16[656,384]{1,0:T(8,128)(2,1)S(1)}, bf16[656,384]{1,0:T(8,128)(2,1)S(1)}, u32[]{:S(2)}, u32[]{:S(2)}) collective-permute-start(bf16[656,384]{1,0:T(8,128)(2,1)S(1)} %get-tuple-element.295), channel_id=1, source_target_pairs={{0,1},{1,0},{2,3},{3,2},{4,5},{5,4},{6,7},{7,6},{8,9},{9,8},{10,11... | collective-permute-start | bytes 1511432 | tf_op jit(solution)/shard_map/ppermute | solution.py:35
  97.0 19.4 %collective-permute-start.33 = (bf16[4,120,640]{2,1,0:T(8,128)(2,1)S(1)}, bf16[4,120,640]{2,1,0:T(8,128)(2,1)S(1)}, u32[]{:S(2)}, u32[]{:S(2)}) collective-permute-start(bf16[4,120,640]{2,1,0:T(8,128)(2,1)S(1)} %bitcast.452), channel_id=1, source_target_pairs={{0,2},{1,3},{2,0},{3,1},{4,6},{5,7},{6,4},{7,5},{8,10},{9,11},{10,... | collective-permute-start | bytes 1843208 | tf_op jit(solution)/shard_map/ppermute | solution.py:35
  101.0 46.8 %collective-permute-start.35 = (bf16[4,120,640]{2,1,0:T(8,128)(2,1)S(1)}, bf16[4,120,640]{2,1,0:T(8,128)(2,1)S(1)}, u32[]{:S(2)}, u32[]{:S(2)}) collective-permute-start(bf16[4,120,640]{2,1,0:T(8,128)(2,1)S(1)} %collective-permute-done.17), channel_id=1, source_target_pairs={{0,2},{1,3},{2,0},{3,1},{4,6},{5,7},{6,4},{7,5},{8,10},{9,11},{10,... | collective-permute-start | bytes 1843208 | tf_op jit(solution)/shard_map/ppermute | solution.py:35
  113.2 35.4 %collective-permute-start.27 = (bf16[8,240,384]{2,1,0:T(8,128)(2,1)}, bf16[8,240,384]{2,1,0:T(8,128)(2,1)}, u32[]{:S(2)}, u32[]{:S(2)}) collective-permute-start(bf16[8,240,384]{2,1,0:T(8,128)(2,1)} %bitcast.86.refs_0_), channel_id=1, source_target_pairs={{0,16},{8,24},{16,0},{24,8},{1,17},{9,25},{17,1},{25,9},{2,18},{10... | collective-permute-start | bytes 4423688 | tf_op jit(solution)/shard_map/ppermute | solution.py:35
  116.5 33.8 %collective-permute-start.29 = (bf16[4,240,256]{2,1,0:T(8,128)(2,1)S(1)}, bf16[4,240,256]{2,1,0:T(8,128)(2,1)S(1)}, u32[]{:S(2)}, u32[]{:S(2)}) collective-permute-start(bf16[4,240,256]{2,1,0:T(8,128)(2,1)S(1)} %bitcast.439), channel_id=1, source_target_pairs={{0,1},{1,0},{2,3},{3,2},{4,5},{5,4},{6,7},{7,6},{8,9},{9,8},{10,11... | collective-permute-start | bytes 1474568 | tf_op jit(solution)/shard_map/ppermute | solution.py:35
  201.6 17.3 %collective-permute-start.37 = (bf16[8,240,384]{2,1,0:T(8,128)(2,1)}, bf16[8,240,384]{2,1,0:T(8,128)(2,1)}, u32[]{:S(2)}, u32[]{:S(2)}) collective-permute-start(bf16[8,240,384]{2,1,0:T(8,128)(2,1)} %get-tuple-element.146), channel_id=1, source_target_pairs={{0,8},{8,0},{16,24},{24,16},{1,9},{9,1},{17,25},{25,17},{2,10},{10... | collective-permute-start | bytes 4423688 | tf_op jit(solution)/shard_map/ppermute | solution.py:35
  202.6 20.9 %collective-permute-start.40 = (bf16[8,240,256]{2,1,0:T(8,128)(2,1)}, bf16[8,240,256]{2,1,0:T(8,128)(2,1)}, u32[]{:S(2)}, u32[]{:S(2)}) collective-permute-start(bf16[8,240,256]{2,1,0:T(8,128)(2,1)} %get-tuple-element.149), channel_id=1, source_target_pairs={{0,8},{8,0},{16,24},{24,16},{1,9},{9,1},{17,25},{25,17},{2,10},{10... | collective-permute-start | bytes 2949128 | tf_op jit(solution)/shard_map/ppermute | solution.py:35
  202.7 23.7 %collective-permute-start.39 = (bf16[8,240,256]{2,1,0:T(8,128)(2,1)}, bf16[8,240,256]{2,1,0:T(8,128)(2,1)}, u32[]{:S(2)}, u32[]{:S(2)}) collective-permute-start(bf16[8,240,256]{2,1,0:T(8,128)(2,1)} %get-tuple-element.148), channel_id=1, source_target_pairs={{0,8},{8,0},{16,24},{24,16},{1,9},{9,1},{17,25},{25,17},{2,10},{10... | collective-permute-start | bytes 2949128 | tf_op jit(solution)/shard_map/ppermute | solution.py:35
  222.3 52.8 %collective-permute-start.47 = (bf16[8,240,384]{2,1,0:T(8,128)(2,1)}, bf16[8,240,384]{2,1,0:T(8,128)(2,1)S(1)}, u32[]{:S(2)}, u32[]{:S(2)}) collective-permute-start(bf16[8,240,384]{2,1,0:T(8,128)(2,1)} %add_convert_fusion.2), channel_id=1, source_target_pairs={{0,16},{8,24},{16,0},{24,8},{1,17},{9,25},{17,1},{25,9},{2,18},{10... | collective-permute-start | bytes 4423688 | tf_op jit(solution)/shard_map/ppermute | solution.py:35
  225.1 33.9 %collective-permute-start.44 = (bf16[4,240,256]{2,1,0:T(8,128)(2,1)S(1)}, bf16[4,240,256]{2,1,0:T(8,128)(2,1)}, u32[]{:S(2)}, u32[]{:S(2)}) collective-permute-start(bf16[4,240,256]{2,1,0:T(8,128)(2,1)S(1)} %dynamic-slice_bitcast_fusion.2), channel_id=1, source_target_pairs={{0,1},{1,0},{2,3},{3,2},{4,5},{5,4},{6,7},{7,6},{8,9},{9,8},{10,11... | collective-permute-start | bytes 1474568 | tf_op jit(solution)/shard_map/ppermute | solution.py:35
  228.1 30.9 %collective-permute-start.43 = (bf16[4,240,256]{2,1,0:T(8,128)(2,1)S(1)}, bf16[4,240,256]{2,1,0:T(8,128)(2,1)}, u32[]{:S(2)}, u32[]{:S(2)}) collective-permute-start(bf16[4,240,256]{2,1,0:T(8,128)(2,1)S(1)} %dynamic-slice_bitcast_fusion.3), channel_id=1, source_target_pairs={{0,1},{1,0},{2,3},{3,2},{4,5},{5,4},{6,7},{7,6},{8,9},{9,8},{10,11... | collective-permute-start | bytes 1474568 | tf_op jit(solution)/shard_map/ppermute | solution.py:35
  230.7 31.6 %collective-permute-start.49 = (bf16[4,120,640]{2,1,0:T(8,128)(2,1)S(1)}, bf16[4,120,640]{2,1,0:T(8,128)(2,1)S(1)}, u32[]{:S(2)}, u32[]{:S(2)}) collective-permute-start(bf16[4,120,640]{2,1,0:T(8,128)(2,1)S(1)} %bitcast.454), channel_id=1, source_target_pairs={{0,2},{1,3},{2,0},{3,1},{4,6},{5,7},{6,4},{7,5},{8,10},{9,11},{10,... | collective-permute-start | bytes 1843208 | tf_op jit(solution)/shard_map/ppermute | solution.py:35
  234.5 40.6 %collective-permute-start.48 = (bf16[4,120,640]{2,1,0:T(8,128)(2,1)}, bf16[4,120,640]{2,1,0:T(8,128)(2,1)S(1)}, u32[]{:S(2)}, u32[]{:S(2)}) collective-permute-start(bf16[4,120,640]{2,1,0:T(8,128)(2,1)} %bitcast.115), channel_id=1, source_target_pairs={{0,2},{1,3},{2,0},{3,1},{4,6},{5,7},{6,4},{7,5},{8,10},{9,11},{10,... | collective-permute-start | bytes 1843208 | tf_op jit(solution)/shard_map/ppermute | solution.py:35
  261.3 30.7 %collective-permute-start.52 = (bf16[4,240,256]{2,1,0:T(8,128)(2,1)}, bf16[4,240,256]{2,1,0:T(8,128)(2,1)}, u32[]{:S(2)}, u32[]{:S(2)}) collective-permute-start(bf16[4,240,256]{2,1,0:T(8,128)(2,1)} %fusion.7), channel_id=1, source_target_pairs={{0,16},{8,24},{16,0},{24,8},{1,17},{9,25},{17,1},{25,9},{2,18},{10... | collective-permute-start | bytes 1474568 | tf_op jit(solution)/shard_map/ppermute | solution.py:35
  262.3 26.6 %collective-permute-start.45 = (bf16[2,320,384]{2,1,0:T(8,128)(2,1)S(1)}, bf16[2,320,384]{2,1,0:T(8,128)(2,1)S(1)}, u32[]{:S(2)}, u32[]{:S(2)}) collective-permute-start(bf16[2,320,384]{2,1,0:T(8,128)(2,1)S(1)} %get-tuple-element.160), channel_id=1, source_target_pairs={{0,1},{1,0},{2,3},{3,2},{4,5},{5,4},{6,7},{7,6},{8,9},{9,8},{10,11... | collective-permute-start | bytes 1474568 | tf_op jit(solution)/shard_map/ppermute | solution.py:35
  283.8 18.3 %collective-permute-start.54 = (bf16[4,240,384]{2,1,0:T(8,128)(2,1)S(1)}, bf16[4,240,384]{2,1,0:T(8,128)(2,1)S(1)}, u32[]{:S(2)}, u32[]{:S(2)}) collective-permute-start(bf16[4,240,384]{2,1,0:T(8,128)(2,1)S(1)} %dynamic-slice_bitcast_fusion), channel_id=1, source_target_pairs={{0,1},{1,0},{2,3},{3,2},{4,5},{5,4},{6,7},{7,6},{8,9},{9,8},{10,11... | collective-permute-start | bytes 2211848 | tf_op jit(solution)/shard_map/ppermute | solution.py:35
  286.9 54.6 %collective-permute-start.63 = (bf16[8,240,240]{2,1,0:T(8,128)(2,1)}, bf16[8,240,240]{2,1,0:T(8,128)(2,1)}, u32[]{:S(2)}, u32[]{:S(2)}) collective-permute-start(bf16[8,240,240]{2,1,0:T(8,128)(2,1)} %pad_maximum_fusion.7), channel_id=1, source_target_pairs={{0,8},{8,0},{16,24},{24,16},{1,9},{9,1},{17,25},{25,17},{2,10},{10... | collective-permute-start | bytes 2764808 | tf_op jit(solution)/shard_map/ppermute | solution.py:35
  287.0 28.3 %collective-permute-start.56 = (bf16[8,240,240]{2,1,0:T(8,128)(2,1)S(1)}, bf16[8,240,240]{2,1,0:T(8,128)(2,1)S(1)}, u32[]{:S(2)}, u32[]{:S(2)}) collective-permute-start(bf16[8,240,240]{2,1,0:T(8,128)(2,1)S(1)} %pad_maximum_fusion.6), channel_id=1, source_target_pairs={{0,8},{8,0},{16,24},{24,16},{1,9},{9,1},{17,25},{25,17},{2,10},{10... | collective-permute-start | bytes 2764808 | tf_op jit(solution)/shard_map/ppermute | solution.py:35
  288.9 24.0 %collective-permute-start.71 = (bf16[2,120,640]{2,1,0:T(8,128)(2,1)S(1)}, bf16[2,120,640]{2,1,0:T(8,128)(2,1)S(1)}, u32[]{:S(2)}, u32[]{:S(2)}) collective-permute-start(bf16[2,120,640]{2,1,0:T(8,128)(2,1)S(1)} %dynamic-slice_bitcast_fusion.5), channel_id=1, source_target_pairs={{0,1},{1,0},{2,3},{3,2},{4,5},{5,4},{6,7},{7,6},{8,9},{9,8},{10,11... | collective-permute-start | bytes 921608 | tf_op jit(solution)/shard_map/ppermute | solution.py:35
  292.0 25.8 %collective-permute-start.51 = (bf16[2,320,384]{2,1,0:T(8,128)(2,1)S(1)}, bf16[2,320,384]{2,1,0:T(8,128)(2,1)S(1)}, u32[]{:S(2)}, u32[]{:S(2)}) collective-permute-start(bf16[2,320,384]{2,1,0:T(8,128)(2,1)S(1)} %add_convert_fusion.10), channel_id=1, source_target_pairs={{2,0},{3,1},{4,2},{5,3},{6,4},{7,5},{10,8},{11,9},{12,10},{13,11},... | collective-permute-start | bytes 1474568 | tf_op jit(solution)/shard_map/ppermute | solution.py:135
  317.8 22.5 %collective-permute-start.57 = (bf16[8,240,240]{2,1,0:T(8,128)(2,1)}, bf16[8,240,240]{2,1,0:T(8,128)(2,1)}, u32[]{:S(2)}, u32[]{:S(2)}) collective-permute-start(bf16[8,240,240]{2,1,0:T(8,128)(2,1)} %add_convert_fusion.5), channel_id=1, source_target_pairs={{0,16},{8,24},{16,0},{24,8},{1,17},{9,25},{17,1},{25,9},{2,18},{10... | collective-permute-start | bytes 2764808 | tf_op jit(solution)/shard_map/ppermute | solution.py:35
  343.5 17.6 %collective-permute-start.64 = (bf16[4,240,240]{2,1,0:T(8,128)(2,1)S(1)}, bf16[4,240,240]{2,1,0:T(8,128)(2,1)S(1)}, u32[]{:S(2)}, u32[]{:S(2)}) collective-permute-start(bf16[4,240,240]{2,1,0:T(8,128)(2,1)S(1)} %dynamic-slice_bitcast_fusion.1), channel_id=1, source_target_pairs={{0,1},{1,0},{2,3},{3,2},{4,5},{5,4},{6,7},{7,6},{8,9},{9,8},{10,11... | collective-permute-start | bytes 1382408 | tf_op jit(solution)/shard_map/ppermute | solution.py:35
  (130 other events, 1266.5 us)
